TPU v7x, 32 devices: a whole 2x2x4 slice. The times are simulated.
32 devices in a mesh: grp: 2 (over y), sec: 4 (over z), blk: 2 (over x), op: 2 (over core).
Axes of the slice: x: 2, y: 2, z: 4, core: 2. Of those that a mesh axis runs over, the one named last changes fastest.
Arguments:
- ground_state: bfloat16 [48, 512, 512], P(('grp', 'sec'), 'blk'), parts along dimension 0, may hold values from -6 to 6
- op_matrices: bfloat16 [16, 512, 512], P(('grp', 'op')), parts along dimension 0, may hold values from -0.25 to 0.25
- shift_map: int32 [16, 24], P('grp'), parts along dimension 0, may hold values from 0 to 23, as said below
- new_slot: int32 [48], P('grp'), parts along dimension 0, may hold values from 0 to 23, as said below
- env_ground: bfloat16 [48, 512, 512], P(('grp', 'sec'), 'blk'), parts along dimension 0, may hold values from -0.25 to 0.25
- env_src: int32 [48, 3], P('grp'), parts along dimension 0, may hold values from 0 to 23, as said below
- env_coef: float32 [48, 3], P('grp'), parts along dimension 0, may hold values from 0.3 to 1
Outputs:
- grown_env: bfloat16 [16, 24, 512, 512], P(('grp', 'op'), 'sec', 'blk'), parts along dimension 0
There are 2 independent parts, one for each index of `grp`. A program takes and returns all parts, laid end to end along the dimension named above; each array names one. Nothing has to cross between parts.
Inputs may be any that keep to these rules, and one draw needn't show every extreme that they name: Each row o maps the 24 ground sectors one to one onto the N+1 sectors. Within each group of 4 consecutive operators, among the pairs (o, s) with one value of s // 6, at most 7 have new_slot[shift_map[o, s]] // 6 equal to one value, and 7 is reached for every value of s // 6. A permutation: N+1 sector t is stored at slot new_slot[t]. For the N+1 sectors t with one value of new_slot[t] // 6, at most 6 of the entries env_src[t, k] have one value of env_src[t, k] // 6, and 6 is reached for every value of new_slot[t] // 6.
All inputs are finite; a program needn't handle non-finite values.
Results may differ from a plain program's by a relative error of at most 0.0057.
Values may be sent and summed in bfloat16 or wider, within the bound.
No kernel may reach another device: no remote copies, remote signals or barrier semaphores. Data moves between devices by JAX's collectives and lax.ppermute only.
A program may use at most 64 MiB of HBM per device.

v0:
```python
import jax
import jax.numpy as jnp
from jax import lax
from jax.sharding import PartitionSpec as P


def pair_ranks(pair_key):
    counter = jnp.arange(pair_key.shape[0])
    same_pair = pair_key[:, None] == pair_key[None, :]
    earlier = counter[None, :] < counter[:, None]
    return jnp.sum((same_pair & earlier).astype(jnp.int32), axis=1)


def local(ground_state, op_matrices, shift_map, new_slot, env_ground, env_src, env_coef):
    owner_count = lax.axis_size("sec")
    owner = lax.axis_index("sec")
    op_group = lax.axis_index("op")
    sec_dev, row_count, columns = ground_state.shape
    ops_dev = op_matrices.shape[0]
    env_terms = env_src.shape[1]
    sectors = sec_dev * owner_count
    capacity = (sec_dev * ops_dev + owner_count - 1) // owner_count + 1
    env_capacity = (sec_dev * env_terms + owner_count - 1) // owner_count + 1
    dest_all = jnp.take(new_slot, shift_map)
    dest_grp = lax.dynamic_slice_in_dim(dest_all, op_group * ops_dev, ops_dev, 0)
    source_of = jnp.argsort(dest_grp, axis=1)
    sources = lax.dynamic_slice_in_dim(source_of, owner * sec_dev, sec_dev, 1)
    products = jnp.einsum(
        "srd,ode->sore", ground_state, op_matrices, preferred_element_type=jnp.float32
    ).astype(jnp.bfloat16)
    entry_ids = jnp.arange(sectors * ops_dev)
    entry_sector = entry_ids // ops_dev
    entry_dest = dest_grp[entry_ids % ops_dev, entry_sector]
    ranking = pair_ranks(entry_sector // sec_dev * owner_count + entry_dest // sec_dev)
    positions = lax.dynamic_slice_in_dim(
        entry_dest // sec_dev * capacity + ranking, owner * sec_dev * ops_dev, sec_dev * ops_dev
    )
    outgoing = jnp.zeros((owner_count * capacity, row_count, columns), jnp.bfloat16)
    outgoing = outgoing.at[positions].set(products.reshape(sec_dev * ops_dev, row_count, columns))
    incoming = lax.all_to_all(outgoing, "sec", split_axis=0, concat_axis=0, tiled=True)
    wanted = sources * ops_dev + jnp.arange(ops_dev)[:, None]
    locate = sources // sec_dev * capacity + ranking[wanted]
    arrived = incoming[locate]
    sector_at = jnp.argsort(new_slot)
    my_sectors = lax.dynamic_slice_in_dim(sector_at, owner * sec_dev, sec_dev)
    my_coef = env_coef[my_sectors]
    flat_src = env_src[sector_at].reshape(-1)
    entry_slot = jnp.arange(sectors * env_terms) // env_terms
    ranking_env = pair_ranks(flat_src // sec_dev * owner_count + entry_slot // sec_dev)
    placing = entry_slot // sec_dev * env_capacity + ranking_env
    is_mine = flat_src // sec_dev == owner
    slot_ids = jnp.arange(owner_count * env_capacity)
    hit_table = ((placing[None, :] == slot_ids[:, None]) & is_mine[None, :]).astype(jnp.float32)
    local_table = ((flat_src - owner * sec_dev)[:, None] == jnp.arange(sec_dev)[None, :]).astype(
        jnp.float32
    )
    selector = jnp.dot(hit_table, local_table, precision=lax.Precision.HIGHEST).astype(jnp.bfloat16)
    outgoing_env = jnp.einsum(
        "pi,ird->prd", selector, env_ground, preferred_element_type=jnp.float32
    ).astype(jnp.bfloat16)
    incoming_env = lax.all_to_all(outgoing_env, "sec", split_axis=0, concat_axis=0, tiled=True)
    mine_entries = (owner * sec_dev + jnp.arange(sec_dev))[:, None] * env_terms + jnp.arange(
        env_terms
    )[None, :]
    locate_env = flat_src[mine_entries] // sec_dev * env_capacity + ranking_env[mine_entries]
    blocks = incoming_env[locate_env].astype(jnp.float32)
    mixed = jnp.sum(my_coef[:, :, None, None] * blocks, axis=1)
    env_rounded = mixed.astype(jnp.bfloat16)
    grown_env = jnp.einsum(
        "olrd,lde->olre",
        arrived,
        lax.all_gather(env_rounded, "blk", axis=1, tiled=True),
        preferred_element_type=jnp.float32,
    )
    return grown_env.astype(jnp.bfloat16)


def solution(mesh):
    return jax.shard_map(
        local,
        mesh=mesh,
        in_specs=(
            P(("grp", "sec"), "blk", None),
            P(("grp", "op"), None, None),
            P("grp", None),
            P("grp"),
            P(("grp", "sec"), "blk", None),
            P("grp", None),
            P("grp", None),
        ),
        out_specs=P(("grp", "op"), "sec", "blk", None),
        check_vma=False,
    )
```

profile of v0, /device:TPU:0, one launch (start us, length us, event | category | flops | bytes accessed | tf_op | source)
XLA Modules:
  0.0 368.3 jit_solution(6414172959295741181)
XLA Ops:
  6.6 0.8 compare_select_fusion.2
  7.4 0.1 reshape.382
  7.5 1.9 gather_fusion.5
  9.4 0.1 reshape.381
  9.5 0.7 and_select_fusion
  10.2 1.5 gather_fusion.6
  11.7 0.2 convert_reduce_fusion
  11.9 2.3 sort.34
  14.2 0.8 copy.39
  14.9 0.1 compare_select_fusion.5
  15.0 0.6 gather_fusion.1
  15.6 0.1 reshape.338
  15.7 0.2 convert_reduce_fusion.1
  15.9 0.2 fusion.9
  16.2 3.3 convolution_convert_fusion
  19.5 4.9 %copy.41 = bf16[24,256,512]{2,1,0:T(8,128)(2,1)} copy(bf16[24,256,512]{2,0,1:T(8,128)(2,1)S(1)} %convolution_convert_fusion) | data formatting | bytes 12582912 | tf_op jit(solution)/shard_map/convert_element_type | solution.py:60
  24.3 6.3 %all-to-all-start = ((bf16[24,256,512]{2,1,0:T(8,128)(2,1)}), bf16[24,256,512]{2,1,0:T(8,128)(2,1)}, u32[]{:S(2)}, u32[]{:S(2)}) async-start(bf16[24,256,512]{2,1,0:T(8,128)(2,1)} %copy.41), calls=%async_computation | async-start | bytes 12582912 | tf_op jit(solution)/shard_map/all_to_all | solution.py:61
  30.7 6.8 %convert_bitcast_fusion.1 = bf16[6,4,256,512]{2,3,0,1:T(8,128)(2,1)} fusion(bf16[4,512,512]{2,1,0:T(8,128)(2,1)S(1)} %copy-done, bf16[6,256,512]{2,1,0:T(8,128)(2,1)} %param.7), kind=kOutput, calls=%fused_computation.15 | convolution fusion | flops 3224371200 | bytes 9961472 | tf_op jit(solution)/shard_map/srd,ode->sore/dot_general | solution.py:28
  37.5 8.7 %copy.44 = bf16[6,4,256,512]{3,2,1,0:T(8,128)(2,1)} copy(bf16[6,4,256,512]{2,3,0,1:T(8,128)(2,1)} %convert_bitcast_fusion.1) | data formatting | bytes 12582912 | tf_op jit(solution)/shard_map/convert_element_type | solution.py:30
  46.1 3.8 %broadcast_in_dim.22 = bf16[28,256,512]{2,1,0:T(8,128)(2,1)} broadcast(bf16[]{:T(256)} %constant.123.clone.1), dimensions={} | broadcast | bytes 7340034 | tf_op jit(solution)/shard_map/broadcast_in_dim | solution.py:38
  49.9 16.1 %scatter_fusion = bf16[28,256,512]{2,1,0:T(8,128)(2,1)} fusion(bf16[28,256,512]{2,1,0:T(8,128)(2,1)} %broadcast_in_dim.22, s32[24]{0:T(128)S(1)} %get-tuple-element.13, bf16[24,256,512]{2,1,0:T(8,128)(2,1)} %bitcast.30), kind=kCustom, calls=%fused_computation.9 | custom fusion | bytes 18874464 | tf_op jit(solution)/shard_map/scatter | solution.py:39
  66.0 103.4 %all-to-all-done = bf16[24,256,512]{2,1,0:T(8,128)(2,1)} async-done(((bf16[24,256,512]{2,1,0:T(8,128)(2,1)}), bf16[24,256,512]{2,1,0:T(8,128)(2,1)}, u32[]{:S(2)}, u32[]{:S(2)}) %all-to-all-start) | async-done | bytes 6291488 | tf_op jit(solution)/shard_map/all_to_all | solution.py:61
  169.4 5.4 %all-to-all-start.1 = ((bf16[28,256,512]{2,1,0:T(8,128)(2,1)}), bf16[28,256,512]{2,1,0:T(8,128)(2,1)}, u32[]{:S(2)}, u32[]{:S(2)}) async-start(bf16[28,256,512]{2,1,0:T(8,128)(2,1)} %scatter_fusion), calls=%async_computation.1 | async-start | bytes 14680064 | tf_op jit(solution)/shard_map/all_to_all | solution.py:40
  174.9 0.2 all-gather.2.cloned.1.call-start
  175.2 0.1 reshape.358
  175.3 0.7 gather_fusion.3
  176.0 0.7 gather_fusion.2
  176.8 0.1 and.169
  176.9 0.1 div.119
  176.9 0.1 reshape.374
  177.0 0.1 copy.38
  177.2 0.6 gather_fusion
  177.8 6.8 %gather_fusion.4 = bf16[18,256,512]{2,1,0:T(8,128)(2,1)} fusion(bf16[24,256,512]{2,1,0:T(8,128)(2,1)} %all-to-all-done, s32[1024]{0:T(1024)S(1)} %pad_clamp_fusion.3), kind=kCustom, calls=%fused_computation.4 | custom fusion | bytes 9437256 | tf_op jit(solution)/shard_map/gather | solution.py:66
  184.5 3.4 fusion
  187.9 1.6 copy.42
  189.5 0.1 copy.45
  189.6 0.8 sort.35
  190.4 0.1 copy.46
  190.5 0.1 reshape.396
  190.6 0.7 gather_fusion.7
  191.3 0.1 reshape.395
  191.4 0.1 copy.47
  191.5 0.1 copy.48
  191.6 0.1 reshape.404
  191.7 143.5 %all-to-all-done.1 = bf16[28,256,512]{2,1,0:T(8,128)(2,1)} async-done(((bf16[28,256,512]{2,1,0:T(8,128)(2,1)}), bf16[28,256,512]{2,1,0:T(8,128)(2,1)}, u32[]{:S(2)}, u32[]{:S(2)}) %all-to-all-start.1) | async-done | bytes 7340064 | tf_op jit(solution)/shard_map/all_to_all | solution.py:40
  335.2 7.6 %gather_fusion.8 = bf16[24,256,512]{2,1,0:T(8,128)(2,1)} fusion(bf16[28,256,512]{2,1,0:T(8,128)(2,1)} %all-to-all-done.1, s32[1024]{0:T(1024)S(1)} %pad_clamp_fusion), kind=kCustom, calls=%fused_computation.8 | custom fusion | bytes 12583008 | tf_op jit(solution)/shard_map/gather | solution.py:43
  342.8 10.0 %convert_bitcast_fusion = bf16[4,6,256,512]{2,3,0,1:T(8,128)(2,1)} fusion(bf16[4,6,256,512]{3,2,1,0:T(8,128)(2,1)} %bitcast.32, bf16[6,512,512]{1,2,0:T(8,128)(2,1)} %all-gather.2.cloned.1.call-done), kind=kOutput, calls=%fused_computation.14 | convolution fusion | flops 3224371200 | bytes 15728640 | tf_op jit(solution)/shard_map/olrd,lde->olre/dot_general | solution.py:69
  352.8 8.6 %copy.50 = bf16[4,6,256,512]{3,2,1,0:T(8,128)(2,1)} copy(bf16[4,6,256,512]{2,3,0,1:T(8,128)(2,1)} %convert_bitcast_fusion) | data formatting | bytes 12582912 | tf_op jit(solution)/shard_map/convert_element_type | solution.py:75
  (34 shorter events, 0.5 us)
Async XLA Ops:
  6.5 24.1 %copy-start = (bf16[4,512,512]{2,1,0:T(8,128)(2,1)S(1)}, bf16[4,512,512]{2,1,0:T(8,128)(2,1)}, u32[]{:S(2)}) copy-start(bf16[4,512,512]{2,1,0:T(8,128)(2,1)} %param.8) | copy-start | bytes 6291460
  24.3 145.1 %all-to-all-start = ((bf16[24,256,512]{2,1,0:T(8,128)(2,1)}), bf16[24,256,512]{2,1,0:T(8,128)(2,1)}, u32[]{:S(2)}, u32[]{:S(2)}) async-start(bf16[24,256,512]{2,1,0:T(8,128)(2,1)} %copy.41), calls=%async_computation | async-start | bytes 12582912 | tf_op jit(solution)/shard_map/all_to_all | solution.py:61
  169.4 165.8 %all-to-all-start.1 = ((bf16[28,256,512]{2,1,0:T(8,128)(2,1)}), bf16[28,256,512]{2,1,0:T(8,128)(2,1)}, u32[]{:S(2)}, u32[]{:S(2)}) async-start(bf16[28,256,512]{2,1,0:T(8,128)(2,1)} %scatter_fusion), calls=%async_computation.1 | async-start | bytes 14680064 | tf_op jit(solution)/shard_map/all_to_all | solution.py:40
  174.8 2.2 copy-start.2
  174.9 167.9 %all-gather.2.cloned.1.call-start = ((), (), s32[]{:S(2)}) async-start(), calls=%async_computation.2 | async-start | bytes 4718592 | tf_op jit(solution)/shard_map/all_gather | solution.py:72
  342.8 18.7 %copy-start.1 = (bf16[4,512,512]{2,1,0:T(8,128)(2,1)S(1)}, bf16[4,512,512]{2,1,0:T(8,128)(2,1)}, u32[]{:S(2)}) copy-start(bf16[4,512,512]{2,1,0:T(8,128)(2,1)} %param.8) | copy-start | bytes 6291460
Sparse Core Ops, SparseCore 0:
  189.6 46.1 all-gather.1
where the time goes:
time: 369 us; the launch traced here: 368 us
  waiting for transfers between devices  247 us (67%)
  local copies, waits for them, and re-layouts  66.7 us (18%)
  matrix products  20.3 us (6%)
  between operations  13.5 us (4%)
  starting transfers between devices  12 us (3%)
  other arithmetic  8.77 us (2%)
    all_to_all x1, waiting for transfers between devices, local(): lax.all_to_all(outgoing, 'sec', split_axis=0, concat_axis=0, tiled=True)  143 us
    all_to_all x1, waiting for transfers between devices, local(): lax.all_to_all(outgoing_env, 'sec', split_axis=0, concat_axis=0, tiled=True)  103 us
    scatter x1, local copies, waits for them, and re-layouts, local(): outgoing.at[positions]  16.1 us
    dot_general x1, matrix products, local(): jnp.einsum('olrd,lde->olre', arrived, lax.all_gather(env_rounded, 'blk',...  10 us
    convert_element_type x1, local copies, waits for them, and re-layouts, local(): products = jnp.einsum('srd,ode->sore', ground_state, op_matrices, preferr...  8.66 us
    convert_element_type x1, local copies, waits for them, and re-layouts, local(): return grown_env.astype(jnp.bfloat16)  8.64 us
    gather x1, local copies, waits for them, and re-layouts, local(): arrived = incoming[locate]  7.57 us
  transfers between devices with their start and end apart: 3, of which 2 were waited for; matrix products, arithmetic and copies ran while one was open for 16% of the time, Pallas kernels for 0%

commit v1 on v0

v1 whole, which is shorter than its diff:
```python
import functools

import jax
import jax.numpy as jnp
from jax import lax
from jax.experimental import pallas as pl
from jax.experimental.pallas import tpu as pltpu
from jax.sharding import PartitionSpec as P

ANY = pl.BlockSpec(memory_space=pl.ANY)
SMEM = pl.BlockSpec(memory_space=pltpu.SMEM)
VMEM = pl.BlockSpec(memory_space=pltpu.VMEM)
BF16 = jnp.bfloat16
LIMIT = 40 << 20


def mix_kernel(dims, picks, places, rows_at, ints, coef, *refs):
    ops, sectors, sec_dev, terms = dims
    count = len(picks)
    sources, refs = refs[:count], refs[count:]
    other = None
    if rows_at is not None:
        other, refs = refs[0], refs[1:]
    outs, (inverse, held, sems) = refs[: len(places)], refs[len(places) :]
    slot_at = ops * sectors
    src_at = slot_at + sectors
    pos_at = src_at + sectors * terms
    busy = ints[pos_at + 2] == 1

    def compute():
        def invert(t, carry):
            inverse[ints[slot_at + t]] = t
            return carry

        lax.fori_loop(0, sectors, invert, 0)

        def copies(place, i, side, act):
            owner = ints[pos_at + place]
            t = inverse[owner * sec_dev + i]
            for k in range(terms):
                source = ints[src_at + t * terms + k]
                if count == 1:
                    act(pltpu.make_async_copy(sources[0].at[source], held.at[side, k], sems.at[side, k]))
                    continue
                code = ints[pos_at + 16 + source // sec_dev]
                for q in range(count):

                    @pl.when(code == q)
                    def _(q=q, k=k, source=source):
                        src = sources[q].at[source % sec_dev]
                        if picks[q] is not None:
                            src = src.at[pl.ds(picks[q], held.shape[2])]
                        act(pltpu.make_async_copy(src, held.at[side, k], sems.at[side, k]))

        steps = [(n, place) for n, place in enumerate(places)]
        for n, place in steps:
            copies(place, 0, 0, lambda c: c.start())

            def step(i, carry, n=n, place=place):
                side = lax.rem(i, 2)

                @pl.when(i + 1 < sec_dev)
                def _():
                    copies(place, i + 1, 1 - side, lambda c: c.start())

                for k in range(terms):
                    pltpu.make_async_copy(held.at[side, k], held.at[side, k], sems.at[side, k]).wait()
                t = inverse[ints[pos_at + place] * sec_dev + i]
                height = min(32, held.shape[2])
                for r in range(0, held.shape[2], height):
                    total = coef[t * terms] * held[side, 0, r : r + height].astype(jnp.float32)
                    for k in range(1, terms):
                        total += coef[t * terms + k] * held[side, k, r : r + height].astype(jnp.float32)
                    outs[n][i, r : r + height] = total.astype(BF16)
                return carry

            lax.fori_loop(0, sec_dev, step, 0)

    if other is None:
        compute()
        return
    pl.when(busy)(compute)

    @pl.when(jnp.logical_not(busy))
    def _():
        copy = pltpu.make_async_copy(other.at[rows_at], outs[0], sems.at[0, 0])
        copy.start()
        copy.wait()


def mix(dims, ints, coef, sources, picks, places, height, other=None, rows_at=None):
    ops, sectors, sec_dev, terms = dims
    columns = sources[0].shape[-1]
    block = jax.ShapeDtypeStruct((sec_dev, height, columns), BF16)
    args = [ints, coef, *sources] + ([] if other is None else [other])
    return pl.pallas_call(
        functools.partial(mix_kernel, dims, picks, places, rows_at),
        out_shape=[block] * len(places),
        in_specs=[SMEM, SMEM] + [ANY] * (len(args) - 2),
        out_specs=[VMEM] * len(places),
        scratch_shapes=[
            pltpu.SMEM((sectors,), jnp.int32),
            pltpu.VMEM((2, terms, height, columns), BF16),
            pltpu.SemaphoreType.DMA((2, terms)),
        ],
        compiler_params=pltpu.CompilerParams(vmem_limit_bytes=LIMIT),
        cost_estimate=pl.CostEstimate(
            flops=2 * terms * len(places) * sec_dev * height * columns,
            bytes_accessed=2 * (terms + 1) * len(places) * sec_dev * height * columns,
            transcendentals=0,
        ),
        name="mix",
    )(*args)


def pair_kernel(dims, ops_dev, counts, pieces, first, ints, where, *refs):
    ops, sectors, sec_dev, terms = dims
    grounds, refs = refs[: len(counts)], refs[len(counts) :]
    op_ref, refs = refs[0], refs[1:]
    env_refs, refs = refs[:pieces], refs[pieces:]
    if not first:
        refs = refs[1:]
    out_ref, found, env, ground, result, env_sem, ground_sem, out_sem = refs
    slot_at = ops * sectors
    pos_at = slot_at + sectors + sectors * terms
    me = ints[pos_at]
    op_base = ints[pos_at + 3] * ops_dev
    env_copies = []
    for n in range(pieces):
        start = pl.multiple_of(where[len(counts) + n], 64)
        env_copies.append(
            pltpu.make_async_copy(env_refs[n], env.at[:, pl.ds(start, env_refs[n].shape[1])], env_sem.at[n])
        )
        env_copies[-1].start()

    def search(n, total):
        base = where[n]

        def candidate(s, total):
            for o in range(ops_dev):
                slot = ints[slot_at + ints[(op_base + o) * sectors + base + s]]
                local = slot - me * sec_dev
                mine = jnp.logical_and(local >= 0, local < sec_dev)
                found[0, total] = n
                found[1, total] = s
                found[2, total] = o
                found[3, total] = local
                total = total + mine.astype(jnp.int32)
            return total

        return lax.fori_loop(0, jnp.where(base >= 0, counts[n], 0), candidate, total)

    total = jnp.int32(0)
    for n in range(len(counts)):
        total = search(n, total)

    def fetch(i, side):
        for n in range(len(counts)):

            @pl.when(found[0, i] == n)
            def _(n=n):
                pltpu.make_async_copy(grounds[n].at[found[1, i]], ground.at[side], ground_sem.at[side]).start()

    @pl.when(total > 0)
    def _():
        fetch(0, 0)

    for copy in env_copies:
        copy.wait()

    def step(i, carry):
        side = lax.rem(i, 2)

        @pl.when(i + 1 < total)
        def _():
            fetch(i + 1, 1 - side)

        pltpu.make_async_copy(ground.at[side], ground.at[side], ground_sem.at[side]).wait()
        o, local = found[2, i], found[3, i]
        product = jnp.dot(ground[side], op_ref[o], preferred_element_type=jnp.float32).astype(BF16)
        grown = jnp.dot(product, env[local], preferred_element_type=jnp.float32).astype(BF16)

        @pl.when(i >= 2)
        def _():
            pltpu.make_async_copy(result.at[side], result.at[side], out_sem.at[side]).wait()

        result[side] = grown
        pltpu.make_async_copy(result.at[side], out_ref.at[o, local], out_sem.at[side]).start()
        return carry

    lax.fori_loop(0, total, step, 0)
    for back in (1, 2):

        @pl.when(total >= back)
        def _(back=back):
            side = lax.rem(total - back, 2)
            pltpu.make_async_copy(result.at[side], result.at[side], out_sem.at[side]).wait()


def pairs(dims, ints, where, grounds, op_matrices, env_pieces, out):
    ops, sectors, sec_dev, terms = dims
    ops_dev = op_matrices.shape[0]
    rows, columns = grounds[0].shape[1:]
    counts = [g.shape[0] for g in grounds]
    shape = jax.ShapeDtypeStruct((ops_dev, sec_dev, rows, columns), BF16)
    args = [ints, where, *grounds, op_matrices, *env_pieces] + ([] if out is None else [out])
    work = max(1, sum(counts) * ops_dev * sec_dev // sectors)
    return pl.pallas_call(
        functools.partial(pair_kernel, dims, ops_dev, counts, len(env_pieces), out is None),
        out_shape=shape,
        in_specs=[SMEM, SMEM] + [ANY] * len(grounds) + [VMEM] + [ANY] * (len(args) - 3 - len(grounds)),
        out_specs=ANY,
        scratch_shapes=[
            pltpu.SMEM((4, sum(counts) * ops_dev + 8), jnp.int32),
            pltpu.VMEM((sec_dev, columns, columns), BF16),
            pltpu.VMEM((2, rows, columns), BF16),
            pltpu.VMEM((2, rows, columns), BF16),
            pltpu.SemaphoreType.DMA((len(env_pieces),)),
            pltpu.SemaphoreType.DMA((2,)),
            pltpu.SemaphoreType.DMA((2,)),
        ],
        input_output_aliases={} if out is None else {len(args) - 1: 0},
        compiler_params=pltpu.CompilerParams(vmem_limit_bytes=LIMIT),
        cost_estimate=pl.CostEstimate(
            flops=4 * work * rows * columns * columns,
            bytes_accessed=2 * (2 * work * rows * columns + (ops_dev + sec_dev) * columns * columns),
            transcendentals=0,
        ),
        name="pairs",
    )(*args)


def pack(shift_map, new_slot, env_src, position):
    return jnp.concatenate(
        [shift_map.reshape(-1), new_slot, env_src.reshape(-1), jnp.stack(position).astype(jnp.int32)]
    )


def whole_gather(ground_state, op_matrices, shift_map, new_slot, env_ground, env_src, env_coef):
    owner = lax.axis_index("sec")
    group = lax.axis_index("op")
    halves = lax.axis_size("op")
    sec_dev, rows, columns = ground_state.shape
    ops, sectors = shift_map.shape
    dims = (ops, sectors, sec_dev, env_src.shape[1])
    zero = jnp.zeros((), jnp.int32)
    ints = pack(shift_map, new_slot, env_src, [owner, zero, zero + 1, group])

    def gather(blocks):
        part = rows // halves
        mine = lax.dynamic_slice_in_dim(blocks, group * part, part, 1)
        whole = lax.all_gather(lax.all_gather(mine, "sec", axis=0, tiled=True), "op", axis=1, tiled=True)
        return whole

    env_all = gather(env_ground)
    (env_new,) = mix(dims, ints, env_coef.reshape(-1), [env_all], [None], [0], rows)
    env_rows = lax.all_gather(env_new, "blk", axis=1, tiled=True)
    where = jnp.zeros((2,), jnp.int32)
    return pairs(dims, ints, where, [gather(ground_state)], op_matrices, [env_rows], None)


def line_of_four(ground_state, op_matrices, shift_map, new_slot, env_ground, env_src, env_coef):
    owner = lax.axis_index("sec")
    group = lax.axis_index("op")
    row_half = lax.axis_index("blk")
    sec_dev, rows, columns = ground_state.shape
    ops, sectors = shift_map.shape
    dims = (ops, sectors, sec_dev, env_src.shape[1])
    half = rows // 2
    spot = jnp.where(group == 0, owner, 3 - owner)

    def stream(steps):
        up = [(2 * a, 2 * a + 2) for a in steps]
        down = [(2 * (3 - a) + 1, 2 * (2 - a) + 1) for a in steps]
        return lambda block: lax.ppermute(block, ("sec", "op"), up + down)

    def swap(block):
        return lax.ppermute(block, "op", [(0, 1), (1, 0)])

    def across(block):
        pairs_of = []
        for z in range(4):
            lead = 0 if z >= 2 else 1
            for x in range(2):
                pairs_of.append(((z * 2 + x) * 2 + lead, (z * 2 + 1 - x) * 2 + 1 - lead))
        return lax.ppermute(block, ("sec", "blk", "op"), pairs_of)

    every, middle, late, last = stream([0, 1, 2]), stream([1]), stream([1, 2]), stream([2])
    ground_half = ground_state.reshape(2, sec_dev, half, columns)
    env_half = env_ground.reshape(sec_dev, 2, half, columns)
    is_two = spot == 2
    ahead = jnp.where(group == 0, owner + 1, owner - 1)
    code = [jnp.where(group == 0, w, 3 - w) for w in range(4)]
    position = [owner, ahead, is_two, group] + [jnp.zeros((), jnp.int32)] * 12 + code
    coef = env_coef.reshape(-1)

    sent0 = [jnp.where(is_two, ground_half[h], env_half[:, h]) for h in range(2)]
    got0 = [every(sent0[h]) for h in range(2)]
    got2 = [middle(got0[h]) for h in range(2)]
    swapped0 = [swap(got0[h]) for h in range(2)]
    ints = pack(shift_map, new_slot, env_src, position)
    sent4, env_new = [], []
    for h in range(2):
        passed, made = mix(
            dims, ints, coef, [got2[h], got0[h], env_ground, swapped0[h]], [None, None, h * half, None], [1, 0],
            half, ground_half, h,
        )
        sent4.append(passed)
        env_new.append(made)
    got4 = [every(sent4[h]) for h in range(2)]
    got6 = [late(got4[h]) for h in range(2)]
    got8 = [last(got6[h]) for h in range(2)]
    swapped4 = [swap(got4[h]) for h in range(2)]
    swapped6 = [swap(got6[h]) for h in range(2)]
    swapped8 = [swap(got8[h]) for h in range(2)]
    env_pieces, env_starts = [], []
    lead = spot >= 2
    for h in range(2):
        mine = jnp.where(is_two, env_new[h], got4[h])
        received = across(mine)
        kept = jnp.where(lead, mine, received)
        env_pieces += [kept, swap(kept)]
        own, far = row_half * rows + h * half, (1 - row_half) * rows + h * half
        env_starts += [jnp.where(lead, own, far), jnp.where(lead, far, own)]

    step = jnp.where(group == 0, -1, 1)

    def base(own_hops, h):
        hops = jnp.asarray(own_hops, jnp.int32)
        own = jnp.where(hops[spot] > 0, (owner + step * hops[spot]) * sec_dev + h * (sec_dev // 2), -1)
        other = hops[3 - spot]
        theirs = jnp.where(other > 0, (owner - step * other) * sec_dev + h * (sec_dev // 2), -1)
        return [own, theirs]

    def blocks(block):
        return block.reshape(sec_dev // 2, rows, columns)

    def stage(out, arrays, bases):
        where = jnp.stack([jnp.asarray(b, jnp.int32) for b in bases + env_starts])
        return pairs(dims, ints, where, arrays, op_matrices, env_pieces, out)

    arrays, bases = [ground_state], [owner * sec_dev]
    for h in range(2):
        arrays += [blocks(got0[h]), blocks(swapped0[h]), blocks(got4[h]), blocks(swapped4[h])]
        bases += base([0, 0, 0, 1], h) + base([0, 1, 1, 0], h)
    out = stage(None, arrays, bases)
    arrays, bases = [], []
    for h in range(2):
        arrays += [blocks(got6[h]), blocks(swapped6[h])]
        bases += base([0, 0, 2, 2], h)
    out = stage(out, arrays, bases)
    for h in range(2):
        out = stage(out, [blocks(got8[h]), blocks(swapped8[h])], base([0, 0, 0, 3], h))
    return out


def solution(mesh):
    four = mesh.shape["sec"] == 4 and mesh.shape["blk"] == 2 and mesh.shape["op"] == 2
    return jax.shard_map(
        line_of_four if four else whole_gather,
        mesh=mesh,
        in_specs=(
            P(("grp", "sec"), "blk", None),
            P(("grp", "op"), None, None),
            P("grp", None),
            P("grp"),
            P(("grp", "sec"), "blk", None),
            P("grp", None),
            P("grp", None),
        ),
        out_specs=P(("grp", "op"), "sec", "blk", None),
        check_vma=False,
    )
```

time: 369 us -> 148 us (0.40)
  waiting for transfers between devices: 247 us -> 21.8 us
  local copies, waits for them, and re-layouts: 66.7 us -> 10.6 us
  starting transfers between devices: 12 us -> 66.2 us
  Pallas kernels: 0 us -> 29 us
  matrix products: 20.3 us -> 0 us
    all_to_all x2 -> x0, waiting for transfers between devices: 247 us -> none  [the longest x1 143 us: local(): lax.all_to_all(outgoing, 'sec', split_axis=0, concat_axis=0, tiled=True)]
    ppermute x0 -> x22, starting transfers between devices: none -> 66.2 us  [the longest x10 43.7 us: stream(): return lambda block: lax.ppermute(block, ('sec', 'op'), up + down)]
    pallas_call x0 -> x6, Pallas kernels: none -> 29 us  [the longest x4 27.6 us: pairs(): pl.pallas_call(functools.partial(pair_kernel, dims, ops_dev, counts, len(...]
    convert_element_type x3 -> x0, local copies, waits for them, and re-layouts: 22.2 us -> none  [the longest x1 8.66 us: local(): products = jnp.einsum('srd,ode->sore', ground_state, op_matrices, preferr...]
    ppermute x0 -> x22, waiting for transfers between devices: none -> 21.8 us  [the longest x10 15.8 us: stream(): return lambda block: lax.ppermute(block, ('sec', 'op'), up + down)]
    gather x13 -> x0, local copies, waits for them, and re-layouts: 21.3 us -> none  [the longest x1 7.57 us: local(): arrived = incoming[locate]]
    dot_general x4 -> x0, matrix products: 20.3 us -> none  [the longest x1 10 us: local(): jnp.einsum('olrd,lde->olre', arrived, lax.all_gather(env_rounded, 'blk',...]
    scatter x1 -> x0, local copies, waits for them, and re-layouts: 16.1 us -> none  [local(): outgoing.at[positions]]
  transfers between devices with their start and end apart: 3 -> 22, of which waited for: 2 -> 4; matrix products, arithmetic and copies ran while one was open for 16% -> 6% of each run, Pallas kernels for 0% -> 17%
where the time goes in v1:
time: 148 us; the launch traced here: 145 us
  starting transfers between devices  66.2 us (45%)
  Pallas kernels  29 us (20%)
  waiting for transfers between devices  21.8 us (15%)
  local copies, waits for them, and re-layouts  10.6 us (7%)
  between operations  10.6 us (7%)
  other arithmetic  6.97 us (5%)
    ppermute x10, starting transfers between devices, stream(): return lambda block: lax.ppermute(block, ('sec', 'op'), up + down)  43.7 us
    pallas_call x4, Pallas kernels, pairs(): pl.pallas_call(functools.partial(pair_kernel, dims, ops_dev, counts, len(...  27.6 us
    ppermute x10, starting transfers between devices, swap(): return lax.ppermute(block, 'op', [(0, 1), (1, 0)])  19.9 us
    ppermute x10, waiting for transfers between devices, stream(): return lambda block: lax.ppermute(block, ('sec', 'op'), up + down)  15.8 us
    ppermute x2, waiting for transfers between devices, across(): return lax.ppermute(block, ('sec', 'blk', 'op'), pairs_of)  5.96 us
    unnamed x38, local copies, waits for them, and re-layouts  5.7 us
    select_n x2, other arithmetic, line_of_four(): kept = jnp.where(lead, mine, received)  3.45 us
    select_n x2, other arithmetic, line_of_four(): mine = jnp.where(is_two, env_new[h], got4[h])  3.36 us
  transfers between devices with their start and end apart: 22, of which 4 were waited for; matrix products, arithmetic and copies ran while one was open for 6% of the time, Pallas kernels for 17%

profile of v1, /device:TPU:0, one launch (start us, length us, event | category | flops | bytes accessed | tf_op | source)
XLA Modules:
  0.0 145.1 jit_solution(9817466187261621701)
XLA Ops:
  0.0 2.8 %fusion.2 = (bf16[3,256,512]{2,1,0:T(8,128)(2,1)}, bf16[3,256,512]{2,1,0:T(8,128)(2,1)}) fusion(bf16[6,256,512]{2,1,0:T(8,128)(2,1)} %refs_0_.1), kind=kLoop, calls=%fused_computation.8 | loop fusion | bytes 3145728 | tf_op jit(solution)/shard_map/slice | solution.py:297
  2.9 0.2 fusion
  3.1 6.0 %collective-permute-start = (bf16[6,128,512]{2,1,0:T(8,128)(2,1)S(1)}, bf16[6,128,512]{2,1,0:T(8,128)(2,1)}, u32[]{:S(2)}, u32[]{:S(2)}) collective-permute-start(bf16[6,128,512]{2,1,0:T(8,128)(2,1)S(1)} %get-tuple-element.14), channel_id=1, source_target_pairs={{0,4},{4,8},{8,12},{13,9},{9,5},{5,1},{2,6},{6,10},{10,14},{15,11}... | collective-permute-start | bytes 2359304 | tf_op jit(solution)/shard_map/ppermute | solution.py:275
  9.0 4.8 %collective-permute-start.7 = (bf16[6,128,512]{2,1,0:T(8,128)(2,1)S(1)}, bf16[6,128,512]{2,1,0:T(8,128)(2,1)}, u32[]{:S(2)}, u32[]{:S(2)}) collective-permute-start(bf16[6,128,512]{2,1,0:T(8,128)(2,1)S(1)} %get-tuple-element.13), channel_id=1, source_target_pairs={{0,4},{4,8},{8,12},{13,9},{9,5},{5,1},{2,6},{6,10},{10,14},{15,11}... | collective-permute-start | bytes 2359304 | tf_op jit(solution)/shard_map/ppermute | solution.py:275
  13.9 3.8 %collective-permute-done.refs_1_ = bf16[6,128,512]{2,1,0:T(8,128)(2,1)} collective-permute-done((bf16[6,128,512]{2,1,0:T(8,128)(2,1)S(1)}, bf16[6,128,512]{2,1,0:T(8,128)(2,1)}, u32[]{:S(2)}, u32[]{:S(2)}) %collective-permute-start) | collective-permute-done | bytes 786464 | tf_op jit(solution)/shard_map/ppermute | solution.py:275
  17.6 0.9 collective-permute-start.2
  18.5 1.5 %collective-permute-start.1 = (bf16[6,128,512]{2,1,0:T(8,128)(2,1)}, bf16[6,128,512]{2,1,0:T(8,128)(2,1)}, u32[]{:S(2)}, u32[]{:S(2)}) collective-permute-start(bf16[6,128,512]{2,1,0:T(8,128)(2,1)} %collective-permute-done.refs_1_), channel_id=1, source_target_pairs={{4,8},{9,5},{6,10},{11,7},{20,24},{25,21},{22,26},{27,23}} | collective-permute-start | bytes 2359304 | tf_op jit(solution)/shard_map/ppermute | solution.py:275
  20.0 6.0 %collective-permute-done.7.refs_1_ = bf16[6,128,512]{2,1,0:T(8,128)(2,1)} collective-permute-done((bf16[6,128,512]{2,1,0:T(8,128)(2,1)S(1)}, bf16[6,128,512]{2,1,0:T(8,128)(2,1)}, u32[]{:S(2)}, u32[]{:S(2)}) %collective-permute-start.7) | collective-permute-done | bytes 786464 | tf_op jit(solution)/shard_map/ppermute | solution.py:275
  26.0 0.9 collective-permute-start.9
  26.9 1.5 %collective-permute-start.8 = (bf16[6,128,512]{2,1,0:T(8,128)(2,1)}, bf16[6,128,512]{2,1,0:T(8,128)(2,1)}, u32[]{:S(2)}, u32[]{:S(2)}) collective-permute-start(bf16[6,128,512]{2,1,0:T(8,128)(2,1)} %collective-permute-done.7.refs_1_), channel_id=1, source_target_pairs={{4,8},{9,5},{6,10},{11,7},{20,24},{25,21},{22,26},{27,23}} | collective-permute-start | bytes 2359304 | tf_op jit(solution)/shard_map/ppermute | solution.py:275
  28.6 0.1 reshape.68
  28.8 0.1 copy.22
  28.8 0.1 reshape.69.coef
  29.0 0.1 concatenate.3.ints
  29.1 0.7 mix.2
  29.8 11.2 %collective-permute-start.3 = (bf16[6,128,512]{2,1,0:T(8,128)(2,1)S(1)}, bf16[6,128,512]{2,1,0:T(8,128)(2,1)}, u32[]{:S(2)}, u32[]{:S(2)}) collective-permute-start(bf16[6,128,512]{2,1,0:T(8,128)(2,1)S(1)} %get-tuple-element.9), channel_id=1, source_target_pairs={{0,4},{4,8},{8,12},{13,9},{9,5},{5,1},{2,6},{6,10},{10,14},{15,11}... | collective-permute-start | bytes 2359304 | tf_op jit(solution)/shard_map/ppermute | solution.py:275
  41.0 0.7 mix.3
  41.7 12.4 %collective-permute-start.10 = (bf16[6,128,512]{2,1,0:T(8,128)(2,1)S(1)}, bf16[6,128,512]{2,1,0:T(8,128)(2,1)}, u32[]{:S(2)}, u32[]{:S(2)}) collective-permute-start(bf16[6,128,512]{2,1,0:T(8,128)(2,1)S(1)} %get-tuple-element.11), channel_id=1, source_target_pairs={{0,4},{4,8},{8,12},{13,9},{9,5},{5,1},{2,6},{6,10},{10,14},{15,11}... | collective-permute-start | bytes 2359304 | tf_op jit(solution)/shard_map/ppermute | solution.py:275
  54.1 1.2 broadcast_select_fusion.2
  55.3 1.3 collective-permute-start.13
  56.6 6.1 %collective-permute-done.10 = bf16[6,128,512]{2,1,0:T(8,128)(2,1)} collective-permute-done((bf16[6,128,512]{2,1,0:T(8,128)(2,1)S(1)}, bf16[6,128,512]{2,1,0:T(8,128)(2,1)}, u32[]{:S(2)}, u32[]{:S(2)}) %collective-permute-start.10) | collective-permute-done | bytes 786464 | tf_op jit(solution)/shard_map/ppermute | solution.py:275
  62.7 2.1 %broadcast_select_fusion.3 = bf16[6,128,512]{2,1,0:T(8,128)(2,1)} fusion(bf16[6,128,512]{2,1,0:T(8,128)(2,1)S(1)} %get-tuple-element.10, bf16[6,128,512]{2,1,0:T(8,128)(2,1)} %collective-permute-done.10, pred[]{:T(512)S(6)} %eq.5), kind=kLoop, calls=%fused_computation.7 | loop fusion | flops 393216 | bytes 2359297 | tf_op jit(solution)/shard_map/jit(_where)/select_n | solution.py:319
  64.8 1.3 collective-permute-start.11
  66.1 1.5 %collective-permute-start.15 = (bf16[6,128,512]{2,1,0:T(8,128)(2,1)}, bf16[6,128,512]{2,1,0:T(8,128)(2,1)}, u32[]{:S(2)}, u32[]{:S(2)}) collective-permute-start(bf16[6,128,512]{2,1,0:T(8,128)(2,1)} %collective-permute-done.10), channel_id=1, source_target_pairs={{4,8},{8,12},{9,5},{5,1},{6,10},{10,14},{11,7},{7,3},{20,24},{24,2... | collective-permute-start | bytes 2359304 | tf_op jit(solution)/shard_map/ppermute | solution.py:275
  67.6 1.6 %collective-permute-start.4 = (bf16[6,128,512]{2,1,0:T(8,128)(2,1)}, bf16[6,128,512]{2,1,0:T(8,128)(2,1)}, u32[]{:S(2)}, u32[]{:S(2)}) collective-permute-start(bf16[6,128,512]{2,1,0:T(8,128)(2,1)} %collective-permute-done.3), channel_id=1, source_target_pairs={{4,8},{8,12},{9,5},{5,1},{6,10},{10,14},{11,7},{7,3},{20,24},{24,2... | collective-permute-start | bytes 2359304 | tf_op jit(solution)/shard_map/ppermute | solution.py:275
  69.2 5.4 %collective-permute-start.20 = (bf16[6,128,512]{2,1,0:T(8,128)(2,1)}, bf16[6,128,512]{2,1,0:T(8,128)(2,1)}, u32[]{:S(2)}, u32[]{:S(2)}) collective-permute-start(bf16[6,128,512]{2,1,0:T(8,128)(2,1)} %collective-permute-done.10), channel_id=1, source_target_pairs={{0,1},{1,0},{2,3},{3,2},{4,5},{5,4},{6,7},{7,6},{8,9},{9,8},{10,11... | collective-permute-start | bytes 2359304 | tf_op jit(solution)/shard_map/ppermute | solution.py:278
  74.6 0.1 collective-permute-start.21
  74.7 1.3 broadcast_select_fusion.refs_12_.refs_7_.refs_5_
  76.1 6.0 %collective-permute-done.11 = bf16[6,128,512]{2,1,0:T(8,128)(2,1)} collective-permute-done((bf16[6,128,512]{2,1,0:T(8,128)(2,1)}, bf16[6,128,512]{2,1,0:T(8,128)(2,1)}, u32[]{:S(2)}, u32[]{:S(2)}) %collective-permute-start.11) | collective-permute-done | bytes 786464 | tf_op jit(solution)/shard_map/ppermute | solution.py:286
  82.0 2.1 %broadcast_select_fusion.1.refs_10_.refs_5_.refs_3_ = bf16[6,128,512]{2,1,0:T(8,128)(2,1)} fusion(bf16[6,128,512]{2,1,0:T(8,128)(2,1)} %broadcast_select_fusion.3, bf16[6,128,512]{2,1,0:T(8,128)(2,1)} %collective-permute-done.11, pred[]{:T(512)S(6)} %ge.3), kind=kLoop, calls=%fused_computation.5 | loop fusion | flops 393216 | bytes 2359297 | tf_op jit(solution)/shard_map/jit(_where)/select_n | solution.py:321
  84.1 1.6 %collective-permute-start.16 = (bf16[6,128,512]{2,1,0:T(8,128)(2,1)}, bf16[6,128,512]{2,1,0:T(8,128)(2,1)}, u32[]{:S(2)}, u32[]{:S(2)}) collective-permute-start(bf16[6,128,512]{2,1,0:T(8,128)(2,1)} %collective-permute-done.15), channel_id=1, source_target_pairs={{8,12},{5,1},{10,14},{7,3},{24,28},{21,17},{26,30},{23,19}} | collective-permute-start | bytes 2359304 | tf_op jit(solution)/shard_map/ppermute | solution.py:275
  85.7 1.6 %collective-permute-start.5 = (bf16[6,128,512]{2,1,0:T(8,128)(2,1)}, bf16[6,128,512]{2,1,0:T(8,128)(2,1)}, u32[]{:S(2)}, u32[]{:S(2)}) collective-permute-start(bf16[6,128,512]{2,1,0:T(8,128)(2,1)} %collective-permute-done.4), channel_id=1, source_target_pairs={{8,12},{5,1},{10,14},{7,3},{24,28},{21,17},{26,30},{23,19}} | collective-permute-start | bytes 2359304 | tf_op jit(solution)/shard_map/ppermute | solution.py:275
  87.3 11.0 %collective-permute-start.12 = (bf16[6,128,512]{2,1,0:T(8,128)(2,1)}, bf16[6,128,512]{2,1,0:T(8,128)(2,1)}, u32[]{:S(2)}, u32[]{:S(2)}) collective-permute-start(bf16[6,128,512]{2,1,0:T(8,128)(2,1)} %broadcast_select_fusion.1.refs_10_.refs_5_.refs_3_), channel_id=1, source_target_pairs={{0,1},{1,0},{2,3},{3,2},{4,5},{5,4},{6,7},{7,6},{8,9},{9,8},{10,11... | collective-permute-start | bytes 2359304 | tf_op jit(solution)/shard_map/ppermute | solution.py:278
  98.3 0.9 copy-done.7
  99.2 0.9 copy-done.4
  100.1 0.5 collective-permute-start.19
  100.6 0.7 fusion.3
  106.4 0.7 fusion.5
  112.5 0.1 stack.147.where
  112.6 0.1 collective-permute-start.17
  112.7 1.0 collective-permute-start.6
  113.8 1.4 copy-done.3
  115.2 1.1 copy-done.5
  116.3 1.1 copy-done.8
  117.5 10.6 %pairs.4.refs_9_ = bf16[4,6,256,512]{3,2,1,0:T(8,128)(2,1)} custom-call(s32[308]{0:T(512)S(1)} %concatenate.3.ints, s32[13]{0:T(128)S(1)} %stack.147.where, bf16[6,256,512]{2,1,0:T(8,128)(2,1)S(1)} %copy-done.3, bf16[3,256,512]{2,1,0:T(8,128)(2,1)} %bitcast.51.refs_1_, bf16[3,256,512]{2,1,0:T(8,128)(2,1)} %bitcast.52.refs_2_, ...), custom_call_target="tpu_custom_call" | custom-call | flops 8053063680 | bytes 20971520 | tf_op jit(solution)/shard_map/pairs/pallas_call | solution.py:208
  128.1 8.3 %pairs.5.refs_7_ = bf16[4,6,256,512]{3,2,1,0:T(8,128)(2,1)} custom-call(s32[308]{0:T(512)S(1)} %concatenate.3.ints, s32[8]{0:T(128)S(1)} %stack.137.where, bf16[3,256,512]{2,1,0:T(8,128)(2,1)} %bitcast.34.refs_0_, bf16[3,256,512]{2,1,0:T(8,128)(2,1)} %bitcast.35.refs_1_, bf16[3,256,512]{2,1,0:T(8,128)(2,1)} %bitcast.36.refs_2_, ...), custom_call_target="tpu_custom_call", output_to_operand_aliasing={{}: (11, {})} | custom-call | flops 3221225472 | bytes 11534336 | tf_op jit(solution)/shard_map/pairs/pallas_call | solution.py:208
  136.3 5.0 %pairs.6.refs_7_ = bf16[4,6,256,512]{3,2,1,0:T(8,128)(2,1)} custom-call(s32[308]{0:T(512)S(1)} %concatenate.3.ints, s32[6]{0:T(128)S(1)} %stack.132.where, bf16[3,256,512]{2,1,0:T(8,128)(2,1)} %bitcast.26.refs_0_, bf16[3,256,512]{2,1,0:T(8,128)(2,1)S(1)} %bitcast.73, bf16[4,512,512]{2,1,0:T(8,128)(2,1)S(1)} %copy-done, ...), custom_call_target="tpu_custom_call", output_to_operand_aliasing={{}: (9, {})} | custom-call | flops 1610612736 | bytes 8388608 | tf_op jit(solution)/shard_map/pairs/pallas_call | solution.py:208
  141.3 3.8 %pairs.7 = bf16[4,6,256,512]{3,2,1,0:T(8,128)(2,1)} custom-call(s32[308]{0:T(512)S(1)} %concatenate.3.ints, s32[6]{0:T(128)S(1)} %stack.129.where, bf16[3,256,512]{2,1,0:T(8,128)(2,1)} %bitcast.20.refs_0_, bf16[3,256,512]{2,1,0:T(8,128)(2,1)S(1)} %bitcast.72, bf16[4,512,512]{2,1,0:T(8,128)(2,1)S(1)} %copy-done, ...), custom_call_target="tpu_custom_call", output_to_operand_aliasing={{}: (9, {})} | custom-call | flops 1610612736 | bytes 8388608 | tf_op jit(solution)/shard_map/pairs/pallas_call | solution.py:208
  (58 shorter events, 0.6 us)
Async XLA Ops:
  0.0 2.8 %copy-start.1 = (bf16[6,256,512]{2,1,0:T(8,128)(2,1)S(1)}, bf16[6,256,512]{2,1,0:T(8,128)(2,1)}, u32[]{:S(2)}) copy-start(bf16[6,256,512]{2,1,0:T(8,128)(2,1)} %refs_2_.5) | copy-start | bytes 4718596
  2.8 25.6 %copy-start.11 = (s32[24,3]{0,1:T(4,128)S(1)}, s32[24,3]{0,1:T(4,128)}, u32[]{:S(2)}) copy-start(s32[24,3]{0,1:T(4,128)} %param.20) | copy-start | bytes 868
  2.8 25.8 %copy-start.10 = (s32[8,24]{1,0:T(8,128)S(1)}, s32[8,24]{1,0:T(8,128)}, u32[]{:S(2)}) copy-start(s32[8,24]{1,0:T(8,128)} %param.17) | copy-start | bytes 2308
  2.8 25.9 %copy-start.12 = (f32[24,3]{0,1:T(4,128)S(1)}, f32[24,3]{0,1:T(4,128)}, u32[]{:S(2)}) copy-start(f32[24,3]{0,1:T(4,128)} %param.21) | copy-start | bytes 868
  2.9 26.1 %copy-start.17 = (s32[24]{0:T(128)S(1)}, s32[24]{0:T(128)}, u32[]{:S(2)}) copy-start(s32[24]{0:T(128)} %param.18) | copy-start | bytes 292
  2.9 26.2 %copy-start.2 = (bf16[6,256,512]{2,1,0:T(8,128)(2,1)S(1)}, bf16[6,256,512]{2,1,0:T(8,128)(2,1)}, u32[]{:S(2)}) copy-start(bf16[6,256,512]{2,1,0:T(8,128)(2,1)} %refs_0_.1) | copy-start | bytes 4718596
  3.1 14.6 %collective-permute-start = (bf16[6,128,512]{2,1,0:T(8,128)(2,1)S(1)}, bf16[6,128,512]{2,1,0:T(8,128)(2,1)}, u32[]{:S(2)}, u32[]{:S(2)}) collective-permute-start(bf16[6,128,512]{2,1,0:T(8,128)(2,1)S(1)} %get-tuple-element.14), channel_id=1, source_target_pairs={{0,4},{4,8},{8,12},{13,9},{9,5},{5,1},{2,6},{6,10},{10,14},{15,11}... | collective-permute-start | bytes 2359304 | tf_op jit(solution)/shard_map/ppermute | solution.py:275
  9.0 17.0 %collective-permute-start.7 = (bf16[6,128,512]{2,1,0:T(8,128)(2,1)S(1)}, bf16[6,128,512]{2,1,0:T(8,128)(2,1)}, u32[]{:S(2)}, u32[]{:S(2)}) collective-permute-start(bf16[6,128,512]{2,1,0:T(8,128)(2,1)S(1)} %get-tuple-element.13), channel_id=1, source_target_pairs={{0,4},{4,8},{8,12},{13,9},{9,5},{5,1},{2,6},{6,10},{10,14},{15,11}... | collective-permute-start | bytes 2359304 | tf_op jit(solution)/shard_map/ppermute | solution.py:275
  17.6 11.5 %collective-permute-start.2 = (bf16[6,128,512]{2,1,0:T(8,128)(2,1)}, bf16[6,128,512]{2,1,0:T(8,128)(2,1)}, u32[]{:S(2)}, u32[]{:S(2)}) collective-permute-start(bf16[6,128,512]{2,1,0:T(8,128)(2,1)} %collective-permute-done.refs_1_), channel_id=1, source_target_pairs={{0,1},{1,0},{2,3},{3,2},{4,5},{5,4},{6,7},{7,6},{8,9},{9,8},{10,11... | collective-permute-start | bytes 2359304 | tf_op jit(solution)/shard_map/ppermute | solution.py:278
  18.5 10.6 %collective-permute-start.1 = (bf16[6,128,512]{2,1,0:T(8,128)(2,1)}, bf16[6,128,512]{2,1,0:T(8,128)(2,1)}, u32[]{:S(2)}, u32[]{:S(2)}) collective-permute-start(bf16[6,128,512]{2,1,0:T(8,128)(2,1)} %collective-permute-done.refs_1_), channel_id=1, source_target_pairs={{4,8},{9,5},{6,10},{11,7},{20,24},{25,21},{22,26},{27,23}} | collective-permute-start | bytes 2359304 | tf_op jit(solution)/shard_map/ppermute | solution.py:275
  26.0 14.9 %collective-permute-start.9 = (bf16[6,128,512]{2,1,0:T(8,128)(2,1)}, bf16[6,128,512]{2,1,0:T(8,128)(2,1)}, u32[]{:S(2)}, u32[]{:S(2)}) collective-permute-start(bf16[6,128,512]{2,1,0:T(8,128)(2,1)} %collective-permute-done.7.refs_1_), channel_id=1, source_target_pairs={{0,1},{1,0},{2,3},{3,2},{4,5},{5,4},{6,7},{7,6},{8,9},{9,8},{10,11... | collective-permute-start | bytes 2359304 | tf_op jit(solution)/shard_map/ppermute | solution.py:278
  26.9 14.1 %collective-permute-start.8 = (bf16[6,128,512]{2,1,0:T(8,128)(2,1)}, bf16[6,128,512]{2,1,0:T(8,128)(2,1)}, u32[]{:S(2)}, u32[]{:S(2)}) collective-permute-start(bf16[6,128,512]{2,1,0:T(8,128)(2,1)} %collective-permute-done.7.refs_1_), channel_id=1, source_target_pairs={{4,8},{9,5},{6,10},{11,7},{20,24},{25,21},{22,26},{27,23}} | collective-permute-start | bytes 2359304 | tf_op jit(solution)/shard_map/ppermute | solution.py:275
  29.8 24.3 %collective-permute-start.3 = (bf16[6,128,512]{2,1,0:T(8,128)(2,1)S(1)}, bf16[6,128,512]{2,1,0:T(8,128)(2,1)}, u32[]{:S(2)}, u32[]{:S(2)}) collective-permute-start(bf16[6,128,512]{2,1,0:T(8,128)(2,1)S(1)} %get-tuple-element.9), channel_id=1, source_target_pairs={{0,4},{4,8},{8,12},{13,9},{9,5},{5,1},{2,6},{6,10},{10,14},{15,11}... | collective-permute-start | bytes 2359304 | tf_op jit(solution)/shard_map/ppermute | solution.py:275
  41.7 21.0 %collective-permute-start.10 = (bf16[6,128,512]{2,1,0:T(8,128)(2,1)S(1)}, bf16[6,128,512]{2,1,0:T(8,128)(2,1)}, u32[]{:S(2)}, u32[]{:S(2)}) collective-permute-start(bf16[6,128,512]{2,1,0:T(8,128)(2,1)S(1)} %get-tuple-element.11), channel_id=1, source_target_pairs={{0,4},{4,8},{8,12},{13,9},{9,5},{5,1},{2,6},{6,10},{10,14},{15,11}... | collective-permute-start | bytes 2359304 | tf_op jit(solution)/shard_map/ppermute | solution.py:275
  55.3 19.3 %copy-start.9 = (bf16[6,128,512]{2,1,0:T(8,128)(2,1)}, bf16[6,128,512]{2,1,0:T(8,128)(2,1)S(1)}, u32[]{:S(2)}) copy-start(bf16[6,128,512]{2,1,0:T(8,128)(2,1)S(1)} %broadcast_select_fusion.2) | copy-start | bytes 2359300
  55.3 19.3 %collective-permute-start.13 = (bf16[6,128,512]{2,1,0:T(8,128)(2,1)S(1)}, bf16[6,128,512]{2,1,0:T(8,128)(2,1)}, u32[]{:S(2)}, u32[]{:S(2)}) collective-permute-start(bf16[6,128,512]{2,1,0:T(8,128)(2,1)S(1)} %broadcast_select_fusion.2), channel_id=1, source_target_pairs={{1,2},{3,0},{5,6},{7,4},{8,11},{10,9},{12,15},{14,13},{17,18},{19,... | collective-permute-start | bytes 2359304 | tf_op jit(solution)/shard_map/ppermute | solution.py:286
  64.8 17.3 %collective-permute-start.11 = (bf16[6,128,512]{2,1,0:T(8,128)(2,1)}, bf16[6,128,512]{2,1,0:T(8,128)(2,1)}, u32[]{:S(2)}, u32[]{:S(2)}) collective-permute-start(bf16[6,128,512]{2,1,0:T(8,128)(2,1)} %broadcast_select_fusion.3), channel_id=1, source_target_pairs={{1,2},{3,0},{5,6},{7,4},{8,11},{10,9},{12,15},{14,13},{17,18},{19,... | collective-permute-start | bytes 2359304 | tf_op jit(solution)/shard_map/ppermute | solution.py:286
  66.1 18.1 %collective-permute-start.15 = (bf16[6,128,512]{2,1,0:T(8,128)(2,1)}, bf16[6,128,512]{2,1,0:T(8,128)(2,1)}, u32[]{:S(2)}, u32[]{:S(2)}) collective-permute-start(bf16[6,128,512]{2,1,0:T(8,128)(2,1)} %collective-permute-done.10), channel_id=1, source_target_pairs={{4,8},{8,12},{9,5},{5,1},{6,10},{10,14},{11,7},{7,3},{20,24},{24,2... | collective-permute-start | bytes 2359304 | tf_op jit(solution)/shard_map/ppermute | solution.py:275
  67.6 18.1 %collective-permute-start.4 = (bf16[6,128,512]{2,1,0:T(8,128)(2,1)}, bf16[6,128,512]{2,1,0:T(8,128)(2,1)}, u32[]{:S(2)}, u32[]{:S(2)}) collective-permute-start(bf16[6,128,512]{2,1,0:T(8,128)(2,1)} %collective-permute-done.3), channel_id=1, source_target_pairs={{4,8},{8,12},{9,5},{5,1},{6,10},{10,14},{11,7},{7,3},{20,24},{24,2... | collective-permute-start | bytes 2359304 | tf_op jit(solution)/shard_map/ppermute | solution.py:275
  69.2 18.1 %collective-permute-start.20 = (bf16[6,128,512]{2,1,0:T(8,128)(2,1)}, bf16[6,128,512]{2,1,0:T(8,128)(2,1)}, u32[]{:S(2)}, u32[]{:S(2)}) collective-permute-start(bf16[6,128,512]{2,1,0:T(8,128)(2,1)} %collective-permute-done.10), channel_id=1, source_target_pairs={{0,1},{1,0},{2,3},{3,2},{4,5},{5,4},{6,7},{7,6},{8,9},{9,8},{10,11... | collective-permute-start | bytes 2359304 | tf_op jit(solution)/shard_map/ppermute | solution.py:278
  74.6 26.0 %copy-start.15 = (s32[4]{0:T(128)S(1)}, s32[4]{0:T(128)}, u32[]{:S(2)}) copy-start(s32[4]{0:T(128)} %constant.42.clone) | copy-start | bytes 52
  74.6 26.0 %copy-start.16 = (s32[4]{0:T(128)S(1)}, s32[4]{0:T(128)}, u32[]{:S(2)}) copy-start(s32[4]{0:T(128)} %constant.43.clone) | copy-start | bytes 52
  74.6 31.8 %copy-start.13 = (s32[4]{0:T(128)S(1)}, s32[4]{0:T(128)}, u32[]{:S(2)}) copy-start(s32[4]{0:T(128)} %constant.44.clone) | copy-start | bytes 52
  74.6 31.8 %copy-start.14 = (s32[4]{0:T(128)S(1)}, s32[4]{0:T(128)}, u32[]{:S(2)}) copy-start(s32[4]{0:T(128)} %constant.45.clone) | copy-start | bytes 52
  74.6 39.2 %copy-start = (bf16[4,512,512]{2,1,0:T(8,128)(2,1)S(1)}, bf16[4,512,512]{2,1,0:T(8,128)(2,1)}, u32[]{:S(2)}) copy-start(bf16[4,512,512]{2,1,0:T(8,128)(2,1)} %refs_2_.7) | copy-start | bytes 6291460
  74.6 23.7 %collective-permute-start.21 = (bf16[6,128,512]{2,1,0:T(8,128)(2,1)}, bf16[6,128,512]{2,1,0:T(8,128)(2,1)S(1)}, u32[]{:S(2)}, u32[]{:S(2)}) collective-permute-start(bf16[6,128,512]{2,1,0:T(8,128)(2,1)} %collective-permute-done.3), channel_id=1, source_target_pairs={{0,1},{1,0},{2,3},{3,2},{4,5},{5,4},{6,7},{7,6},{8,9},{9,8},{10,11... | collective-permute-start | bytes 2359304 | tf_op jit(solution)/shard_map/ppermute | solution.py:278
  82.0 17.2 %collective-permute-start.14 = (bf16[6,128,512]{2,1,0:T(8,128)(2,1)S(1)}, bf16[6,128,512]{2,1,0:T(8,128)(2,1)S(1)}, u32[]{:S(2)}, u32[]{:S(2)}) collective-permute-start(bf16[6,128,512]{2,1,0:T(8,128)(2,1)S(1)} %broadcast_select_fusion.refs_12_.refs_7_.refs_5_), channel_id=1, source_target_pairs={{0,1},{1,0},{2,3},{3,2},{4,5},{5,4},{6,7},{7,6},{8,9},{9,8},{10,11... | collective-permute-start | bytes 2359304 | tf_op jit(solution)/shard_map/ppermute | solution.py:278
  84.1 28.5 %collective-permute-start.16 = (bf16[6,128,512]{2,1,0:T(8,128)(2,1)}, bf16[6,128,512]{2,1,0:T(8,128)(2,1)}, u32[]{:S(2)}, u32[]{:S(2)}) collective-permute-start(bf16[6,128,512]{2,1,0:T(8,128)(2,1)} %collective-permute-done.15), channel_id=1, source_target_pairs={{8,12},{5,1},{10,14},{7,3},{24,28},{21,17},{26,30},{23,19}} | collective-permute-start | bytes 2359304 | tf_op jit(solution)/shard_map/ppermute | solution.py:275
  85.7 27.0 %collective-permute-start.5 = (bf16[6,128,512]{2,1,0:T(8,128)(2,1)}, bf16[6,128,512]{2,1,0:T(8,128)(2,1)}, u32[]{:S(2)}, u32[]{:S(2)}) collective-permute-start(bf16[6,128,512]{2,1,0:T(8,128)(2,1)} %collective-permute-done.4), channel_id=1, source_target_pairs={{8,12},{5,1},{10,14},{7,3},{24,28},{21,17},{26,30},{23,19}} | collective-permute-start | bytes 2359304 | tf_op jit(solution)/shard_map/ppermute | solution.py:275
  87.3 26.5 %collective-permute-start.12 = (bf16[6,128,512]{2,1,0:T(8,128)(2,1)}, bf16[6,128,512]{2,1,0:T(8,128)(2,1)}, u32[]{:S(2)}, u32[]{:S(2)}) collective-permute-start(bf16[6,128,512]{2,1,0:T(8,128)(2,1)} %broadcast_select_fusion.1.refs_10_.refs_5_.refs_3_), channel_id=1, source_target_pairs={{0,1},{1,0},{2,3},{3,2},{4,5},{5,4},{6,7},{7,6},{8,9},{9,8},{10,11... | collective-permute-start | bytes 2359304 | tf_op jit(solution)/shard_map/ppermute | solution.py:278
  98.3 0.9 copy-start.7
  99.2 28.9 %collective-permute-start.18 = (bf16[6,128,512]{2,1,0:T(8,128)(2,1)}, bf16[6,128,512]{2,1,0:T(8,128)(2,1)}, u32[]{:S(2)}, u32[]{:S(2)}) collective-permute-start(bf16[6,128,512]{2,1,0:T(8,128)(2,1)} %collective-permute-done.15), channel_id=1, source_target_pairs={{0,1},{1,0},{2,3},{3,2},{4,5},{5,4},{6,7},{7,6},{8,9},{9,8},{10,11... | collective-permute-start | bytes 2359304 | tf_op jit(solution)/shard_map/ppermute | solution.py:278
  99.2 0.9 copy-start.4
  100.1 27.9 %collective-permute-start.19 = (bf16[6,128,512]{2,1,0:T(8,128)(2,1)}, bf16[6,128,512]{2,1,0:T(8,128)(2,1)}, u32[]{:S(2)}, u32[]{:S(2)}) collective-permute-start(bf16[6,128,512]{2,1,0:T(8,128)(2,1)} %collective-permute-done.4), channel_id=1, source_target_pairs={{0,1},{1,0},{2,3},{3,2},{4,5},{5,4},{6,7},{7,6},{8,9},{9,8},{10,11... | collective-permute-start | bytes 2359304 | tf_op jit(solution)/shard_map/ppermute | solution.py:278
  112.6 23.7 %collective-permute-start.17 = (bf16[6,128,512]{2,1,0:T(8,128)(2,1)}, bf16[6,128,512]{2,1,0:T(8,128)(2,1)S(1)}, u32[]{:S(2)}, u32[]{:S(2)}) collective-permute-start(bf16[6,128,512]{2,1,0:T(8,128)(2,1)} %collective-permute-done.16), channel_id=1, source_target_pairs={{0,1},{1,0},{2,3},{3,2},{4,5},{5,4},{6,7},{7,6},{8,9},{9,8},{10,11... | collective-permute-start | bytes 2359304 | tf_op jit(solution)/shard_map/ppermute | solution.py:278
  112.7 28.6 %collective-permute-start.6 = (bf16[6,128,512]{2,1,0:T(8,128)(2,1)}, bf16[6,128,512]{2,1,0:T(8,128)(2,1)S(1)}, u32[]{:S(2)}, u32[]{:S(2)}) collective-permute-start(bf16[6,128,512]{2,1,0:T(8,128)(2,1)} %collective-permute-done.5), channel_id=1, source_target_pairs={{0,1},{1,0},{2,3},{3,2},{4,5},{5,4},{6,7},{7,6},{8,9},{9,8},{10,11... | collective-permute-start | bytes 2359304 | tf_op jit(solution)/shard_map/ppermute | solution.py:278
  113.8 1.4 copy-start.3
  115.2 1.1 copy-start.5
  116.3 1.1 copy-start.8
  117.5 10.6 %copy-start.6 = (bf16[6,128,512]{2,1,0:T(8,128)(2,1)S(1)}, bf16[6,128,512]{2,1,0:T(8,128)(2,1)}, u32[]{:S(2)}) copy-start(bf16[6,128,512]{2,1,0:T(8,128)(2,1)} %copy-done.4) | copy-start | bytes 2359300

commit v2 on v1

--- a/solution.py
+++ b/solution.py
@@ -8,10 +8,13 @@
 from jax.sharding import PartitionSpec as P
 
 ANY = pl.BlockSpec(memory_space=pl.ANY)
+HBM = pl.BlockSpec(memory_space=pltpu.HBM)
 SMEM = pl.BlockSpec(memory_space=pltpu.SMEM)
 VMEM = pl.BlockSpec(memory_space=pltpu.VMEM)
 BF16 = jnp.bfloat16
 LIMIT = 40 << 20
+LARGE = 60 << 20
+MEDIUM = 28 << 20
 
 
 def mix_kernel(dims, picks, places, rows_at, ints, coef, *refs):
@@ -259,99 +262,417 @@
     return pairs(dims, ints, where, [gather(ground_state)], op_matrices, [env_rows], None)
 
 
+DEPTH = 4
+GROW_COST = 40 * 10**9
+MIX_WIDTH = 8
+LIST = 16
+
+
+def device_place():
+    owner, core = lax.axis_index("sec"), lax.axis_index("op")
+    return owner, core, jnp.where(core == 0, owner, 3 - owner)
+
+
+def by_spot(spot, values):
+    result = jnp.int32(values[0])
+    for n in range(1, 4):
+        result = jnp.where(spot == n, values[n], result)
+    return result
+
+
+def head_kernel(env, ground, first, second, sems):
+    _, _, spot = device_place()
+    half = env.shape[1] // 2
+
+    def send(sources):
+        copies = [pltpu.make_async_copy(sources[h], (first, second)[h], sems.at[h]) for h in range(2)]
+        for copy in copies:
+            copy.start()
+        for copy in copies:
+            copy.wait()
+
+    pl.when(spot == 2)(lambda: send([ground.at[h] for h in range(2)]))
+    pl.when(spot != 2)(lambda: send([env.at[:, pl.ds(h * half, half)] for h in range(2)]))
+
+
+def head(env_ground, ground_half):
+    sec_dev, rows, columns = env_ground.shape
+    block = jax.ShapeDtypeStruct((sec_dev, rows // 2, columns), BF16)
+    return pl.pallas_call(
+        head_kernel,
+        out_shape=[block, block],
+        in_specs=[HBM, HBM],
+        out_specs=[VMEM, VMEM],
+        scratch_shapes=[pltpu.SemaphoreType.DMA((2,))],
+        compiler_params=pltpu.CompilerParams(vmem_limit_bytes=LARGE),
+        cost_estimate=pl.CostEstimate(flops=0, bytes_accessed=4 * sec_dev * rows * columns, transcendentals=0),
+        name="head",
+    )(env_ground, ground_half)
+
+
+def tables_kernel(dims, ops_dev, shift, slot, src, table, inverse):
+    ops, sectors, sec_dev, terms = dims
+    owner, core, _ = device_place()
+    ahead = jnp.where(core == 0, jnp.minimum(owner + 1, 3), jnp.maximum(owner - 1, 0))
+
+    def invert(t, carry):
+        inverse[slot[t]] = t
+        return carry
+
+    lax.fori_loop(0, sectors, invert, 0)
+
+    def terms_of(i, carry):
+        place = jnp.where(i < sec_dev, ahead * sec_dev + i, owner * sec_dev + i - sec_dev)
+        t = inverse[place]
+        table[i * MIX_WIDTH] = t
+        for k in range(terms):
+            source = src[k, t]
+            from_owner = source // sec_dev
+            table[i * MIX_WIDTH + 1 + 2 * k] = jnp.where(core == 0, from_owner, 3 - from_owner)
+            table[i * MIX_WIDTH + 2 + 2 * k] = source - from_owner * sec_dev
+        return carry
+
+    lax.fori_loop(0, 2 * sec_dev, terms_of, 0)
+    count_at = 2 * sec_dev * MIX_WIDTH
+    list_at = count_at + 8
+    width = sec_dev // 2
+
+    def pairs_of(n, carry):
+        total = jnp.int32(0)
+        for s in range(width):
+            for o in range(ops_dev):
+                local = slot[shift[core * ops_dev + o, n * width + s]] - owner * sec_dev
+                table[list_at + n * LIST + total] = (s * ops_dev + o) * sec_dev + local
+                total = total + jnp.logical_and(local >= 0, local < sec_dev).astype(jnp.int32)
+        table[count_at + n] = total
+        return carry
+
+    lax.fori_loop(0, sectors // width, pairs_of, 0)
+
+
+def tables(dims, ops_dev, shift_map, new_slot, env_src):
+    ops, sectors, sec_dev, terms = dims
+    return pl.pallas_call(
+        functools.partial(tables_kernel, dims, ops_dev),
+        out_shape=jax.ShapeDtypeStruct((2 * sec_dev * MIX_WIDTH + 8 + 8 * LIST,), jnp.int32),
+        in_specs=[SMEM, SMEM, SMEM],
+        out_specs=SMEM,
+        scratch_shapes=[pltpu.SMEM((sectors,), jnp.int32)],
+        cost_estimate=pl.CostEstimate(flops=10000, bytes_accessed=4000, transcendentals=0),
+        name="tables",
+    )(shift_map, new_slot, env_src)
+
+
+def blend_kernel(dims, which, table, coef, second, first, env, other, ground, passed, made, held, sems):
+    ops, sectors, sec_dev, terms = dims
+    _, _, spot = device_place()
+    height = held.shape[2]
+    sources = [second, first, env.at[:, pl.ds(which * height, height)], other]
+
+    @pl.when(spot == 2)
+    def _():
+        def fetch(i, carry):
+            for k in range(terms):
+                code, block = table[i * MIX_WIDTH + 1 + 2 * k], table[i * MIX_WIDTH + 2 + 2 * k]
+                for q in range(4):
+
+                    @pl.when(code == q)
+                    def _(q=q, k=k, block=block):
+                        pltpu.make_async_copy(sources[q].at[block], held.at[i, k], sems.at[i]).start()
+
+            return carry
+
+        lax.fori_loop(0, 2 * sec_dev, fetch, 0)
+
+        def sums(out, lead):
+            def one(i, carry):
+                at = i + lead
+                pltpu.make_async_copy(held.at[at], held.at[at], sems.at[at]).wait()
+                t = table[at * MIX_WIDTH]
+                weights = [coef[k, t] for k in range(terms)]
+                for r in range(0, height, 32):
+                    total = weights[0] * held[at, 0, r : r + 32].astype(jnp.float32)
+                    for k in range(1, terms):
+                        total += weights[k] * held[at, k, r : r + 32].astype(jnp.float32)
+                    out[i, r : r + 32] = total.astype(BF16)
+                return carry
+
+            lax.fori_loop(0, sec_dev, one, 0)
+
+        sums(passed, 0)
+        sums(made, sec_dev)
+
+    @pl.when(spot != 2)
+    def _():
+        copy = pltpu.make_async_copy(ground.at[which], passed, sems.at[0])
+        copy.start()
+        copy.wait()
+
+
+def blend(dims, which, table, coef, second, first, env_ground, other, ground_half):
+    ops, sectors, sec_dev, terms = dims
+    block = jax.ShapeDtypeStruct(first.shape, BF16)
+    _, height, columns = first.shape
+    return pl.pallas_call(
+        functools.partial(blend_kernel, dims, which),
+        out_shape=[block, block],
+        in_specs=[SMEM, SMEM] + [HBM] * 5,
+        out_specs=[VMEM, VMEM],
+        scratch_shapes=[
+            pltpu.VMEM((2 * sec_dev, terms, height, columns), BF16),
+            pltpu.SemaphoreType.DMA((2 * sec_dev,)),
+        ],
+        compiler_params=pltpu.CompilerParams(vmem_limit_bytes=MEDIUM),
+        cost_estimate=pl.CostEstimate(
+            flops=4 * terms * sec_dev * height * columns,
+            bytes_accessed=4 * (terms + 1) * sec_dev * height * columns,
+            transcendentals=0,
+        ),
+        name="blend",
+    )(table, coef, second, first, env_ground, other, ground_half)
+
+
+def half_owner(owner, core, spot, hops, h, sibling):
+    if hops is None:
+        return 2 * owner + h
+    n = by_spot(3 - spot if sibling else spot, hops)
+    back = jnp.where(core == 0, -1, 1) * (-1 if sibling else 1)
+    return jnp.where(n > 0, 2 * (owner + back * n) + h, -1)
+
+
+def grow_kernel(dims, ops_dev, parts, arrays, table, *refs):
+    ops, sectors, sec_dev, terms = dims
+    grounds, op_ref, refs = refs[:arrays], refs[arrays], refs[arrays + 1 :]
+    owner, core, spot = device_place()
+    rows, columns = grounds[0].shape[1:]
+    width = sec_dev // 2
+    pieces, (out_ref, env, found, ground, result, ground_sem, out_sem, env_sem) = refs[:16], refs[16:]
+    count_at = 2 * sec_dev * MIX_WIDTH
+    list_at = count_at + 8
+    part_of = [half_owner(owner, core, spot, hops, h, sibling) for _, hops, h, sibling, _ in parts]
+    for m, (n, _, _, _, lead) in enumerate(parts):
+
+        @pl.when(part_of[m] >= 0)
+        def _(m=m, n=n, lead=lead):
+            source = grounds[n].at[pl.ds(lead, width)]
+            pltpu.make_async_copy(source, ground.at[pl.ds(m * width, width)], ground_sem.at[m]).start()
+
+    env_copies = []
+    half = rows // 2
+    own = lax.axis_index("blk") * rows
+    for n, start in enumerate((own, rows - own, own + half, rows - own + half)):
+        target = env.at[:, pl.ds(pl.multiple_of(start, half), half)]
+        for q in range(4):
+
+            @pl.when(spot == q)
+            def _(n=n, q=q, target=target):
+                pltpu.make_async_copy(pieces[4 * n + q], target, env_sem.at[n]).start()
+
+        env_copies.append(pltpu.make_async_copy(target, target, env_sem.at[n]))
+
+    total = jnp.int32(0)
+    for m in range(len(parts)):
+        part = part_of[m]
+        count = jnp.where(part >= 0, table[count_at + jnp.maximum(part, 0)], 0)
+
+        def take(i, carry, total=total, part=part, m=m):
+            entry = table[list_at + part * LIST + i]
+            rest = entry // sec_dev
+            found[0, total + i] = m * width + rest // ops_dev
+            found[1, total + i] = lax.rem(rest, ops_dev)
+            found[2, total + i] = lax.rem(entry, sec_dev)
+            return carry
+
+        lax.fori_loop(0, count, take, 0)
+        total = total + count
+    for copy in env_copies:
+        copy.wait()
+    for m in range(len(parts)):
+
+        @pl.when(part_of[m] >= 0)
+        def _(m=m):
+            here = ground.at[pl.ds(m * width, width)]
+            pltpu.make_async_copy(here, here, ground_sem.at[m]).wait()
+
+    def drain(side):
+        pltpu.make_async_copy(result.at[side], result.at[side], out_sem.at[side]).wait()
+
+    def step(i, carry):
+        side = lax.rem(i, DEPTH)
+        o, local = found[1, i], found[2, i]
+        product = jnp.dot(ground[found[0, i]], op_ref[o], preferred_element_type=jnp.float32).astype(BF16)
+        grown = jnp.dot(product, env[local], preferred_element_type=jnp.float32).astype(BF16)
+        pl.when(i >= DEPTH)(lambda: drain(side))
+        result[side] = grown
+        pltpu.make_async_copy(result.at[side], out_ref.at[o, local], out_sem.at[side]).start()
+        return carry
+
+    lax.fori_loop(0, total, step, 0)
+    for back in range(1, DEPTH + 1):
+        pl.when(total >= back)(lambda back=back: drain(lax.rem(total - back, DEPTH)))
+
+
+def grow(dims, table, parts, grounds, op_matrices, pieces):
+    ops, sectors, sec_dev, terms = dims
+    ops_dev = op_matrices.shape[0]
+    rows, columns = grounds[0].shape[1:]
+    return pl.pallas_call(
+        functools.partial(grow_kernel, dims, ops_dev, parts, len(grounds)),
+        out_shape=[
+            jax.ShapeDtypeStruct((ops_dev, sec_dev, rows, columns), BF16),
+            jax.ShapeDtypeStruct((sec_dev, columns, columns), BF16),
+        ],
+        in_specs=[SMEM] + [ANY] * len(grounds) + [VMEM] + [ANY] * len(pieces),
+        out_specs=[ANY, VMEM],
+        scratch_shapes=[
+            pltpu.SMEM((3, LIST * len(parts)), jnp.int32),
+            pltpu.VMEM((sec_dev // 2 * len(parts), rows, columns), BF16),
+            pltpu.VMEM((DEPTH, rows, columns), BF16),
+            pltpu.SemaphoreType.DMA((len(parts),)),
+            pltpu.SemaphoreType.DMA((DEPTH,)),
+            pltpu.SemaphoreType.DMA((4,)),
+        ],
+        compiler_params=pltpu.CompilerParams(vmem_limit_bytes=MEDIUM),
+        cost_estimate=pl.CostEstimate(flops=1 << 20, bytes_accessed=1 << 12, transcendentals=0),
+        name="grow",
+    )(table, *grounds, op_matrices, *pieces)
+
+
+def finish_kernel(dims, ops_dev, table, own_a, other_a, own_b, other_b, op_ref, env, _, out_ref, found, result, out_sem):
+    ops, sectors, sec_dev, terms = dims
+    owner, core, spot = device_place()
+    count_at = 2 * sec_dev * MIX_WIDTH
+    list_at = count_at + 8
+    total = jnp.int32(0)
+    for h in range(2):
+        part = jnp.where(spot == 3, half_owner(owner, core, spot, [0, 0, 0, 3], h, False), -1)
+        part = jnp.where(spot == 0, half_owner(owner, core, spot, [0, 0, 0, 3], h, True), part)
+        count = jnp.where(part >= 0, table[count_at + jnp.maximum(part, 0)], 0)
+
+        def take(n, carry, part=part, total=total, h=h):
+            entry = table[list_at + part * LIST + n]
+            rest = entry // sec_dev
+            found[0, total + n] = h
+            found[1, total + n] = rest // ops_dev
+            found[2, total + n] = lax.rem(rest, ops_dev)
+            found[3, total + n] = lax.rem(entry, sec_dev)
+            return carry
+
+        lax.fori_loop(0, count, take, 0)
+        total = total + count
+
+    def drain(side):
+        pltpu.make_async_copy(result.at[side], result.at[side], out_sem.at[side]).wait()
+
+    def step(i, carry):
+        side = lax.rem(i, DEPTH)
+        h, s, o, local = (found[k, i] for k in range(4))
+        first = jnp.where(spot == 3, own_a[s], other_a[s])
+        second = jnp.where(spot == 3, own_b[s], other_b[s])
+        block = jnp.where(h == 0, first, second)
+        product = jnp.dot(block, op_ref[o], preferred_element_type=jnp.float32).astype(BF16)
+        grown = jnp.dot(product, env[local], preferred_element_type=jnp.float32).astype(BF16)
+        pl.when(i >= DEPTH)(lambda: drain(side))
+        result[side] = grown
+        pltpu.make_async_copy(result.at[side], out_ref.at[o, local], out_sem.at[side]).start()
+        return carry
+
+    lax.fori_loop(0, total, step, 0)
+    for back in range(1, DEPTH + 1):
+        pl.when(total >= back)(lambda back=back: drain(lax.rem(total - back, DEPTH)))
+
+
+def finish(dims, table, ends, op_matrices, env, out):
+    ops, sectors, sec_dev, terms = dims
+    ops_dev, _, rows, columns = out.shape
+    return pl.pallas_call(
+        functools.partial(finish_kernel, dims, ops_dev),
+        out_shape=jax.ShapeDtypeStruct(out.shape, BF16),
+        in_specs=[SMEM] + [VMEM] * 6 + [ANY],
+        out_specs=ANY,
+        scratch_shapes=[
+            pltpu.SMEM((4, sec_dev * ops_dev), jnp.int32),
+            pltpu.VMEM((DEPTH, rows, columns), BF16),
+            pltpu.SemaphoreType.DMA((DEPTH,)),
+        ],
+        input_output_aliases={7: 0},
+        compiler_params=pltpu.CompilerParams(vmem_limit_bytes=MEDIUM),
+        cost_estimate=pl.CostEstimate(flops=GROW_COST, bytes_accessed=1 << 20, transcendentals=0),
+        name="finish",
+    )(table, *ends, op_matrices, env, out)
+
+
 def line_of_four(ground_state, op_matrices, shift_map, new_slot, env_ground, env_src, env_coef):
-    owner = lax.axis_index("sec")
-    group = lax.axis_index("op")
-    row_half = lax.axis_index("blk")
     sec_dev, rows, columns = ground_state.shape
     ops, sectors = shift_map.shape
+    ops_dev = op_matrices.shape[0]
     dims = (ops, sectors, sec_dev, env_src.shape[1])
     half = rows // 2
-    spot = jnp.where(group == 0, owner, 3 - owner)
 
     def stream(steps):
         up = [(2 * a, 2 * a + 2) for a in steps]
         down = [(2 * (3 - a) + 1, 2 * (2 - a) + 1) for a in steps]
         return lambda block: lax.ppermute(block, ("sec", "op"), up + down)
 
-    def swap(block):
-        return lax.ppermute(block, "op", [(0, 1), (1, 0)])
-
-    def across(block):
-        pairs_of = []
-        for z in range(4):
-            lead = 0 if z >= 2 else 1
-            for x in range(2):
-                pairs_of.append(((z * 2 + x) * 2 + lead, (z * 2 + 1 - x) * 2 + 1 - lead))
+    def hand(block, spots):
+        pairs_of = [(2 * z + core, 2 * z + 1 - core) for spot in spots for z, core in at[spot]]
+        return lax.ppermute(block, ("sec", "op"), pairs_of)
+
+    def across(block, spot):
+        pairs_of = [((z * 2 + x) * 2 + core, (z * 2 + 1 - x) * 2 + 1 - core) for z, core in at[spot] for x in range(2)]
         return lax.ppermute(block, ("sec", "blk", "op"), pairs_of)
 
+    def after(block, *others):
+        return lax.optimization_barrier((block, *others))[0]
+
+    at = [[(0, 0), (3, 1)], [(1, 0), (2, 1)], [(2, 0), (1, 1)], [(3, 0), (0, 1)]]
     every, middle, late, last = stream([0, 1, 2]), stream([1]), stream([1, 2]), stream([2])
     ground_half = ground_state.reshape(2, sec_dev, half, columns)
-    env_half = env_ground.reshape(sec_dev, 2, half, columns)
-    is_two = spot == 2
-    ahead = jnp.where(group == 0, owner + 1, owner - 1)
-    code = [jnp.where(group == 0, w, 3 - w) for w in range(4)]
-    position = [owner, ahead, is_two, group] + [jnp.zeros((), jnp.int32)] * 12 + code
-    coef = env_coef.reshape(-1)
-
-    sent0 = [jnp.where(is_two, ground_half[h], env_half[:, h]) for h in range(2)]
-    got0 = [every(sent0[h]) for h in range(2)]
-    got2 = [middle(got0[h]) for h in range(2)]
-    swapped0 = [swap(got0[h]) for h in range(2)]
-    ints = pack(shift_map, new_slot, env_src, position)
-    sent4, env_new = [], []
-    for h in range(2):
-        passed, made = mix(
-            dims, ints, coef, [got2[h], got0[h], env_ground, swapped0[h]], [None, None, h * half, None], [1, 0],
-            half, ground_half, h,
-        )
-        sent4.append(passed)
-        env_new.append(made)
-    got4 = [every(sent4[h]) for h in range(2)]
-    got6 = [late(got4[h]) for h in range(2)]
-    got8 = [last(got6[h]) for h in range(2)]
-    swapped4 = [swap(got4[h]) for h in range(2)]
-    swapped6 = [swap(got6[h]) for h in range(2)]
-    swapped8 = [swap(got8[h]) for h in range(2)]
-    env_pieces, env_starts = [], []
-    lead = spot >= 2
-    for h in range(2):
-        mine = jnp.where(is_two, env_new[h], got4[h])
-        received = across(mine)
-        kept = jnp.where(lead, mine, received)
-        env_pieces += [kept, swap(kept)]
-        own, far = row_half * rows + h * half, (1 - row_half) * rows + h * half
-        env_starts += [jnp.where(lead, own, far), jnp.where(lead, far, own)]
-
-    step = jnp.where(group == 0, -1, 1)
-
-    def base(own_hops, h):
-        hops = jnp.asarray(own_hops, jnp.int32)
-        own = jnp.where(hops[spot] > 0, (owner + step * hops[spot]) * sec_dev + h * (sec_dev // 2), -1)
-        other = hops[3 - spot]
-        theirs = jnp.where(other > 0, (owner - step * other) * sec_dev + h * (sec_dev // 2), -1)
-        return [own, theirs]
-
-    def blocks(block):
-        return block.reshape(sec_dev // 2, rows, columns)
-
-    def stage(out, arrays, bases):
-        where = jnp.stack([jnp.asarray(b, jnp.int32) for b in bases + env_starts])
-        return pairs(dims, ints, where, arrays, op_matrices, env_pieces, out)
-
-    arrays, bases = [ground_state], [owner * sec_dev]
-    for h in range(2):
-        arrays += [blocks(got0[h]), blocks(swapped0[h]), blocks(got4[h]), blocks(swapped4[h])]
-        bases += base([0, 0, 0, 1], h) + base([0, 1, 1, 0], h)
-    out = stage(None, arrays, bases)
-    arrays, bases = [], []
-    for h in range(2):
-        arrays += [blocks(got6[h]), blocks(swapped6[h])]
-        bases += base([0, 0, 2, 2], h)
-    out = stage(out, arrays, bases)
-    for h in range(2):
-        out = stage(out, [blocks(got8[h]), blocks(swapped8[h])], base([0, 0, 0, 3], h))
-    return out
+    both = range(2)
+
+    sent0 = head(env_ground, ground_half)
+    got0 = [every(sent0[h]) for h in both]
+    got2 = [middle(got0[h]) for h in both]
+    swapped0 = [hand(got0[h], [1, 3]) for h in both]
+    table = tables(dims, ops_dev, shift_map, new_slot, env_src.T)
+    sent4, made = zip(
+        *[blend(dims, h, table, env_coef.T, got2[h], got0[h], env_ground, swapped0[h], ground_half) for h in both]
+    )
+    got4 = [every(sent4[h]) for h in both]
+    got6 = [late(got4[h]) for h in both]
+    far1 = [across(after(made[0], got2[1]), 2), across(after(made[1], got4[0]), 2)]
+    far2 = [across(got4[0], 3), across(got4[1], 3)]
+    near1 = [hand(after(made[0], got4[1]), [2]), hand(after(made[1], got4[1]), [2])]
+    back1 = [hand(after(far1[0], got4[1]), [1]), hand(after(far1[1], got4[1]), [1])]
+    swapped4 = [hand(after(got4[0], got4[1]), [1, 2, 3]), hand(after(got4[1], far2[0]), [1, 2, 3])]
+    back2 = [hand(far2[0], [0]), hand(after(far2[1], got6[1]), [0])]
+    swapped6 = [hand(after(got6[h], got6[1]), [2, 3]) for h in both]
+    got8 = [
+        last(after(got6[0], *far1, far2[0], near1[0], back1[0], swapped4[0])),
+        last(after(got6[1], *near1, *back1, back2[0], *swapped4)),
+    ]
+    pieces = []
+    for h in both:
+        pieces += [swapped4[h], near1[h], made[h], got4[h]]
+        pieces += [far2[h], far1[h], back1[h], back2[h]]
+
+    parts = [(0, None, h, False, h * sec_dev // 2) for h in both]
+    arrays = [ground_state]
+
+    def hold(mine, theirs, hops, h):
+        for block, sibling in ((mine, False), (theirs, True)):
+            parts.append((len(arrays), hops, h, sibling, 0))
+            arrays.append(block.reshape(sec_dev // 2, rows, columns))
+
+    for h in both:
+        hold(got0[h], swapped0[h], [0, 0, 0, 1], h)
+        hold(got4[h], swapped4[h], [0, 1, 1, 0], h)
+    for h in both:
+        hold(got6[h], swapped6[h], [0, 0, 2, 2], h)
+    out, env = grow(dims, table, parts, arrays, op_matrices, pieces)
+    swapped8 = [hand(after(got8[h], out), [3]) for h in both]
+    ends = [block[h].reshape(sec_dev // 2, rows, columns) for h in both for block in (got8, swapped8)]
+    return finish(dims, table, ends, op_matrices, env, out)
 
 
 def solution(mesh):

time: 148 us -> 119 us (0.80); the launches traced: 145 us -> 118 us
  waiting for transfers between devices: 21.8 us -> 34.2 us
  between operations: 10.6 us -> 0.44 us
  local copies, waits for them, and re-layouts: 10.6 us -> 0.7 us
  starting transfers between devices: 66.2 us -> 58.3 us
  other arithmetic: 6.97 us -> 0 us
  Pallas kernels: 29 us -> 24.2 us
    ppermute x10, starting transfers between devices: 43.7 us -> 29.6 us  [stream(): return lambda block: lax.ppermute(block, ('sec', 'op'), up + down)]
    ppermute x10 -> x14, waiting for transfers between devices: 0.03 us -> 9.67 us  [hand(): return lax.ppermute(block, ('sec', 'op'), pairs_of)]
    select_n x5 -> x0, other arithmetic: 6.97 us -> none  [the longest x2 3.45 us: line_of_four(): kept = jnp.where(lead, mine, received)]
    unnamed x38 -> x12, local copies, waits for them, and re-layouts: 5.7 us -> 0.7 us
    ppermute x10 -> x14, starting transfers between devices: 19.9 us -> 24.8 us  [hand(): return lax.ppermute(block, ('sec', 'op'), pairs_of)]
    pallas_call x6, Pallas kernels: 29 us -> 24.2 us  [the longest x1 12.7 us: grow(): pl.pallas_call(functools.partial(grow_kernel, dims, ops_dev, parts, len(g...]
    slice x1 -> x0, local copies, waits for them, and re-layouts: 2.83 us -> none  [line_of_four(): ground_half[h]]
    ppermute x10, waiting for transfers between devices: 15.8 us -> 17.8 us  [stream(): return lambda block: lax.ppermute(block, ('sec', 'op'), up + down)]
  transfers between devices with their start and end apart: 22 -> 28, of which waited for: 4 -> 9; matrix products, arithmetic and copies ran while one was open for 6% -> 0% of each run, Pallas kernels for 17% -> 14%
where the time goes in v2:
time: 119 us; the launch traced here: 118 us
  starting transfers between devices  58.3 us (49%)
  waiting for transfers between devices  34.2 us (29%)
  Pallas kernels  24.2 us (20%)
    ppermute x10, starting transfers between devices, stream(): return lambda block: lax.ppermute(block, ('sec', 'op'), up + down)  29.6 us
    ppermute x14, starting transfers between devices, hand(): return lax.ppermute(block, ('sec', 'op'), pairs_of)  24.8 us
    ppermute x10, waiting for transfers between devices, stream(): return lambda block: lax.ppermute(block, ('sec', 'op'), up + down)  17.8 us
    pallas_call x1, Pallas kernels, grow(): pl.pallas_call(functools.partial(grow_kernel, dims, ops_dev, parts, len(g...  12.7 us
    ppermute x14, waiting for transfers between devices, hand(): return lax.ppermute(block, ('sec', 'op'), pairs_of)  9.67 us
    ppermute x4, waiting for transfers between devices, across(): return lax.ppermute(block, ('sec', 'blk', 'op'), pairs_of)  6.73 us
    pallas_call x1, Pallas kernels, finish(): pl.pallas_call(functools.partial(finish_kernel, dims, ops_dev), out_shape...  4.79 us
    ppermute x4, starting transfers between devices, across(): return lax.ppermute(block, ('sec', 'blk', 'op'), pairs_of)  3.98 us
  transfers between devices with their start and end apart: 28, of which 9 were waited for; matrix products, arithmetic and copies ran while one was open for 0% of the time, Pallas kernels for 14%

profile of v2, /device:TPU:0, one launch (start us, length us, event | category | flops | bytes accessed | tf_op | source)
XLA Modules:
  0.0 117.8 jit_solution(7654005375997765529)
XLA Ops:
  0.0 2.7 %head.1 = (bf16[6,128,512]{2,1,0:T(8,128)(2,1)}, bf16[6,128,512]{2,1,0:T(8,128)(2,1)}) custom-call(bf16[6,256,512]{2,1,0:T(8,128)(2,1)} %env.5, bf16[2,6,128,512]{3,2,1,0:T(8,128)(2,1)} %bitcast.19), custom_call_target="tpu_custom_call" | custom-call | bytes 3145728 | tf_op jit(solution)/shard_map/head/pallas_call | solution.py:301
  2.7 5.8 %collective-permute-start = (bf16[6,128,512]{2,1,0:T(8,128)(2,1)}, bf16[6,128,512]{2,1,0:T(8,128)(2,1)}, u32[]{:S(2)}, u32[]{:S(2)}) collective-permute-start(bf16[6,128,512]{2,1,0:T(8,128)(2,1)} %get-tuple-element.28), channel_id=1, source_target_pairs={{0,4},{4,8},{8,12},{13,9},{9,5},{5,1},{2,6},{6,10},{10,14},{15,11}... | collective-permute-start | bytes 2359304 | tf_op jit(solution)/shard_map/ppermute | solution.py:615
  8.5 3.5 %collective-permute-start.5 = (bf16[6,128,512]{2,1,0:T(8,128)(2,1)}, bf16[6,128,512]{2,1,0:T(8,128)(2,1)}, u32[]{:S(2)}, u32[]{:S(2)}) collective-permute-start(bf16[6,128,512]{2,1,0:T(8,128)(2,1)} %get-tuple-element.31), channel_id=1, source_target_pairs={{0,4},{4,8},{8,12},{13,9},{9,5},{5,1},{2,6},{6,10},{10,14},{15,11}... | collective-permute-start | bytes 2359304 | tf_op jit(solution)/shard_map/ppermute | solution.py:615
  12.0 5.4 %collective-permute-done.first = bf16[6,128,512]{2,1,0:T(8,128)(2,1)} collective-permute-done((bf16[6,128,512]{2,1,0:T(8,128)(2,1)}, bf16[6,128,512]{2,1,0:T(8,128)(2,1)}, u32[]{:S(2)}, u32[]{:S(2)}) %collective-permute-start) | collective-permute-done | bytes 786464 | tf_op jit(solution)/shard_map/ppermute | solution.py:615
  17.5 1.3 %collective-permute-start.2 = (bf16[6,128,512]{2,1,0:T(8,128)(2,1)}, bf16[6,128,512]{2,1,0:T(8,128)(2,1)}, u32[]{:S(2)}, u32[]{:S(2)}) collective-permute-start(bf16[6,128,512]{2,1,0:T(8,128)(2,1)} %collective-permute-done.first), channel_id=1, source_target_pairs={{4,5},{9,8},{12,13},{1,0},{6,7},{11,10},{14,15},{3,2},{20,21},{25,... | collective-permute-start | bytes 2359304 | tf_op jit(solution)/shard_map/ppermute | solution.py:619
  18.7 1.5 %collective-permute-start.1 = (bf16[6,128,512]{2,1,0:T(8,128)(2,1)}, bf16[6,128,512]{2,1,0:T(8,128)(2,1)}, u32[]{:S(2)}, u32[]{:S(2)}) collective-permute-start(bf16[6,128,512]{2,1,0:T(8,128)(2,1)} %collective-permute-done.first), channel_id=1, source_target_pairs={{4,8},{9,5},{6,10},{11,7},{20,24},{25,21},{22,26},{27,23}} | collective-permute-start | bytes 2359304 | tf_op jit(solution)/shard_map/ppermute | solution.py:615
  20.3 5.6 %collective-permute-done.5.first = bf16[6,128,512]{2,1,0:T(8,128)(2,1)} collective-permute-done((bf16[6,128,512]{2,1,0:T(8,128)(2,1)}, bf16[6,128,512]{2,1,0:T(8,128)(2,1)}, u32[]{:S(2)}, u32[]{:S(2)}) %collective-permute-start.5) | collective-permute-done | bytes 786464 | tf_op jit(solution)/shard_map/ppermute | solution.py:615
  25.9 1.3 %collective-permute-start.8 = (bf16[6,128,512]{2,1,0:T(8,128)(2,1)}, bf16[6,128,512]{2,1,0:T(8,128)(2,1)}, u32[]{:S(2)}, u32[]{:S(2)}) collective-permute-start(bf16[6,128,512]{2,1,0:T(8,128)(2,1)} %collective-permute-done.5.first), channel_id=1, source_target_pairs={{4,5},{9,8},{12,13},{1,0},{6,7},{11,10},{14,15},{3,2},{20,21},{25,... | collective-permute-start | bytes 2359304 | tf_op jit(solution)/shard_map/ppermute | solution.py:619
  27.2 1.6 %collective-permute-start.6 = (bf16[6,128,512]{2,1,0:T(8,128)(2,1)}, bf16[6,128,512]{2,1,0:T(8,128)(2,1)}, u32[]{:S(2)}, u32[]{:S(2)}) collective-permute-start(bf16[6,128,512]{2,1,0:T(8,128)(2,1)} %collective-permute-done.5.first), channel_id=1, source_target_pairs={{4,8},{9,5},{6,10},{11,7},{20,24},{25,21},{22,26},{27,23}} | collective-permute-start | bytes 2359304 | tf_op jit(solution)/shard_map/ppermute | solution.py:615
  28.7 2.5 %tables.1.table = s32[232]{0:T(256)} custom-call(s32[8,24]{1,0:T(8,128)} %shift.1, s32[24]{0:T(128)} %slot.1, s32[3,24]{1,0:T(4,128)} %bitcast.36), custom_call_target="tpu_custom_call" | custom-call | flops 10000 | bytes 4000 | tf_op jit(solution)/shard_map/tables/pallas_call | solution.py:355
  31.3 0.0 copy-start.3
  31.3 0.7 copy-done.3
  32.0 0.8 blend.2
  32.7 0.0 copy-start.2
  32.7 0.0 copy-start.4
  32.7 7.4 %collective-permute-start.3 = (bf16[6,128,512]{2,1,0:T(8,128)(2,1)S(1)}, bf16[6,128,512]{2,1,0:T(8,128)(2,1)S(1)}, u32[]{:S(2)}, u32[]{:S(2)}) collective-permute-start(bf16[6,128,512]{2,1,0:T(8,128)(2,1)S(1)} %get-tuple-element.29), channel_id=1, source_target_pairs={{0,4},{4,8},{8,12},{13,9},{9,5},{5,1},{2,6},{6,10},{10,14},{15,11}... | collective-permute-start | bytes 2359304 | tf_op jit(solution)/shard_map/ppermute | solution.py:615
  40.1 0.0 collective-permute-done.8.other
  40.2 0.8 blend.3
  40.9 6.9 %collective-permute-start.11 = (bf16[6,128,512]{2,1,0:T(8,128)(2,1)S(1)}, bf16[6,128,512]{2,1,0:T(8,128)(2,1)S(1)}, u32[]{:S(2)}, u32[]{:S(2)}) collective-permute-start(bf16[6,128,512]{2,1,0:T(8,128)(2,1)S(1)} %get-tuple-element.35), channel_id=1, source_target_pairs={{0,4},{4,8},{8,12},{13,9},{9,5},{5,1},{2,6},{6,10},{10,14},{15,11}... | collective-permute-start | bytes 2359304 | tf_op jit(solution)/shard_map/ppermute | solution.py:615
  47.8 0.7 collective-permute-start.7
  48.5 1.0 collective-permute-done.3.refs_17_
  49.6 1.3 %collective-permute-start.10 = (bf16[6,128,512]{2,1,0:T(8,128)(2,1)S(1)}, bf16[6,128,512]{2,1,0:T(8,128)(2,1)S(1)}, u32[]{:S(2)}, u32[]{:S(2)}) collective-permute-start(bf16[6,128,512]{2,1,0:T(8,128)(2,1)S(1)} %collective-permute-done.3.refs_17_), channel_id=1, source_target_pairs={{12,15},{14,13},{1,2},{3,0},{28,31},{30,29},{17,18},{19,16}} | collective-permute-start | bytes 2359304 | tf_op jit(solution)/shard_map/ppermute | solution.py:623
  50.9 0.7 collective-permute-start.4
  51.6 0.7 collective-permute-start.9
  52.3 5.7 %collective-permute-done.11.refs_25_ = bf16[6,128,512]{2,1,0:T(8,128)(2,1)S(1)} collective-permute-done((bf16[6,128,512]{2,1,0:T(8,128)(2,1)S(1)}, bf16[6,128,512]{2,1,0:T(8,128)(2,1)S(1)}, u32[]{:S(2)}, u32[]{:S(2)}) %collective-permute-start.11) | collective-permute-done | bytes 786464 | tf_op jit(solution)/shard_map/ppermute | solution.py:615
  58.0 0.7 collective-permute-start.12
  58.7 0.7 collective-permute-start.13
  59.4 3.9 %collective-permute-done.10.refs_18_ = bf16[6,128,512]{2,1,0:T(8,128)(2,1)S(1)} collective-permute-done((bf16[6,128,512]{2,1,0:T(8,128)(2,1)S(1)}, bf16[6,128,512]{2,1,0:T(8,128)(2,1)S(1)}, u32[]{:S(2)}, u32[]{:S(2)}) %collective-permute-start.10) | collective-permute-done | bytes 786464 | tf_op jit(solution)/shard_map/ppermute | solution.py:623
  63.3 1.3 %collective-permute-start.22 = (bf16[6,128,512]{2,1,0:T(8,128)(2,1)S(1)}, bf16[6,128,512]{2,1,0:T(8,128)(2,1)S(1)}, u32[]{:S(2)}, u32[]{:S(2)}) collective-permute-start(bf16[6,128,512]{2,1,0:T(8,128)(2,1)S(1)} %collective-permute-done.11.refs_25_), channel_id=1, source_target_pairs={{12,15},{14,13},{1,2},{3,0},{28,31},{30,29},{17,18},{19,16}} | collective-permute-start | bytes 2359304 | tf_op jit(solution)/shard_map/ppermute | solution.py:623
  64.6 0.7 collective-permute-start.17
  65.4 1.3 %collective-permute-start.14 = (bf16[6,128,512]{2,1,0:T(8,128)(2,1)S(1)}, bf16[6,128,512]{2,1,0:T(8,128)(2,1)S(1)}, u32[]{:S(2)}, u32[]{:S(2)}) collective-permute-start(bf16[6,128,512]{2,1,0:T(8,128)(2,1)S(1)} %collective-permute-done.3.refs_17_), channel_id=1, source_target_pairs={{4,5},{9,8},{8,9},{5,4},{12,13},{1,0},{6,7},{11,10},{10,11},{7,6},... | collective-permute-start | bytes 2359304 | tf_op jit(solution)/shard_map/ppermute | solution.py:619
  66.7 0.7 collective-permute-start.21
  67.4 6.4 %collective-permute-start.20 = (bf16[6,128,512]{2,1,0:T(8,128)(2,1)S(1)}, bf16[6,128,512]{2,1,0:T(8,128)(2,1)S(1)}, u32[]{:S(2)}, u32[]{:S(2)}) collective-permute-start(bf16[6,128,512]{2,1,0:T(8,128)(2,1)S(1)} %collective-permute-done.10.refs_18_), channel_id=1, source_target_pairs={{0,1},{13,12},{2,3},{15,14},{16,17},{29,28},{18,19},{31,30}} | collective-permute-start | bytes 2359304 | tf_op jit(solution)/shard_map/ppermute | solution.py:619
  73.8 2.8 %collective-permute-done.22.refs_26_ = bf16[6,128,512]{2,1,0:T(8,128)(2,1)S(1)} collective-permute-done((bf16[6,128,512]{2,1,0:T(8,128)(2,1)S(1)}, bf16[6,128,512]{2,1,0:T(8,128)(2,1)S(1)}, u32[]{:S(2)}, u32[]{:S(2)}) %collective-permute-start.22) | collective-permute-done | bytes 786464 | tf_op jit(solution)/shard_map/ppermute | solution.py:623
  76.6 1.3 %collective-permute-start.16 = (bf16[6,128,512]{2,1,0:T(8,128)(2,1)S(1)}, bf16[6,128,512]{2,1,0:T(8,128)(2,1)S(1)}, u32[]{:S(2)}, u32[]{:S(2)}) collective-permute-start(bf16[6,128,512]{2,1,0:T(8,128)(2,1)S(1)} %collective-permute-done.11.refs_25_), channel_id=1, source_target_pairs={{4,5},{9,8},{8,9},{5,4},{12,13},{1,0},{6,7},{11,10},{10,11},{7,6},... | collective-permute-start | bytes 2359304 | tf_op jit(solution)/shard_map/ppermute | solution.py:619
  77.9 0.7 collective-permute-start.23
  78.7 1.3 %collective-permute-start.18 = (bf16[6,128,512]{2,1,0:T(8,128)(2,1)S(1)}, bf16[6,128,512]{2,1,0:T(8,128)(2,1)S(1)}, u32[]{:S(2)}, u32[]{:S(2)}) collective-permute-start(bf16[6,128,512]{2,1,0:T(8,128)(2,1)S(1)} %collective-permute-done.4), channel_id=1, source_target_pairs={{8,9},{5,4},{12,13},{1,0},{10,11},{7,6},{14,15},{3,2},{24,25},{21,... | collective-permute-start | bytes 2359304 | tf_op jit(solution)/shard_map/ppermute | solution.py:619
  80.0 1.3 %collective-permute-start.19 = (bf16[6,128,512]{2,1,0:T(8,128)(2,1)S(1)}, bf16[6,128,512]{2,1,0:T(8,128)(2,1)S(1)}, u32[]{:S(2)}, u32[]{:S(2)}) collective-permute-start(bf16[6,128,512]{2,1,0:T(8,128)(2,1)S(1)} %collective-permute-done.17), channel_id=1, source_target_pairs={{8,9},{5,4},{12,13},{1,0},{10,11},{7,6},{14,15},{3,2},{24,25},{21,... | collective-permute-start | bytes 2359304 | tf_op jit(solution)/shard_map/ppermute | solution.py:619
  81.3 5.3 %collective-permute-start.24 = (bf16[6,128,512]{2,1,0:T(8,128)(2,1)S(1)}, bf16[6,128,512]{2,1,0:T(8,128)(2,1)S(1)}, u32[]{:S(2)}, u32[]{:S(2)}) collective-permute-start(bf16[6,128,512]{2,1,0:T(8,128)(2,1)S(1)} %collective-permute-done.22.refs_26_), channel_id=1, source_target_pairs={{0,1},{13,12},{2,3},{15,14},{16,17},{29,28},{18,19},{31,30}} | collective-permute-start | bytes 2359304 | tf_op jit(solution)/shard_map/ppermute | solution.py:619
  86.6 0.7 collective-permute-start.15
  87.3 0.7 collective-permute-start.26
  88.0 0.4 collective-permute-done.24.refs_29_
  88.4 12.7 %grow.1 = (bf16[4,6,256,512]{3,2,1,0:T(8,128)(2,1)}, bf16[6,512,512]{2,1,0:T(8,128)(2,1)S(1)}) custom-call(s32[232]{0:T(256)S(1)} %copy-done.4, bf16[6,256,512]{2,1,0:T(8,128)(2,1)S(1)} %copy-done, bf16[3,256,512]{2,1,0:T(8,128)(2,1)} %bitcast.4.refs_1_, bf16[3,256,512]{2,1,0:T(8,128)(2,1)} %bitcast.5.refs_2_, bf16[3,256,512]{2,1,0:T(8,128)(2,1)S(1)} %bitcast.22, ...), custom_call_target="tpu_custom_call" | custom-call | flops 1048576 | bytes 4096 | tf_op jit(solution)/shard_map/grow/pallas_call | solution.py:519
  101.2 1.3 %collective-permute-start.25 = (bf16[6,128,512]{2,1,0:T(8,128)(2,1)S(1)}, bf16[6,128,512]{2,1,0:T(8,128)(2,1)S(1)}, u32[]{:S(2)}, u32[]{:S(2)}) collective-permute-start(bf16[6,128,512]{2,1,0:T(8,128)(2,1)S(1)} %collective-permute-done.15), channel_id=1, source_target_pairs={{12,13},{1,0},{14,15},{3,2},{28,29},{17,16},{30,31},{19,18}} | collective-permute-start | bytes 2359304 | tf_op jit(solution)/shard_map/ppermute | solution.py:619
  102.5 1.3 %collective-permute-start.27 = (bf16[6,128,512]{2,1,0:T(8,128)(2,1)S(1)}, bf16[6,128,512]{2,1,0:T(8,128)(2,1)S(1)}, u32[]{:S(2)}, u32[]{:S(2)}) collective-permute-start(bf16[6,128,512]{2,1,0:T(8,128)(2,1)S(1)} %collective-permute-done.26), channel_id=1, source_target_pairs={{12,13},{1,0},{14,15},{3,2},{28,29},{17,16},{30,31},{19,18}} | collective-permute-start | bytes 2359304 | tf_op jit(solution)/shard_map/ppermute | solution.py:619
  103.8 1.6 %collective-permute-done.25 = bf16[6,128,512]{2,1,0:T(8,128)(2,1)S(1)} collective-permute-done((bf16[6,128,512]{2,1,0:T(8,128)(2,1)S(1)}, bf16[6,128,512]{2,1,0:T(8,128)(2,1)S(1)}, u32[]{:S(2)}, u32[]{:S(2)}) %collective-permute-start.25) | collective-permute-done | bytes 786464 | tf_op jit(solution)/shard_map/ppermute | solution.py:619
  105.3 7.7 %collective-permute-done.27 = bf16[6,128,512]{2,1,0:T(8,128)(2,1)S(1)} collective-permute-done((bf16[6,128,512]{2,1,0:T(8,128)(2,1)S(1)}, bf16[6,128,512]{2,1,0:T(8,128)(2,1)S(1)}, u32[]{:S(2)}, u32[]{:S(2)}) %collective-permute-start.27) | collective-permute-done | bytes 786464 | tf_op jit(solution)/shard_map/ppermute | solution.py:619
  113.0 4.8 %finish.1 = bf16[4,6,256,512]{3,2,1,0:T(8,128)(2,1)} custom-call(s32[232]{0:T(256)S(1)} %copy-done.4, bf16[3,256,512]{2,1,0:T(8,128)(2,1)S(1)} %bitcast.32, bf16[3,256,512]{2,1,0:T(8,128)(2,1)S(1)} %bitcast.34, bf16[3,256,512]{2,1,0:T(8,128)(2,1)S(1)} %bitcast.33, bf16[3,256,512]{2,1,0:T(8,128)(2,1)S(1)} %bitcast.35, ...), custom_call_target="tpu_custom_call", output_to_operand_aliasing={{}: (7, {})} | custom-call | flops 40000000000 | bytes 1048576 | tf_op jit(solution)/shard_map/finish/pallas_call | solution.py:588
  (26 shorter events, 0.1 us)
Async XLA Ops:
  0.0 31.2 %copy-start.1 = (bf16[6,256,512]{2,1,0:T(8,128)(2,1)S(1)}, bf16[6,256,512]{2,1,0:T(8,128)(2,1)}, u32[]{:S(2)}) copy-start(bf16[6,256,512]{2,1,0:T(8,128)(2,1)} %env.5) | copy-start | bytes 4718596
  0.0 31.3 %copy-start = (bf16[6,256,512]{2,1,0:T(8,128)(2,1)S(1)}, bf16[6,256,512]{2,1,0:T(8,128)(2,1)}, u32[]{:S(2)}) copy-start(bf16[6,256,512]{2,1,0:T(8,128)(2,1)} %refs_0_.1) | copy-start | bytes 4718596
  0.0 31.3 %copy-start.5 = (f32[24,3]{0,1:T(4,128)S(1)}, f32[24,3]{0,1:T(4,128)}, u32[]{:S(2)}) copy-start(f32[24,3]{0,1:T(4,128)} %param.13) | copy-start | bytes 868
  2.7 14.8 %collective-permute-start = (bf16[6,128,512]{2,1,0:T(8,128)(2,1)}, bf16[6,128,512]{2,1,0:T(8,128)(2,1)}, u32[]{:S(2)}, u32[]{:S(2)}) collective-permute-start(bf16[6,128,512]{2,1,0:T(8,128)(2,1)} %get-tuple-element.28), channel_id=1, source_target_pairs={{0,4},{4,8},{8,12},{13,9},{9,5},{5,1},{2,6},{6,10},{10,14},{15,11}... | collective-permute-start | bytes 2359304 | tf_op jit(solution)/shard_map/ppermute | solution.py:615
  8.5 17.3 %collective-permute-start.5 = (bf16[6,128,512]{2,1,0:T(8,128)(2,1)}, bf16[6,128,512]{2,1,0:T(8,128)(2,1)}, u32[]{:S(2)}, u32[]{:S(2)}) collective-permute-start(bf16[6,128,512]{2,1,0:T(8,128)(2,1)} %get-tuple-element.31), channel_id=1, source_target_pairs={{0,4},{4,8},{8,12},{13,9},{9,5},{5,1},{2,6},{6,10},{10,14},{15,11}... | collective-permute-start | bytes 2359304 | tf_op jit(solution)/shard_map/ppermute | solution.py:615
  17.5 13.8 %collective-permute-start.2 = (bf16[6,128,512]{2,1,0:T(8,128)(2,1)}, bf16[6,128,512]{2,1,0:T(8,128)(2,1)}, u32[]{:S(2)}, u32[]{:S(2)}) collective-permute-start(bf16[6,128,512]{2,1,0:T(8,128)(2,1)} %collective-permute-done.first), channel_id=1, source_target_pairs={{4,5},{9,8},{12,13},{1,0},{6,7},{11,10},{14,15},{3,2},{20,21},{25,... | collective-permute-start | bytes 2359304 | tf_op jit(solution)/shard_map/ppermute | solution.py:619
  18.7 12.5 %collective-permute-start.1 = (bf16[6,128,512]{2,1,0:T(8,128)(2,1)}, bf16[6,128,512]{2,1,0:T(8,128)(2,1)}, u32[]{:S(2)}, u32[]{:S(2)}) collective-permute-start(bf16[6,128,512]{2,1,0:T(8,128)(2,1)} %collective-permute-done.first), channel_id=1, source_target_pairs={{4,8},{9,5},{6,10},{11,7},{20,24},{25,21},{22,26},{27,23}} | collective-permute-start | bytes 2359304 | tf_op jit(solution)/shard_map/ppermute | solution.py:615
  25.9 14.3 %collective-permute-start.8 = (bf16[6,128,512]{2,1,0:T(8,128)(2,1)}, bf16[6,128,512]{2,1,0:T(8,128)(2,1)}, u32[]{:S(2)}, u32[]{:S(2)}) collective-permute-start(bf16[6,128,512]{2,1,0:T(8,128)(2,1)} %collective-permute-done.5.first), channel_id=1, source_target_pairs={{4,5},{9,8},{12,13},{1,0},{6,7},{11,10},{14,15},{3,2},{20,21},{25,... | collective-permute-start | bytes 2359304 | tf_op jit(solution)/shard_map/ppermute | solution.py:619
  27.2 13.0 %collective-permute-start.6 = (bf16[6,128,512]{2,1,0:T(8,128)(2,1)}, bf16[6,128,512]{2,1,0:T(8,128)(2,1)}, u32[]{:S(2)}, u32[]{:S(2)}) collective-permute-start(bf16[6,128,512]{2,1,0:T(8,128)(2,1)} %collective-permute-done.5.first), channel_id=1, source_target_pairs={{4,8},{9,5},{6,10},{11,7},{20,24},{25,21},{22,26},{27,23}} | collective-permute-start | bytes 2359304 | tf_op jit(solution)/shard_map/ppermute | solution.py:615
  31.3 0.7 copy-start.3
  32.7 55.7 %copy-start.2 = (bf16[4,512,512]{2,1,0:T(8,128)(2,1)S(1)}, bf16[4,512,512]{2,1,0:T(8,128)(2,1)}, u32[]{:S(2)}) copy-start(bf16[4,512,512]{2,1,0:T(8,128)(2,1)} %op_ref.1) | copy-start | bytes 6291460
  32.7 55.7 %copy-start.4 = (s32[232]{0:T(256)S(1)}, s32[232]{0:T(256)}, u32[]{:S(2)}) copy-start(s32[232]{0:T(256)} %tables.1.table) | copy-start | bytes 2788
  32.7 16.8 %collective-permute-start.3 = (bf16[6,128,512]{2,1,0:T(8,128)(2,1)S(1)}, bf16[6,128,512]{2,1,0:T(8,128)(2,1)S(1)}, u32[]{:S(2)}, u32[]{:S(2)}) collective-permute-start(bf16[6,128,512]{2,1,0:T(8,128)(2,1)S(1)} %get-tuple-element.29), channel_id=1, source_target_pairs={{0,4},{4,8},{8,12},{13,9},{9,5},{5,1},{2,6},{6,10},{10,14},{15,11}... | collective-permute-start | bytes 2359304 | tf_op jit(solution)/shard_map/ppermute | solution.py:615
  40.9 17.1 %collective-permute-start.11 = (bf16[6,128,512]{2,1,0:T(8,128)(2,1)S(1)}, bf16[6,128,512]{2,1,0:T(8,128)(2,1)S(1)}, u32[]{:S(2)}, u32[]{:S(2)}) collective-permute-start(bf16[6,128,512]{2,1,0:T(8,128)(2,1)S(1)} %get-tuple-element.35), channel_id=1, source_target_pairs={{0,4},{4,8},{8,12},{13,9},{9,5},{5,1},{2,6},{6,10},{10,14},{15,11}... | collective-permute-start | bytes 2359304 | tf_op jit(solution)/shard_map/ppermute | solution.py:615
  47.8 10.9 %collective-permute-start.7 = (bf16[6,128,512]{2,1,0:T(8,128)(2,1)S(1)}, bf16[6,128,512]{2,1,0:T(8,128)(2,1)S(1)}, u32[]{:S(2)}, u32[]{:S(2)}) collective-permute-start(bf16[6,128,512]{2,1,0:T(8,128)(2,1)S(1)} %get-tuple-element.36.refs_16_), channel_id=1, source_target_pairs={{8,11},{10,9},{5,6},{7,4},{24,27},{26,25},{21,22},{23,20}} | collective-permute-start | bytes 2359304 | tf_op jit(solution)/shard_map/ppermute | solution.py:623
  49.6 13.8 %collective-permute-start.10 = (bf16[6,128,512]{2,1,0:T(8,128)(2,1)S(1)}, bf16[6,128,512]{2,1,0:T(8,128)(2,1)S(1)}, u32[]{:S(2)}, u32[]{:S(2)}) collective-permute-start(bf16[6,128,512]{2,1,0:T(8,128)(2,1)S(1)} %collective-permute-done.3.refs_17_), channel_id=1, source_target_pairs={{12,15},{14,13},{1,2},{3,0},{28,31},{30,29},{17,18},{19,16}} | collective-permute-start | bytes 2359304 | tf_op jit(solution)/shard_map/ppermute | solution.py:623
  50.9 13.8 %collective-permute-start.4 = (bf16[6,128,512]{2,1,0:T(8,128)(2,1)S(1)}, bf16[6,128,512]{2,1,0:T(8,128)(2,1)S(1)}, u32[]{:S(2)}, u32[]{:S(2)}) collective-permute-start(bf16[6,128,512]{2,1,0:T(8,128)(2,1)S(1)} %collective-permute-done.3.refs_17_), channel_id=1, source_target_pairs={{4,8},{8,12},{9,5},{5,1},{6,10},{10,14},{11,7},{7,3},{20,24},{24,2... | collective-permute-start | bytes 2359304 | tf_op jit(solution)/shard_map/ppermute | solution.py:615
  51.6 13.8 %collective-permute-start.9 = (bf16[6,128,512]{2,1,0:T(8,128)(2,1)S(1)}, bf16[6,128,512]{2,1,0:T(8,128)(2,1)S(1)}, u32[]{:S(2)}, u32[]{:S(2)}) collective-permute-start(bf16[6,128,512]{2,1,0:T(8,128)(2,1)S(1)} %get-tuple-element.43.refs_24_), channel_id=1, source_target_pairs={{8,11},{10,9},{5,6},{7,4},{24,27},{26,25},{21,22},{23,20}} | collective-permute-start | bytes 2359304 | tf_op jit(solution)/shard_map/ppermute | solution.py:623
  58.0 8.7 %collective-permute-start.12 = (bf16[6,128,512]{2,1,0:T(8,128)(2,1)S(1)}, bf16[6,128,512]{2,1,0:T(8,128)(2,1)S(1)}, u32[]{:S(2)}, u32[]{:S(2)}) collective-permute-start(bf16[6,128,512]{2,1,0:T(8,128)(2,1)S(1)} %get-tuple-element.36.refs_16_), channel_id=1, source_target_pairs={{8,9},{5,4},{10,11},{7,6},{24,25},{21,20},{26,27},{23,22}} | collective-permute-start | bytes 2359304 | tf_op jit(solution)/shard_map/ppermute | solution.py:619
  58.7 8.7 %collective-permute-start.13 = (bf16[6,128,512]{2,1,0:T(8,128)(2,1)S(1)}, bf16[6,128,512]{2,1,0:T(8,128)(2,1)S(1)}, u32[]{:S(2)}, u32[]{:S(2)}) collective-permute-start(bf16[6,128,512]{2,1,0:T(8,128)(2,1)S(1)} %collective-permute-done.7.refs_19_), channel_id=1, source_target_pairs={{4,5},{9,8},{6,7},{11,10},{20,21},{25,24},{22,23},{27,26}} | collective-permute-start | bytes 2359304 | tf_op jit(solution)/shard_map/ppermute | solution.py:619
  63.3 13.3 %collective-permute-start.22 = (bf16[6,128,512]{2,1,0:T(8,128)(2,1)S(1)}, bf16[6,128,512]{2,1,0:T(8,128)(2,1)S(1)}, u32[]{:S(2)}, u32[]{:S(2)}) collective-permute-start(bf16[6,128,512]{2,1,0:T(8,128)(2,1)S(1)} %collective-permute-done.11.refs_25_), channel_id=1, source_target_pairs={{12,15},{14,13},{1,2},{3,0},{28,31},{30,29},{17,18},{19,16}} | collective-permute-start | bytes 2359304 | tf_op jit(solution)/shard_map/ppermute | solution.py:623
  64.6 13.3 %collective-permute-start.17 = (bf16[6,128,512]{2,1,0:T(8,128)(2,1)S(1)}, bf16[6,128,512]{2,1,0:T(8,128)(2,1)S(1)}, u32[]{:S(2)}, u32[]{:S(2)}) collective-permute-start(bf16[6,128,512]{2,1,0:T(8,128)(2,1)S(1)} %collective-permute-done.11.refs_25_), channel_id=1, source_target_pairs={{4,8},{8,12},{9,5},{5,1},{6,10},{10,14},{11,7},{7,3},{20,24},{24,2... | collective-permute-start | bytes 2359304 | tf_op jit(solution)/shard_map/ppermute | solution.py:615
  65.4 13.3 %collective-permute-start.14 = (bf16[6,128,512]{2,1,0:T(8,128)(2,1)S(1)}, bf16[6,128,512]{2,1,0:T(8,128)(2,1)S(1)}, u32[]{:S(2)}, u32[]{:S(2)}) collective-permute-start(bf16[6,128,512]{2,1,0:T(8,128)(2,1)S(1)} %collective-permute-done.3.refs_17_), channel_id=1, source_target_pairs={{4,5},{9,8},{8,9},{5,4},{12,13},{1,0},{6,7},{11,10},{10,11},{7,6},... | collective-permute-start | bytes 2359304 | tf_op jit(solution)/shard_map/ppermute | solution.py:619
  66.7 13.3 %collective-permute-start.21 = (bf16[6,128,512]{2,1,0:T(8,128)(2,1)S(1)}, bf16[6,128,512]{2,1,0:T(8,128)(2,1)S(1)}, u32[]{:S(2)}, u32[]{:S(2)}) collective-permute-start(bf16[6,128,512]{2,1,0:T(8,128)(2,1)S(1)} %get-tuple-element.43.refs_24_), channel_id=1, source_target_pairs={{8,9},{5,4},{10,11},{7,6},{24,25},{21,20},{26,27},{23,22}} | collective-permute-start | bytes 2359304 | tf_op jit(solution)/shard_map/ppermute | solution.py:619
  67.4 13.9 %collective-permute-start.20 = (bf16[6,128,512]{2,1,0:T(8,128)(2,1)S(1)}, bf16[6,128,512]{2,1,0:T(8,128)(2,1)S(1)}, u32[]{:S(2)}, u32[]{:S(2)}) collective-permute-start(bf16[6,128,512]{2,1,0:T(8,128)(2,1)S(1)} %collective-permute-done.10.refs_18_), channel_id=1, source_target_pairs={{0,1},{13,12},{2,3},{15,14},{16,17},{29,28},{18,19},{31,30}} | collective-permute-start | bytes 2359304 | tf_op jit(solution)/shard_map/ppermute | solution.py:619
  76.6 9.9 %collective-permute-start.16 = (bf16[6,128,512]{2,1,0:T(8,128)(2,1)S(1)}, bf16[6,128,512]{2,1,0:T(8,128)(2,1)S(1)}, u32[]{:S(2)}, u32[]{:S(2)}) collective-permute-start(bf16[6,128,512]{2,1,0:T(8,128)(2,1)S(1)} %collective-permute-done.11.refs_25_), channel_id=1, source_target_pairs={{4,5},{9,8},{8,9},{5,4},{12,13},{1,0},{6,7},{11,10},{10,11},{7,6},... | collective-permute-start | bytes 2359304 | tf_op jit(solution)/shard_map/ppermute | solution.py:619
  77.9 9.4 %collective-permute-start.23 = (bf16[6,128,512]{2,1,0:T(8,128)(2,1)S(1)}, bf16[6,128,512]{2,1,0:T(8,128)(2,1)S(1)}, u32[]{:S(2)}, u32[]{:S(2)}) collective-permute-start(bf16[6,128,512]{2,1,0:T(8,128)(2,1)S(1)} %collective-permute-done.9.refs_27_), channel_id=1, source_target_pairs={{4,5},{9,8},{6,7},{11,10},{20,21},{25,24},{22,23},{27,26}} | collective-permute-start | bytes 2359304 | tf_op jit(solution)/shard_map/ppermute | solution.py:619
  78.7 9.4 %collective-permute-start.18 = (bf16[6,128,512]{2,1,0:T(8,128)(2,1)S(1)}, bf16[6,128,512]{2,1,0:T(8,128)(2,1)S(1)}, u32[]{:S(2)}, u32[]{:S(2)}) collective-permute-start(bf16[6,128,512]{2,1,0:T(8,128)(2,1)S(1)} %collective-permute-done.4), channel_id=1, source_target_pairs={{8,9},{5,4},{12,13},{1,0},{10,11},{7,6},{14,15},{3,2},{24,25},{21,... | collective-permute-start | bytes 2359304 | tf_op jit(solution)/shard_map/ppermute | solution.py:619
  80.0 8.1 %collective-permute-start.19 = (bf16[6,128,512]{2,1,0:T(8,128)(2,1)S(1)}, bf16[6,128,512]{2,1,0:T(8,128)(2,1)S(1)}, u32[]{:S(2)}, u32[]{:S(2)}) collective-permute-start(bf16[6,128,512]{2,1,0:T(8,128)(2,1)S(1)} %collective-permute-done.17), channel_id=1, source_target_pairs={{8,9},{5,4},{12,13},{1,0},{10,11},{7,6},{14,15},{3,2},{24,25},{21,... | collective-permute-start | bytes 2359304 | tf_op jit(solution)/shard_map/ppermute | solution.py:619
  81.3 7.1 %collective-permute-start.24 = (bf16[6,128,512]{2,1,0:T(8,128)(2,1)S(1)}, bf16[6,128,512]{2,1,0:T(8,128)(2,1)S(1)}, u32[]{:S(2)}, u32[]{:S(2)}) collective-permute-start(bf16[6,128,512]{2,1,0:T(8,128)(2,1)S(1)} %collective-permute-done.22.refs_26_), channel_id=1, source_target_pairs={{0,1},{13,12},{2,3},{15,14},{16,17},{29,28},{18,19},{31,30}} | collective-permute-start | bytes 2359304 | tf_op jit(solution)/shard_map/ppermute | solution.py:619
  86.6 14.6 %collective-permute-start.15 = (bf16[6,128,512]{2,1,0:T(8,128)(2,1)S(1)}, bf16[6,128,512]{2,1,0:T(8,128)(2,1)S(1)}, u32[]{:S(2)}, u32[]{:S(2)}) collective-permute-start(bf16[6,128,512]{2,1,0:T(8,128)(2,1)S(1)} %collective-permute-done.4), channel_id=1, source_target_pairs={{8,12},{5,1},{10,14},{7,3},{24,28},{21,17},{26,30},{23,19}} | collective-permute-start | bytes 2359304 | tf_op jit(solution)/shard_map/ppermute | solution.py:615
  87.3 15.2 %collective-permute-start.26 = (bf16[6,128,512]{2,1,0:T(8,128)(2,1)S(1)}, bf16[6,128,512]{2,1,0:T(8,128)(2,1)S(1)}, u32[]{:S(2)}, u32[]{:S(2)}) collective-permute-start(bf16[6,128,512]{2,1,0:T(8,128)(2,1)S(1)} %collective-permute-done.17), channel_id=1, source_target_pairs={{8,12},{5,1},{10,14},{7,3},{24,28},{21,17},{26,30},{23,19}} | collective-permute-start | bytes 2359304 | tf_op jit(solution)/shard_map/ppermute | solution.py:615
  101.2 4.2 %collective-permute-start.25 = (bf16[6,128,512]{2,1,0:T(8,128)(2,1)S(1)}, bf16[6,128,512]{2,1,0:T(8,128)(2,1)S(1)}, u32[]{:S(2)}, u32[]{:S(2)}) collective-permute-start(bf16[6,128,512]{2,1,0:T(8,128)(2,1)S(1)} %collective-permute-done.15), channel_id=1, source_target_pairs={{12,13},{1,0},{14,15},{3,2},{28,29},{17,16},{30,31},{19,18}} | collective-permute-start | bytes 2359304 | tf_op jit(solution)/shard_map/ppermute | solution.py:619
  102.5 10.6 %collective-permute-start.27 = (bf16[6,128,512]{2,1,0:T(8,128)(2,1)S(1)}, bf16[6,128,512]{2,1,0:T(8,128)(2,1)S(1)}, u32[]{:S(2)}, u32[]{:S(2)}) collective-permute-start(bf16[6,128,512]{2,1,0:T(8,128)(2,1)S(1)} %collective-permute-done.26), channel_id=1, source_target_pairs={{12,13},{1,0},{14,15},{3,2},{28,29},{17,16},{30,31},{19,18}} | collective-permute-start | bytes 2359304 | tf_op jit(solution)/shard_map/ppermute | solution.py:619

commit v3 on v2

--- a/solution.py
+++ b/solution.py
@@ -446,7 +446,7 @@
     owner, core, spot = device_place()
     rows, columns = grounds[0].shape[1:]
     width = sec_dev // 2
-    pieces, (out_ref, env, found, ground, result, ground_sem, out_sem, env_sem) = refs[:16], refs[16:]
+    pieces, (out_ref, env, found, ground, result, ground_sem, out_sem, env_sem) = refs[:4], refs[4:]
     count_at = 2 * sec_dev * MIX_WIDTH
     list_at = count_at + 8
     part_of = [half_owner(owner, core, spot, hops, h, sibling) for _, hops, h, sibling, _ in parts]
@@ -460,15 +460,12 @@
     env_copies = []
     half = rows // 2
     own = lax.axis_index("blk") * rows
-    for n, start in enumerate((own, rows - own, own + half, rows - own + half)):
-        target = env.at[:, pl.ds(pl.multiple_of(start, half), half)]
-        for q in range(4):
-
-            @pl.when(spot == q)
-            def _(n=n, q=q, target=target):
-                pltpu.make_async_copy(pieces[4 * n + q], target, env_sem.at[n]).start()
-
-        env_copies.append(pltpu.make_async_copy(target, target, env_sem.at[n]))
+    lead = spot >= 2
+    starts = [jnp.where(lead, own, rows - own), jnp.where(lead, rows - own, own)]
+    for n in range(4):
+        start = pl.multiple_of(starts[n % 2] + n // 2 * half, half)
+        env_copies.append(pltpu.make_async_copy(pieces[n], env.at[:, pl.ds(start, half)], env_sem.at[n]))
+        env_copies[-1].start()
 
     total = jnp.int32(0)
     for m in range(len(parts)):
@@ -603,6 +600,7 @@
 
 
 def line_of_four(ground_state, op_matrices, shift_map, new_slot, env_ground, env_src, env_coef):
+    _, _, spot = device_place()
     sec_dev, rows, columns = ground_state.shape
     ops, sectors = shift_map.shape
     ops_dev = op_matrices.shape[0]
@@ -618,8 +616,9 @@
         pairs_of = [(2 * z + core, 2 * z + 1 - core) for spot in spots for z, core in at[spot]]
         return lax.ppermute(block, ("sec", "op"), pairs_of)
 
-    def across(block, spot):
-        pairs_of = [((z * 2 + x) * 2 + core, (z * 2 + 1 - x) * 2 + 1 - core) for z, core in at[spot] for x in range(2)]
+    def across(block):
+        leads = at[2] + at[3]
+        pairs_of = [((z * 2 + x) * 2 + core, (z * 2 + 1 - x) * 2 + 1 - core) for z, core in leads for x in range(2)]
         return lax.ppermute(block, ("sec", "blk", "op"), pairs_of)
 
     def after(block, *others):
@@ -640,21 +639,15 @@
     )
     got4 = [every(sent4[h]) for h in both]
     got6 = [late(got4[h]) for h in both]
-    far1 = [across(after(made[0], got2[1]), 2), across(after(made[1], got4[0]), 2)]
-    far2 = [across(got4[0], 3), across(got4[1], 3)]
-    near1 = [hand(after(made[0], got4[1]), [2]), hand(after(made[1], got4[1]), [2])]
-    back1 = [hand(after(far1[0], got4[1]), [1]), hand(after(far1[1], got4[1]), [1])]
-    swapped4 = [hand(after(got4[0], got4[1]), [1, 2, 3]), hand(after(got4[1], far2[0]), [1, 2, 3])]
-    back2 = [hand(far2[0], [0]), hand(after(far2[1], got6[1]), [0])]
-    swapped6 = [hand(after(got6[h], got6[1]), [2, 3]) for h in both]
-    got8 = [
-        last(after(got6[0], *far1, far2[0], near1[0], back1[0], swapped4[0])),
-        last(after(got6[1], *near1, *back1, back2[0], *swapped4)),
-    ]
+    swapped4 = [hand(got4[h], [1, 2, 3]) for h in both]
+    swapped6 = [hand(got6[h], [2, 3]) for h in both]
     pieces = []
     for h in both:
-        pieces += [swapped4[h], near1[h], made[h], got4[h]]
-        pieces += [far2[h], far1[h], back1[h], back2[h]]
+        mine = jnp.where(spot == 2, made[h], got4[h])
+        received = after(across(mine), got6[h])
+        kept = jnp.where(spot >= 2, mine, received)
+        pieces += [kept, hand(kept, [0, 1, 2, 3])]
+    got8 = [last(got6[0]), last(after(got6[1], *swapped4, swapped6[0], pieces[1]))]
 
     parts = [(0, None, h, False, h * sec_dev // 2) for h in both]
     arrays = [ground_state]

time: 119 us -> 116 us (0.975)
  waiting for transfers between devices: 34.2 us -> 27.7 us
  other arithmetic: 0 us -> 5.55 us
  starting transfers between devices: 58.3 us -> 53.5 us
  Pallas kernels: 24.2 us -> 25.9 us
    select_n x0 -> x4, other arithmetic: none -> 5.55 us  [the longest x2 3.09 us: line_of_four(): mine = jnp.where(spot == 2, made[h], got4[h])]
    ppermute x4 -> x2, waiting for transfers between devices: 6.73 us -> 2.45 us  [across(): return lax.ppermute(block, ('sec', 'blk', 'op'), pairs_of)]
    ppermute x14 -> x10, starting transfers between devices: 24.8 us -> 20.7 us  [hand(): return lax.ppermute(block, ('sec', 'op'), pairs_of)]
    pallas_call x2, Pallas kernels: 1.52 us -> 3.3 us  [blend(): pl.pallas_call(functools.partial(blend_kernel, dims, which), out_shape=[b...]
    ppermute x4 -> x2, starting transfers between devices: 3.98 us -> 2.56 us  [across(): return lax.ppermute(block, ('sec', 'blk', 'op'), pairs_of)]
    ppermute x14 -> x10, waiting for transfers between devices: 9.67 us -> 8.62 us  [hand(): return lax.ppermute(block, ('sec', 'op'), pairs_of)]
  transfers between devices with their start and end apart: 28 -> 22, of which waited for: 9 -> 9; matrix products, arithmetic and copies ran while one was open for 0% -> 5% of each run, Pallas kernels for 14% -> 16%
where the time goes in v3:
time: 116 us; the launch traced here: 115 us
  starting transfers between devices  53.5 us (46%)
  waiting for transfers between devices  27.7 us (24%)
  Pallas kernels  25.9 us (22%)
  other arithmetic  5.55 us (5%)
  local copies, waits for them, and re-layouts  1.52 us (1%)
    ppermute x10, starting transfers between devices, stream(): return lambda block: lax.ppermute(block, ('sec', 'op'), up + down)  30.3 us
    ppermute x10, starting transfers between devices, hand(): return lax.ppermute(block, ('sec', 'op'), pairs_of)  20.7 us
    ppermute x10, waiting for transfers between devices, stream(): return lambda block: lax.ppermute(block, ('sec', 'op'), up + down)  16.6 us
    pallas_call x1, Pallas kernels, grow(): pl.pallas_call(functools.partial(grow_kernel, dims, ops_dev, parts, len(g...  12.7 us
    ppermute x10, waiting for transfers between devices, hand(): return lax.ppermute(block, ('sec', 'op'), pairs_of)  8.62 us
    pallas_call x1, Pallas kernels, finish(): pl.pallas_call(functools.partial(finish_kernel, dims, ops_dev), out_shape...  4.75 us
    pallas_call x2, Pallas kernels, blend(): pl.pallas_call(functools.partial(blend_kernel, dims, which), out_shape=[b...  3.3 us
    select_n x2, other arithmetic, line_of_four(): mine = jnp.where(spot == 2, made[h], got4[h])  3.09 us
  transfers between devices with their start and end apart: 22, of which 9 were waited for; matrix products, arithmetic and copies ran while one was open for 5% of the time, Pallas kernels for 16%

profile of v3, /device:TPU:0, one launch (start us, length us, event | category | flops | bytes accessed | tf_op | source)
XLA Modules:
  0.0 114.5 jit_solution(4265745253432157260)
XLA Ops:
  0.0 2.7 %head.1 = (bf16[6,128,512]{2,1,0:T(8,128)(2,1)}, bf16[6,128,512]{2,1,0:T(8,128)(2,1)}) custom-call(bf16[6,256,512]{2,1,0:T(8,128)(2,1)} %env.5, bf16[2,6,128,512]{3,2,1,0:T(8,128)(2,1)} %bitcast.19), custom_call_target="tpu_custom_call" | custom-call | bytes 3145728 | tf_op jit(solution)/shard_map/head/pallas_call | solution.py:301
  2.7 5.9 %collective-permute-start = (bf16[6,128,512]{2,1,0:T(8,128)(2,1)}, bf16[6,128,512]{2,1,0:T(8,128)(2,1)}, u32[]{:S(2)}, u32[]{:S(2)}) collective-permute-start(bf16[6,128,512]{2,1,0:T(8,128)(2,1)} %get-tuple-element.18), channel_id=1, source_target_pairs={{0,4},{4,8},{8,12},{13,9},{9,5},{5,1},{2,6},{6,10},{10,14},{15,11}... | collective-permute-start | bytes 2359304 | tf_op jit(solution)/shard_map/ppermute | solution.py:613
  8.5 3.5 %collective-permute-start.7 = (bf16[6,128,512]{2,1,0:T(8,128)(2,1)}, bf16[6,128,512]{2,1,0:T(8,128)(2,1)}, u32[]{:S(2)}, u32[]{:S(2)}) collective-permute-start(bf16[6,128,512]{2,1,0:T(8,128)(2,1)} %get-tuple-element.20), channel_id=1, source_target_pairs={{0,4},{4,8},{8,12},{13,9},{9,5},{5,1},{2,6},{6,10},{10,14},{15,11}... | collective-permute-start | bytes 2359304 | tf_op jit(solution)/shard_map/ppermute | solution.py:613
  12.0 5.4 %collective-permute-done.first = bf16[6,128,512]{2,1,0:T(8,128)(2,1)} collective-permute-done((bf16[6,128,512]{2,1,0:T(8,128)(2,1)}, bf16[6,128,512]{2,1,0:T(8,128)(2,1)}, u32[]{:S(2)}, u32[]{:S(2)}) %collective-permute-start) | collective-permute-done | bytes 786464 | tf_op jit(solution)/shard_map/ppermute | solution.py:613
  17.4 1.3 %collective-permute-start.2 = (bf16[6,128,512]{2,1,0:T(8,128)(2,1)}, bf16[6,128,512]{2,1,0:T(8,128)(2,1)}, u32[]{:S(2)}, u32[]{:S(2)}) collective-permute-start(bf16[6,128,512]{2,1,0:T(8,128)(2,1)} %collective-permute-done.first), channel_id=1, source_target_pairs={{4,5},{9,8},{12,13},{1,0},{6,7},{11,10},{14,15},{3,2},{20,21},{25,... | collective-permute-start | bytes 2359304 | tf_op jit(solution)/shard_map/ppermute | solution.py:617
  18.7 1.6 %collective-permute-start.1 = (bf16[6,128,512]{2,1,0:T(8,128)(2,1)}, bf16[6,128,512]{2,1,0:T(8,128)(2,1)}, u32[]{:S(2)}, u32[]{:S(2)}) collective-permute-start(bf16[6,128,512]{2,1,0:T(8,128)(2,1)} %collective-permute-done.first), channel_id=1, source_target_pairs={{4,8},{9,5},{6,10},{11,7},{20,24},{25,21},{22,26},{27,23}} | collective-permute-start | bytes 2359304 | tf_op jit(solution)/shard_map/ppermute | solution.py:613
  20.3 5.6 %collective-permute-done.7.first = bf16[6,128,512]{2,1,0:T(8,128)(2,1)} collective-permute-done((bf16[6,128,512]{2,1,0:T(8,128)(2,1)}, bf16[6,128,512]{2,1,0:T(8,128)(2,1)}, u32[]{:S(2)}, u32[]{:S(2)}) %collective-permute-start.7) | collective-permute-done | bytes 786464 | tf_op jit(solution)/shard_map/ppermute | solution.py:613
  25.9 1.5 %collective-permute-start.9 = (bf16[6,128,512]{2,1,0:T(8,128)(2,1)}, bf16[6,128,512]{2,1,0:T(8,128)(2,1)}, u32[]{:S(2)}, u32[]{:S(2)}) collective-permute-start(bf16[6,128,512]{2,1,0:T(8,128)(2,1)} %collective-permute-done.7.first), channel_id=1, source_target_pairs={{4,8},{9,5},{6,10},{11,7},{20,24},{25,21},{22,26},{27,23}} | collective-permute-start | bytes 2359304 | tf_op jit(solution)/shard_map/ppermute | solution.py:613
  27.4 1.3 %collective-permute-start.8 = (bf16[6,128,512]{2,1,0:T(8,128)(2,1)}, bf16[6,128,512]{2,1,0:T(8,128)(2,1)}, u32[]{:S(2)}, u32[]{:S(2)}) collective-permute-start(bf16[6,128,512]{2,1,0:T(8,128)(2,1)} %collective-permute-done.7.first), channel_id=1, source_target_pairs={{4,5},{9,8},{12,13},{1,0},{6,7},{11,10},{14,15},{3,2},{20,21},{25,... | collective-permute-start | bytes 2359304 | tf_op jit(solution)/shard_map/ppermute | solution.py:617
  28.7 2.5 %tables.1.table = s32[232]{0:T(256)} custom-call(s32[8,24]{1,0:T(8,128)} %shift.1, s32[24]{0:T(128)} %slot.1, s32[3,24]{1,0:T(4,128)} %bitcast.34), custom_call_target="tpu_custom_call" | custom-call | flops 10000 | bytes 4000 | tf_op jit(solution)/shard_map/tables/pallas_call | solution.py:355
  31.2 0.0 collective-permute-done.2.other
  31.2 0.0 collective-permute-done.1.second
  31.3 0.6 copy-done.5
  31.9 1.6 %blend.2 = (bf16[6,128,512]{2,1,0:T(8,128)(2,1)}, bf16[6,128,512]{2,1,0:T(8,128)(2,1)S(1)}) custom-call(s32[232]{0:T(256)S(1)} %copy-done.5, f32[3,24]{1,0:T(4,128)S(1)} %bitcast.28, bf16[6,128,512]{2,1,0:T(8,128)(2,1)} %collective-permute-done.1.second, bf16[6,128,512]{2,1,0:T(8,128)(2,1)} %collective-permute-done.first, ...), custom_call_target="tpu_custom_call" | custom-call | flops 4718592 | bytes 6291456 | tf_op jit(solution)/shard_map/blend/pallas_call | solution.py:416
  33.5 9.0 %collective-permute-start.3 = (bf16[6,128,512]{2,1,0:T(8,128)(2,1)}, bf16[6,128,512]{2,1,0:T(8,128)(2,1)}, u32[]{:S(2)}, u32[]{:S(2)}) collective-permute-start(bf16[6,128,512]{2,1,0:T(8,128)(2,1)} %get-tuple-element.19), channel_id=1, source_target_pairs={{0,4},{4,8},{8,12},{13,9},{9,5},{5,1},{2,6},{6,10},{10,14},{15,11}... | collective-permute-start | bytes 2359304 | tf_op jit(solution)/shard_map/ppermute | solution.py:613
  42.5 0.0 collective-permute-done.9.second
  42.5 1.7 %blend.3 = (bf16[6,128,512]{2,1,0:T(8,128)(2,1)}, bf16[6,128,512]{2,1,0:T(8,128)(2,1)S(1)}) custom-call(s32[232]{0:T(256)S(1)} %copy-done.5, f32[3,24]{1,0:T(4,128)S(1)} %bitcast.29, bf16[6,128,512]{2,1,0:T(8,128)(2,1)} %collective-permute-done.9.second, bf16[6,128,512]{2,1,0:T(8,128)(2,1)} %collective-permute-done.7.first, ...), custom_call_target="tpu_custom_call" | custom-call | flops 4718592 | bytes 6291456 | tf_op jit(solution)/shard_map/blend/pallas_call | solution.py:416
  44.2 0.9 copy-done.3
  45.1 5.2 %collective-permute-start.10 = (bf16[6,128,512]{2,1,0:T(8,128)(2,1)}, bf16[6,128,512]{2,1,0:T(8,128)(2,1)S(1)}, u32[]{:S(2)}, u32[]{:S(2)}) collective-permute-start(bf16[6,128,512]{2,1,0:T(8,128)(2,1)} %get-tuple-element.21), channel_id=1, source_target_pairs={{0,4},{4,8},{8,12},{13,9},{9,5},{5,1},{2,6},{6,10},{10,14},{15,11}... | collective-permute-start | bytes 2359304 | tf_op jit(solution)/shard_map/ppermute | solution.py:613
  50.3 1.1 collective-permute-done.3
  51.4 2.1 %broadcast_select_fusion.1 = bf16[6,128,512]{2,1,0:T(8,128)(2,1)} fusion(bf16[6,128,512]{2,1,0:T(8,128)(2,1)} %copy-done.4, bf16[6,128,512]{2,1,0:T(8,128)(2,1)} %collective-permute-done.3, pred[]{:T(512)S(6)} %eq.8), kind=kLoop, calls=%fused_computation.1 | loop fusion | flops 393216 | bytes 2359297 | tf_op jit(solution)/shard_map/jit(_where)/select_n | solution.py:646
  53.5 1.3 %collective-permute-start.15 = (bf16[6,128,512]{2,1,0:T(8,128)(2,1)}, bf16[6,128,512]{2,1,0:T(8,128)(2,1)}, u32[]{:S(2)}, u32[]{:S(2)}) collective-permute-start(bf16[6,128,512]{2,1,0:T(8,128)(2,1)} %broadcast_select_fusion.1), channel_id=1, source_target_pairs={{8,11},{10,9},{5,6},{7,4},{12,15},{14,13},{1,2},{3,0},{24,27},{26,... | collective-permute-start | bytes 2359304 | tf_op jit(solution)/shard_map/ppermute | solution.py:622
  54.8 0.7 collective-permute-start.4
  55.5 4.5 %collective-permute-done.10 = bf16[6,128,512]{2,1,0:T(8,128)(2,1)S(1)} collective-permute-done((bf16[6,128,512]{2,1,0:T(8,128)(2,1)}, bf16[6,128,512]{2,1,0:T(8,128)(2,1)S(1)}, u32[]{:S(2)}, u32[]{:S(2)}) %collective-permute-start.10) | collective-permute-done | bytes 786464 | tf_op jit(solution)/shard_map/ppermute | solution.py:613
  60.0 1.0 broadcast_select_fusion
  61.0 1.3 %collective-permute-start.17 = (bf16[6,128,512]{2,1,0:T(8,128)(2,1)}, bf16[6,128,512]{2,1,0:T(8,128)(2,1)}, u32[]{:S(2)}, u32[]{:S(2)}) collective-permute-start(bf16[6,128,512]{2,1,0:T(8,128)(2,1)} %broadcast_select_fusion), channel_id=1, source_target_pairs={{8,11},{10,9},{5,6},{7,4},{12,15},{14,13},{1,2},{3,0},{24,27},{26,... | collective-permute-start | bytes 2359304 | tf_op jit(solution)/shard_map/ppermute | solution.py:622
  62.3 1.6 %collective-permute-start.13 = (bf16[6,128,512]{2,1,0:T(8,128)(2,1)S(1)}, bf16[6,128,512]{2,1,0:T(8,128)(2,1)}, u32[]{:S(2)}, u32[]{:S(2)}) collective-permute-start(bf16[6,128,512]{2,1,0:T(8,128)(2,1)S(1)} %collective-permute-done.10), channel_id=1, source_target_pairs={{4,8},{8,12},{9,5},{5,1},{6,10},{10,14},{11,7},{7,3},{20,24},{24,2... | collective-permute-start | bytes 2359304 | tf_op jit(solution)/shard_map/ppermute | solution.py:613
  63.9 1.4 %collective-permute-start.6 = (bf16[6,128,512]{2,1,0:T(8,128)(2,1)}, bf16[6,128,512]{2,1,0:T(8,128)(2,1)S(1)}, u32[]{:S(2)}, u32[]{:S(2)}) collective-permute-start(bf16[6,128,512]{2,1,0:T(8,128)(2,1)} %collective-permute-done.3), channel_id=1, source_target_pairs={{4,5},{9,8},{8,9},{5,4},{12,13},{1,0},{6,7},{11,10},{10,11},{7,6},... | collective-permute-start | bytes 2359304 | tf_op jit(solution)/shard_map/ppermute | solution.py:617
  65.3 1.8 %collective-permute-done.15 = bf16[6,128,512]{2,1,0:T(8,128)(2,1)} collective-permute-done((bf16[6,128,512]{2,1,0:T(8,128)(2,1)}, bf16[6,128,512]{2,1,0:T(8,128)(2,1)}, u32[]{:S(2)}, u32[]{:S(2)}) %collective-permute-start.15) | collective-permute-done | bytes 786464 | tf_op jit(solution)/shard_map/ppermute | solution.py:622
  67.1 1.3 %collective-permute-start.11 = (bf16[6,128,512]{2,1,0:T(8,128)(2,1)S(1)}, bf16[6,128,512]{2,1,0:T(8,128)(2,1)S(1)}, u32[]{:S(2)}, u32[]{:S(2)}) collective-permute-start(bf16[6,128,512]{2,1,0:T(8,128)(2,1)S(1)} %collective-permute-done.10), channel_id=1, source_target_pairs={{4,5},{9,8},{8,9},{5,4},{12,13},{1,0},{6,7},{11,10},{10,11},{7,6},... | collective-permute-start | bytes 2359304 | tf_op jit(solution)/shard_map/ppermute | solution.py:617
  68.4 0.0 collective-permute-done.4
  68.4 1.2 %broadcast_select_fusion.3.refs_14_ = bf16[6,128,512]{2,1,0:T(8,128)(2,1)S(1)} fusion(bf16[6,128,512]{2,1,0:T(8,128)(2,1)} %broadcast_select_fusion.1, bf16[6,128,512]{2,1,0:T(8,128)(2,1)} %collective-permute-done.15, pred[]{:T(512)S(6)} %ge.4), kind=kLoop, calls=%fused_computation.3 | loop fusion | flops 393216 | bytes 2359297 | tf_op jit(solution)/shard_map/jit(_where)/select_n | solution.py:648
  69.7 5.3 %collective-permute-start.16 = (bf16[6,128,512]{2,1,0:T(8,128)(2,1)S(1)}, bf16[6,128,512]{2,1,0:T(8,128)(2,1)S(1)}, u32[]{:S(2)}, u32[]{:S(2)}) collective-permute-start(bf16[6,128,512]{2,1,0:T(8,128)(2,1)S(1)} %broadcast_select_fusion.3.refs_14_), channel_id=1, source_target_pairs={{0,1},{13,12},{4,5},{9,8},{8,9},{5,4},{12,13},{1,0},{2,3},{15,14},... | collective-permute-start | bytes 2359304 | tf_op jit(solution)/shard_map/ppermute | solution.py:617
  75.0 0.6 collective-permute-done.17
  75.6 1.3 %collective-permute-start.12 = (bf16[6,128,512]{2,1,0:T(8,128)(2,1)S(1)}, bf16[6,128,512]{2,1,0:T(8,128)(2,1)S(1)}, u32[]{:S(2)}, u32[]{:S(2)}) collective-permute-start(bf16[6,128,512]{2,1,0:T(8,128)(2,1)S(1)} %collective-permute-done.4), channel_id=1, source_target_pairs={{8,9},{5,4},{12,13},{1,0},{10,11},{7,6},{14,15},{3,2},{24,25},{21,... | collective-permute-start | bytes 2359304 | tf_op jit(solution)/shard_map/ppermute | solution.py:617
  76.9 1.2 %broadcast_select_fusion.2.refs_16_ = bf16[6,128,512]{2,1,0:T(8,128)(2,1)S(1)} fusion(bf16[6,128,512]{2,1,0:T(8,128)(2,1)} %broadcast_select_fusion, bf16[6,128,512]{2,1,0:T(8,128)(2,1)} %collective-permute-done.17, pred[]{:T(512)S(6)} %ge.4), kind=kLoop, calls=%fused_computation.2 | loop fusion | flops 393216 | bytes 2359297 | tf_op jit(solution)/shard_map/jit(_where)/select_n | solution.py:648
  78.1 5.0 %collective-permute-start.18 = (bf16[6,128,512]{2,1,0:T(8,128)(2,1)S(1)}, bf16[6,128,512]{2,1,0:T(8,128)(2,1)S(1)}, u32[]{:S(2)}, u32[]{:S(2)}) collective-permute-start(bf16[6,128,512]{2,1,0:T(8,128)(2,1)S(1)} %broadcast_select_fusion.2.refs_16_), channel_id=1, source_target_pairs={{0,1},{13,12},{4,5},{9,8},{8,9},{5,4},{12,13},{1,0},{2,3},{15,14},... | collective-permute-start | bytes 2359304 | tf_op jit(solution)/shard_map/ppermute | solution.py:617
  83.1 0.0 collective-permute-done.6
  83.1 1.3 %collective-permute-start.14 = (bf16[6,128,512]{2,1,0:T(8,128)(2,1)}, bf16[6,128,512]{2,1,0:T(8,128)(2,1)S(1)}, u32[]{:S(2)}, u32[]{:S(2)}) collective-permute-start(bf16[6,128,512]{2,1,0:T(8,128)(2,1)} %collective-permute-done.13), channel_id=1, source_target_pairs={{8,9},{5,4},{12,13},{1,0},{10,11},{7,6},{14,15},{3,2},{24,25},{21,... | collective-permute-start | bytes 2359304 | tf_op jit(solution)/shard_map/ppermute | solution.py:617
  84.4 0.7 collective-permute-start.5
  85.1 0.7 collective-permute-start.20
  85.9 1.6 %collective-permute-done.14 = bf16[6,128,512]{2,1,0:T(8,128)(2,1)S(1)} collective-permute-done((bf16[6,128,512]{2,1,0:T(8,128)(2,1)}, bf16[6,128,512]{2,1,0:T(8,128)(2,1)S(1)}, u32[]{:S(2)}, u32[]{:S(2)}) %collective-permute-start.14) | collective-permute-done | bytes 786464 | tf_op jit(solution)/shard_map/ppermute | solution.py:617
  87.5 12.7 %grow.1 = (bf16[4,6,256,512]{3,2,1,0:T(8,128)(2,1)}, bf16[6,512,512]{2,1,0:T(8,128)(2,1)S(1)}) custom-call(s32[232]{0:T(256)S(1)} %copy-done.6, bf16[6,256,512]{2,1,0:T(8,128)(2,1)S(1)} %copy-done, bf16[3,256,512]{2,1,0:T(8,128)(2,1)} %bitcast.4.refs_1_, bf16[3,256,512]{2,1,0:T(8,128)(2,1)} %bitcast.5.refs_2_, bf16[3,256,512]{2,1,0:T(8,128)(2,1)} %bitcast.6.refs_3_, ...), custom_call_target="tpu_custom_call" | custom-call | flops 1048576 | bytes 4096 | tf_op jit(solution)/shard_map/grow/pallas_call | solution.py:516
  100.2 1.3 %collective-permute-start.19 = (bf16[6,128,512]{2,1,0:T(8,128)(2,1)S(1)}, bf16[6,128,512]{2,1,0:T(8,128)(2,1)S(1)}, u32[]{:S(2)}, u32[]{:S(2)}) collective-permute-start(bf16[6,128,512]{2,1,0:T(8,128)(2,1)S(1)} %collective-permute-done.5), channel_id=1, source_target_pairs={{12,13},{1,0},{14,15},{3,2},{28,29},{17,16},{30,31},{19,18}} | collective-permute-start | bytes 2359304 | tf_op jit(solution)/shard_map/ppermute | solution.py:617
  101.5 1.3 %collective-permute-start.21 = (bf16[6,128,512]{2,1,0:T(8,128)(2,1)S(1)}, bf16[6,128,512]{2,1,0:T(8,128)(2,1)S(1)}, u32[]{:S(2)}, u32[]{:S(2)}) collective-permute-start(bf16[6,128,512]{2,1,0:T(8,128)(2,1)S(1)} %collective-permute-done.20), channel_id=1, source_target_pairs={{12,13},{1,0},{14,15},{3,2},{28,29},{17,16},{30,31},{19,18}} | collective-permute-start | bytes 2359304 | tf_op jit(solution)/shard_map/ppermute | solution.py:617
  102.8 1.6 %collective-permute-done.19 = bf16[6,128,512]{2,1,0:T(8,128)(2,1)S(1)} collective-permute-done((bf16[6,128,512]{2,1,0:T(8,128)(2,1)S(1)}, bf16[6,128,512]{2,1,0:T(8,128)(2,1)S(1)}, u32[]{:S(2)}, u32[]{:S(2)}) %collective-permute-start.19) | collective-permute-done | bytes 786464 | tf_op jit(solution)/shard_map/ppermute | solution.py:617
  104.3 5.4 %collective-permute-done.21 = bf16[6,128,512]{2,1,0:T(8,128)(2,1)S(1)} collective-permute-done((bf16[6,128,512]{2,1,0:T(8,128)(2,1)S(1)}, bf16[6,128,512]{2,1,0:T(8,128)(2,1)S(1)}, u32[]{:S(2)}, u32[]{:S(2)}) %collective-permute-start.21) | collective-permute-done | bytes 786464 | tf_op jit(solution)/shard_map/ppermute | solution.py:617
  109.8 4.7 %finish.1 = bf16[4,6,256,512]{3,2,1,0:T(8,128)(2,1)} custom-call(s32[232]{0:T(256)S(1)} %copy-done.6, bf16[3,256,512]{2,1,0:T(8,128)(2,1)S(1)} %bitcast.30, bf16[3,256,512]{2,1,0:T(8,128)(2,1)S(1)} %bitcast.32, bf16[3,256,512]{2,1,0:T(8,128)(2,1)S(1)} %bitcast.31, bf16[3,256,512]{2,1,0:T(8,128)(2,1)S(1)} %bitcast.33, ...), custom_call_target="tpu_custom_call", output_to_operand_aliasing={{}: (7, {})} | custom-call | flops 40000000000 | bytes 1048576 | tf_op jit(solution)/shard_map/finish/pallas_call | solution.py:585
  (22 shorter events, 0.0 us)
Async XLA Ops:
  0.0 31.2 %copy-start.1 = (bf16[6,256,512]{2,1,0:T(8,128)(2,1)S(1)}, bf16[6,256,512]{2,1,0:T(8,128)(2,1)}, u32[]{:S(2)}) copy-start(bf16[6,256,512]{2,1,0:T(8,128)(2,1)} %env.5) | copy-start | bytes 4718596
  0.0 31.2 %copy-start = (bf16[6,256,512]{2,1,0:T(8,128)(2,1)S(1)}, bf16[6,256,512]{2,1,0:T(8,128)(2,1)}, u32[]{:S(2)}) copy-start(bf16[6,256,512]{2,1,0:T(8,128)(2,1)} %refs_0_.1) | copy-start | bytes 4718596
  0.0 31.3 %copy-start.7 = (f32[24,3]{0,1:T(4,128)S(1)}, f32[24,3]{0,1:T(4,128)}, u32[]{:S(2)}) copy-start(f32[24,3]{0,1:T(4,128)} %param.13) | copy-start | bytes 868
  2.7 14.8 %collective-permute-start = (bf16[6,128,512]{2,1,0:T(8,128)(2,1)}, bf16[6,128,512]{2,1,0:T(8,128)(2,1)}, u32[]{:S(2)}, u32[]{:S(2)}) collective-permute-start(bf16[6,128,512]{2,1,0:T(8,128)(2,1)} %get-tuple-element.18), channel_id=1, source_target_pairs={{0,4},{4,8},{8,12},{13,9},{9,5},{5,1},{2,6},{6,10},{10,14},{15,11}... | collective-permute-start | bytes 2359304 | tf_op jit(solution)/shard_map/ppermute | solution.py:613
  8.5 17.3 %collective-permute-start.7 = (bf16[6,128,512]{2,1,0:T(8,128)(2,1)}, bf16[6,128,512]{2,1,0:T(8,128)(2,1)}, u32[]{:S(2)}, u32[]{:S(2)}) collective-permute-start(bf16[6,128,512]{2,1,0:T(8,128)(2,1)} %get-tuple-element.20), channel_id=1, source_target_pairs={{0,4},{4,8},{8,12},{13,9},{9,5},{5,1},{2,6},{6,10},{10,14},{15,11}... | collective-permute-start | bytes 2359304 | tf_op jit(solution)/shard_map/ppermute | solution.py:613
  17.4 13.8 %collective-permute-start.2 = (bf16[6,128,512]{2,1,0:T(8,128)(2,1)}, bf16[6,128,512]{2,1,0:T(8,128)(2,1)}, u32[]{:S(2)}, u32[]{:S(2)}) collective-permute-start(bf16[6,128,512]{2,1,0:T(8,128)(2,1)} %collective-permute-done.first), channel_id=1, source_target_pairs={{4,5},{9,8},{12,13},{1,0},{6,7},{11,10},{14,15},{3,2},{20,21},{25,... | collective-permute-start | bytes 2359304 | tf_op jit(solution)/shard_map/ppermute | solution.py:617
  18.7 12.5 %collective-permute-start.1 = (bf16[6,128,512]{2,1,0:T(8,128)(2,1)}, bf16[6,128,512]{2,1,0:T(8,128)(2,1)}, u32[]{:S(2)}, u32[]{:S(2)}) collective-permute-start(bf16[6,128,512]{2,1,0:T(8,128)(2,1)} %collective-permute-done.first), channel_id=1, source_target_pairs={{4,8},{9,5},{6,10},{11,7},{20,24},{25,21},{22,26},{27,23}} | collective-permute-start | bytes 2359304 | tf_op jit(solution)/shard_map/ppermute | solution.py:613
  25.9 16.6 %collective-permute-start.9 = (bf16[6,128,512]{2,1,0:T(8,128)(2,1)}, bf16[6,128,512]{2,1,0:T(8,128)(2,1)}, u32[]{:S(2)}, u32[]{:S(2)}) collective-permute-start(bf16[6,128,512]{2,1,0:T(8,128)(2,1)} %collective-permute-done.7.first), channel_id=1, source_target_pairs={{4,8},{9,5},{6,10},{11,7},{20,24},{25,21},{22,26},{27,23}} | collective-permute-start | bytes 2359304 | tf_op jit(solution)/shard_map/ppermute | solution.py:613
  27.4 15.1 %collective-permute-start.8 = (bf16[6,128,512]{2,1,0:T(8,128)(2,1)}, bf16[6,128,512]{2,1,0:T(8,128)(2,1)}, u32[]{:S(2)}, u32[]{:S(2)}) collective-permute-start(bf16[6,128,512]{2,1,0:T(8,128)(2,1)} %collective-permute-done.7.first), channel_id=1, source_target_pairs={{4,5},{9,8},{12,13},{1,0},{6,7},{11,10},{14,15},{3,2},{20,21},{25,... | collective-permute-start | bytes 2359304 | tf_op jit(solution)/shard_map/ppermute | solution.py:617
  31.3 0.6 copy-start.5
  33.5 9.0 %copy-start.4 = (bf16[6,128,512]{2,1,0:T(8,128)(2,1)}, bf16[6,128,512]{2,1,0:T(8,128)(2,1)S(1)}, u32[]{:S(2)}) copy-start(bf16[6,128,512]{2,1,0:T(8,128)(2,1)S(1)} %get-tuple-element.22) | copy-start | bytes 2359300
  33.5 17.9 %collective-permute-start.3 = (bf16[6,128,512]{2,1,0:T(8,128)(2,1)}, bf16[6,128,512]{2,1,0:T(8,128)(2,1)}, u32[]{:S(2)}, u32[]{:S(2)}) collective-permute-start(bf16[6,128,512]{2,1,0:T(8,128)(2,1)} %get-tuple-element.19), channel_id=1, source_target_pairs={{0,4},{4,8},{8,12},{13,9},{9,5},{5,1},{2,6},{6,10},{10,14},{15,11}... | collective-permute-start | bytes 2359304 | tf_op jit(solution)/shard_map/ppermute | solution.py:613
  44.2 0.9 copy-start.3
  45.1 15.0 %collective-permute-start.10 = (bf16[6,128,512]{2,1,0:T(8,128)(2,1)}, bf16[6,128,512]{2,1,0:T(8,128)(2,1)S(1)}, u32[]{:S(2)}, u32[]{:S(2)}) collective-permute-start(bf16[6,128,512]{2,1,0:T(8,128)(2,1)} %get-tuple-element.21), channel_id=1, source_target_pairs={{0,4},{4,8},{8,12},{13,9},{9,5},{5,1},{2,6},{6,10},{10,14},{15,11}... | collective-permute-start | bytes 2359304 | tf_op jit(solution)/shard_map/ppermute | solution.py:613
  53.5 13.6 %collective-permute-start.15 = (bf16[6,128,512]{2,1,0:T(8,128)(2,1)}, bf16[6,128,512]{2,1,0:T(8,128)(2,1)}, u32[]{:S(2)}, u32[]{:S(2)}) collective-permute-start(bf16[6,128,512]{2,1,0:T(8,128)(2,1)} %broadcast_select_fusion.1), channel_id=1, source_target_pairs={{8,11},{10,9},{5,6},{7,4},{12,15},{14,13},{1,2},{3,0},{24,27},{26,... | collective-permute-start | bytes 2359304 | tf_op jit(solution)/shard_map/ppermute | solution.py:622
  54.8 13.6 %collective-permute-start.4 = (bf16[6,128,512]{2,1,0:T(8,128)(2,1)}, bf16[6,128,512]{2,1,0:T(8,128)(2,1)S(1)}, u32[]{:S(2)}, u32[]{:S(2)}) collective-permute-start(bf16[6,128,512]{2,1,0:T(8,128)(2,1)} %collective-permute-done.3), channel_id=1, source_target_pairs={{4,8},{8,12},{9,5},{5,1},{6,10},{10,14},{11,7},{7,3},{20,24},{24,2... | collective-permute-start | bytes 2359304 | tf_op jit(solution)/shard_map/ppermute | solution.py:613
  60.0 27.4 %copy-start.6 = (s32[232]{0:T(256)S(1)}, s32[232]{0:T(256)}, u32[]{:S(2)}) copy-start(s32[232]{0:T(256)} %tables.1.table) | copy-start | bytes 2788
  61.0 14.5 %collective-permute-start.17 = (bf16[6,128,512]{2,1,0:T(8,128)(2,1)}, bf16[6,128,512]{2,1,0:T(8,128)(2,1)}, u32[]{:S(2)}, u32[]{:S(2)}) collective-permute-start(bf16[6,128,512]{2,1,0:T(8,128)(2,1)} %broadcast_select_fusion), channel_id=1, source_target_pairs={{8,11},{10,9},{5,6},{7,4},{12,15},{14,13},{1,2},{3,0},{24,27},{26,... | collective-permute-start | bytes 2359304 | tf_op jit(solution)/shard_map/ppermute | solution.py:622
  62.3 14.5 %collective-permute-start.13 = (bf16[6,128,512]{2,1,0:T(8,128)(2,1)S(1)}, bf16[6,128,512]{2,1,0:T(8,128)(2,1)}, u32[]{:S(2)}, u32[]{:S(2)}) collective-permute-start(bf16[6,128,512]{2,1,0:T(8,128)(2,1)S(1)} %collective-permute-done.10), channel_id=1, source_target_pairs={{4,8},{8,12},{9,5},{5,1},{6,10},{10,14},{11,7},{7,3},{20,24},{24,2... | collective-permute-start | bytes 2359304 | tf_op jit(solution)/shard_map/ppermute | solution.py:613
  63.9 23.6 %copy-start.2 = (bf16[4,512,512]{2,1,0:T(8,128)(2,1)S(1)}, bf16[4,512,512]{2,1,0:T(8,128)(2,1)}, u32[]{:S(2)}) copy-start(bf16[4,512,512]{2,1,0:T(8,128)(2,1)} %op_ref.1) | copy-start | bytes 6291460
  63.9 19.2 %collective-permute-start.6 = (bf16[6,128,512]{2,1,0:T(8,128)(2,1)}, bf16[6,128,512]{2,1,0:T(8,128)(2,1)S(1)}, u32[]{:S(2)}, u32[]{:S(2)}) collective-permute-start(bf16[6,128,512]{2,1,0:T(8,128)(2,1)} %collective-permute-done.3), channel_id=1, source_target_pairs={{4,5},{9,8},{8,9},{5,4},{12,13},{1,0},{6,7},{11,10},{10,11},{7,6},... | collective-permute-start | bytes 2359304 | tf_op jit(solution)/shard_map/ppermute | solution.py:617
  67.1 17.2 %collective-permute-start.11 = (bf16[6,128,512]{2,1,0:T(8,128)(2,1)S(1)}, bf16[6,128,512]{2,1,0:T(8,128)(2,1)S(1)}, u32[]{:S(2)}, u32[]{:S(2)}) collective-permute-start(bf16[6,128,512]{2,1,0:T(8,128)(2,1)S(1)} %collective-permute-done.10), channel_id=1, source_target_pairs={{4,5},{9,8},{8,9},{5,4},{12,13},{1,0},{6,7},{11,10},{10,11},{7,6},... | collective-permute-start | bytes 2359304 | tf_op jit(solution)/shard_map/ppermute | solution.py:617
  69.7 15.4 %collective-permute-start.16 = (bf16[6,128,512]{2,1,0:T(8,128)(2,1)S(1)}, bf16[6,128,512]{2,1,0:T(8,128)(2,1)S(1)}, u32[]{:S(2)}, u32[]{:S(2)}) collective-permute-start(bf16[6,128,512]{2,1,0:T(8,128)(2,1)S(1)} %broadcast_select_fusion.3.refs_14_), channel_id=1, source_target_pairs={{0,1},{13,12},{4,5},{9,8},{8,9},{5,4},{12,13},{1,0},{2,3},{15,14},... | collective-permute-start | bytes 2359304 | tf_op jit(solution)/shard_map/ppermute | solution.py:617
  75.6 9.6 %collective-permute-start.12 = (bf16[6,128,512]{2,1,0:T(8,128)(2,1)S(1)}, bf16[6,128,512]{2,1,0:T(8,128)(2,1)S(1)}, u32[]{:S(2)}, u32[]{:S(2)}) collective-permute-start(bf16[6,128,512]{2,1,0:T(8,128)(2,1)S(1)} %collective-permute-done.4), channel_id=1, source_target_pairs={{8,9},{5,4},{12,13},{1,0},{10,11},{7,6},{14,15},{3,2},{24,25},{21,... | collective-permute-start | bytes 2359304 | tf_op jit(solution)/shard_map/ppermute | solution.py:617
  78.1 7.8 %collective-permute-start.18 = (bf16[6,128,512]{2,1,0:T(8,128)(2,1)S(1)}, bf16[6,128,512]{2,1,0:T(8,128)(2,1)S(1)}, u32[]{:S(2)}, u32[]{:S(2)}) collective-permute-start(bf16[6,128,512]{2,1,0:T(8,128)(2,1)S(1)} %broadcast_select_fusion.2.refs_16_), channel_id=1, source_target_pairs={{0,1},{13,12},{4,5},{9,8},{8,9},{5,4},{12,13},{1,0},{2,3},{15,14},... | collective-permute-start | bytes 2359304 | tf_op jit(solution)/shard_map/ppermute | solution.py:617
  83.1 4.4 %collective-permute-start.14 = (bf16[6,128,512]{2,1,0:T(8,128)(2,1)}, bf16[6,128,512]{2,1,0:T(8,128)(2,1)S(1)}, u32[]{:S(2)}, u32[]{:S(2)}) collective-permute-start(bf16[6,128,512]{2,1,0:T(8,128)(2,1)} %collective-permute-done.13), channel_id=1, source_target_pairs={{8,9},{5,4},{12,13},{1,0},{10,11},{7,6},{14,15},{3,2},{24,25},{21,... | collective-permute-start | bytes 2359304 | tf_op jit(solution)/shard_map/ppermute | solution.py:617
  84.4 15.8 %collective-permute-start.5 = (bf16[6,128,512]{2,1,0:T(8,128)(2,1)S(1)}, bf16[6,128,512]{2,1,0:T(8,128)(2,1)S(1)}, u32[]{:S(2)}, u32[]{:S(2)}) collective-permute-start(bf16[6,128,512]{2,1,0:T(8,128)(2,1)S(1)} %collective-permute-done.4), channel_id=1, source_target_pairs={{8,12},{5,1},{10,14},{7,3},{24,28},{21,17},{26,30},{23,19}} | collective-permute-start | bytes 2359304 | tf_op jit(solution)/shard_map/ppermute | solution.py:613
  85.1 16.3 %collective-permute-start.20 = (bf16[6,128,512]{2,1,0:T(8,128)(2,1)}, bf16[6,128,512]{2,1,0:T(8,128)(2,1)S(1)}, u32[]{:S(2)}, u32[]{:S(2)}) collective-permute-start(bf16[6,128,512]{2,1,0:T(8,128)(2,1)} %collective-permute-done.13), channel_id=1, source_target_pairs={{8,12},{5,1},{10,14},{7,3},{24,28},{21,17},{26,30},{23,19}} | collective-permute-start | bytes 2359304 | tf_op jit(solution)/shard_map/ppermute | solution.py:613
  100.2 4.2 %collective-permute-start.19 = (bf16[6,128,512]{2,1,0:T(8,128)(2,1)S(1)}, bf16[6,128,512]{2,1,0:T(8,128)(2,1)S(1)}, u32[]{:S(2)}, u32[]{:S(2)}) collective-permute-start(bf16[6,128,512]{2,1,0:T(8,128)(2,1)S(1)} %collective-permute-done.5), channel_id=1, source_target_pairs={{12,13},{1,0},{14,15},{3,2},{28,29},{17,16},{30,31},{19,18}} | collective-permute-start | bytes 2359304 | tf_op jit(solution)/shard_map/ppermute | solution.py:617
  101.5 8.3 %collective-permute-start.21 = (bf16[6,128,512]{2,1,0:T(8,128)(2,1)S(1)}, bf16[6,128,512]{2,1,0:T(8,128)(2,1)S(1)}, u32[]{:S(2)}, u32[]{:S(2)}) collective-permute-start(bf16[6,128,512]{2,1,0:T(8,128)(2,1)S(1)} %collective-permute-done.20), channel_id=1, source_target_pairs={{12,13},{1,0},{14,15},{3,2},{28,29},{17,16},{30,31},{19,18}} | collective-permute-start | bytes 2359304 | tf_op jit(solution)/shard_map/ppermute | solution.py:617

commit v4 on v3

--- a/solution.py
+++ b/solution.py
@@ -263,7 +263,6 @@
 
 
 DEPTH = 4
-GROW_COST = 40 * 10**9
 MIX_WIDTH = 8
 LIST = 16
 
@@ -280,32 +279,29 @@
     return result
 
 
-def head_kernel(env, ground, first, second, sems):
+def head_kernel(h, env, ground, sent, sem):
     _, _, spot = device_place()
     half = env.shape[1] // 2
 
-    def send(sources):
-        copies = [pltpu.make_async_copy(sources[h], (first, second)[h], sems.at[h]) for h in range(2)]
-        for copy in copies:
-            copy.start()
-        for copy in copies:
-            copy.wait()
-
-    pl.when(spot == 2)(lambda: send([ground.at[h] for h in range(2)]))
-    pl.when(spot != 2)(lambda: send([env.at[:, pl.ds(h * half, half)] for h in range(2)]))
-
-
-def head(env_ground, ground_half):
+    def send(source):
+        copy = pltpu.make_async_copy(source, sent, sem)
+        copy.start()
+        copy.wait()
+
+    pl.when(spot == 2)(lambda: send(ground.at[h]))
+    pl.when(spot != 2)(lambda: send(env.at[:, pl.ds(h * half, half)]))
+
+
+def head(h, env_ground, ground_half):
     sec_dev, rows, columns = env_ground.shape
-    block = jax.ShapeDtypeStruct((sec_dev, rows // 2, columns), BF16)
     return pl.pallas_call(
-        head_kernel,
-        out_shape=[block, block],
+        functools.partial(head_kernel, h),
+        out_shape=jax.ShapeDtypeStruct((sec_dev, rows // 2, columns), BF16),
         in_specs=[HBM, HBM],
-        out_specs=[VMEM, VMEM],
-        scratch_shapes=[pltpu.SemaphoreType.DMA((2,))],
+        out_specs=VMEM,
+        scratch_shapes=[pltpu.SemaphoreType.DMA],
         compiler_params=pltpu.CompilerParams(vmem_limit_bytes=LARGE),
-        cost_estimate=pl.CostEstimate(flops=0, bytes_accessed=4 * sec_dev * rows * columns, transcendentals=0),
+        cost_estimate=pl.CostEstimate(flops=0, bytes_accessed=2 * sec_dev * rows * columns, transcendentals=0),
         name="head",
     )(env_ground, ground_half)
 
@@ -446,7 +442,7 @@
     owner, core, spot = device_place()
     rows, columns = grounds[0].shape[1:]
     width = sec_dev // 2
-    pieces, (out_ref, env, found, ground, result, ground_sem, out_sem, env_sem) = refs[:4], refs[4:]
+    pieces, (out_ref, env, found, ground, result, ground_sem, out_sem, env_sem) = refs[:12], refs[12:]
     count_at = 2 * sec_dev * MIX_WIDTH
     list_at = count_at + 8
     part_of = [half_owner(owner, core, spot, hops, h, sibling) for _, hops, h, sibling, _ in parts]
@@ -460,12 +456,18 @@
     env_copies = []
     half = rows // 2
     own = lax.axis_index("blk") * rows
-    lead = spot >= 2
-    starts = [jnp.where(lead, own, rows - own), jnp.where(lead, rows - own, own)]
-    for n in range(4):
-        start = pl.multiple_of(starts[n % 2] + n // 2 * half, half)
-        env_copies.append(pltpu.make_async_copy(pieces[n], env.at[:, pl.ds(start, half)], env_sem.at[n]))
-        env_copies[-1].start()
+    for h in range(2):
+        made, near, got, swapped, far, back = pieces[6 * h : 6 * h + 6]
+        choices = [[swapped, near, made, got], [far, far, back, back]]
+        for n, start in enumerate((own + h * half, rows - own + h * half)):
+            target = env.at[:, pl.ds(pl.multiple_of(start, half), half)]
+            for q in range(4):
+
+                @pl.when(spot == q)
+                def _(source=choices[n][q], target=target, sem=env_sem.at[2 * h + n]):
+                    pltpu.make_async_copy(source, target, sem).start()
+
+            env_copies.append(pltpu.make_async_copy(target, target, env_sem.at[2 * h + n]))
 
     total = jnp.int32(0)
     for m in range(len(parts)):
@@ -535,24 +537,24 @@
     )(table, *grounds, op_matrices, *pieces)
 
 
-def finish_kernel(dims, ops_dev, table, own_a, other_a, own_b, other_b, op_ref, env, _, out_ref, found, result, out_sem):
-    ops, sectors, sec_dev, terms = dims
+def finish_kernel(dims, ops_dev, parts, table, *refs):
+    ops, sectors, sec_dev, terms = dims
+    grounds, (op_ref, env, _, out_ref, found, result, out_sem) = refs[: len(parts)], refs[len(parts) :]
     owner, core, spot = device_place()
     count_at = 2 * sec_dev * MIX_WIDTH
     list_at = count_at + 8
     total = jnp.int32(0)
-    for h in range(2):
-        part = jnp.where(spot == 3, half_owner(owner, core, spot, [0, 0, 0, 3], h, False), -1)
-        part = jnp.where(spot == 0, half_owner(owner, core, spot, [0, 0, 0, 3], h, True), part)
+    for n, (hops, h, sibling) in enumerate(parts):
+        part = half_owner(owner, core, spot, hops, h, sibling)
         count = jnp.where(part >= 0, table[count_at + jnp.maximum(part, 0)], 0)
 
-        def take(n, carry, part=part, total=total, h=h):
-            entry = table[list_at + part * LIST + n]
+        def take(i, carry, part=part, total=total, n=n):
+            entry = table[list_at + part * LIST + i]
             rest = entry // sec_dev
-            found[0, total + n] = h
-            found[1, total + n] = rest // ops_dev
-            found[2, total + n] = lax.rem(rest, ops_dev)
-            found[3, total + n] = lax.rem(entry, sec_dev)
+            found[0, total + i] = n
+            found[1, total + i] = rest // ops_dev
+            found[2, total + i] = lax.rem(rest, ops_dev)
+            found[3, total + i] = lax.rem(entry, sec_dev)
             return carry
 
         lax.fori_loop(0, count, take, 0)
@@ -563,10 +565,10 @@
 
     def step(i, carry):
         side = lax.rem(i, DEPTH)
-        h, s, o, local = (found[k, i] for k in range(4))
-        first = jnp.where(spot == 3, own_a[s], other_a[s])
-        second = jnp.where(spot == 3, own_b[s], other_b[s])
-        block = jnp.where(h == 0, first, second)
+        which, s, o, local = (found[k, i] for k in range(4))
+        block = grounds[0][s]
+        for n in range(1, len(parts)):
+            block = jnp.where(which == n, grounds[n][s], block)
         product = jnp.dot(block, op_ref[o], preferred_element_type=jnp.float32).astype(BF16)
         grown = jnp.dot(product, env[local], preferred_element_type=jnp.float32).astype(BF16)
         pl.when(i >= DEPTH)(lambda: drain(side))
@@ -579,24 +581,24 @@
         pl.when(total >= back)(lambda back=back: drain(lax.rem(total - back, DEPTH)))
 
 
-def finish(dims, table, ends, op_matrices, env, out):
+def finish(dims, table, parts, grounds, op_matrices, env, out, cost):
     ops, sectors, sec_dev, terms = dims
     ops_dev, _, rows, columns = out.shape
     return pl.pallas_call(
-        functools.partial(finish_kernel, dims, ops_dev),
+        functools.partial(finish_kernel, dims, ops_dev, parts),
         out_shape=jax.ShapeDtypeStruct(out.shape, BF16),
-        in_specs=[SMEM] + [VMEM] * 6 + [ANY],
+        in_specs=[SMEM] + [VMEM] * (len(parts) + 2) + [ANY],
         out_specs=ANY,
         scratch_shapes=[
-            pltpu.SMEM((4, sec_dev * ops_dev), jnp.int32),
+            pltpu.SMEM((4, LIST * len(parts)), jnp.int32),
             pltpu.VMEM((DEPTH, rows, columns), BF16),
             pltpu.SemaphoreType.DMA((DEPTH,)),
         ],
-        input_output_aliases={7: 0},
+        input_output_aliases={len(parts) + 3: 0},
         compiler_params=pltpu.CompilerParams(vmem_limit_bytes=MEDIUM),
-        cost_estimate=pl.CostEstimate(flops=GROW_COST, bytes_accessed=1 << 20, transcendentals=0),
+        cost_estimate=pl.CostEstimate(flops=cost, bytes_accessed=1 << 12, transcendentals=0),
         name="finish",
-    )(table, *ends, op_matrices, env, out)
+    )(table, *grounds, op_matrices, env, out)
 
 
 def line_of_four(ground_state, op_matrices, shift_map, new_slot, env_ground, env_src, env_coef):
@@ -629,7 +631,7 @@
     ground_half = ground_state.reshape(2, sec_dev, half, columns)
     both = range(2)
 
-    sent0 = head(env_ground, ground_half)
+    sent0 = [head(h, env_ground, ground_half) for h in both]
     got0 = [every(sent0[h]) for h in both]
     got2 = [middle(got0[h]) for h in both]
     swapped0 = [hand(got0[h], [1, 3]) for h in both]
@@ -638,34 +640,42 @@
         *[blend(dims, h, table, env_coef.T, got2[h], got0[h], env_ground, swapped0[h], ground_half) for h in both]
     )
     got4 = [every(sent4[h]) for h in both]
-    got6 = [late(got4[h]) for h in both]
+    near = [hand(made[h], [2]) for h in both]
+    got6 = [late(got4[0]), late(after(got4[1], *near))]
     swapped4 = [hand(got4[h], [1, 2, 3]) for h in both]
-    swapped6 = [hand(got6[h], [2, 3]) for h in both]
-    pieces = []
-    for h in both:
-        mine = jnp.where(spot == 2, made[h], got4[h])
-        received = after(across(mine), got6[h])
-        kept = jnp.where(spot >= 2, mine, received)
-        pieces += [kept, hand(kept, [0, 1, 2, 3])]
-    got8 = [last(got6[0]), last(after(got6[1], *swapped4, swapped6[0], pieces[1]))]
+    swapped6 = [hand(got6[0], [2, 3])]
+    far = [across(jnp.where(spot == 2, made[h], got4[h])) for h in both]
+    back = [hand(after(far[h], got6[0]), [0, 1]) for h in both]
+    got8 = [last(got6[0]), last(after(got6[1], *swapped4, swapped6[0], back[0]))]
+    pieces = [block[h] for h in both for block in (made, near, got4, swapped4, far, back)]
 
     parts = [(0, None, h, False, h * sec_dev // 2) for h in both]
     arrays = [ground_state]
+
+    def blocks(block):
+        return block.reshape(sec_dev // 2, rows, columns)
 
     def hold(mine, theirs, hops, h):
         for block, sibling in ((mine, False), (theirs, True)):
             parts.append((len(arrays), hops, h, sibling, 0))
-            arrays.append(block.reshape(sec_dev // 2, rows, columns))
+            arrays.append(blocks(block))
 
     for h in both:
         hold(got0[h], swapped0[h], [0, 0, 0, 1], h)
         hold(got4[h], swapped4[h], [0, 1, 1, 0], h)
+    hold(got6[0], swapped6[0], [0, 0, 2, 2], 0)
+    parts.append((len(arrays), [0, 0, 2, 2], 1, False, 0))
+    arrays.append(blocks(got6[1]))
+    out, env = grow(dims, table, parts, arrays, op_matrices, pieces)
+    swapped6.append(hand(after(got6[1], out), [2, 3]))
+    swapped8 = [hand(after(got8[h], out), [3]) for h in both]
+    ends, owners = [blocks(swapped6[1])], [([0, 0, 2, 2], 1, True)]
     for h in both:
-        hold(got6[h], swapped6[h], [0, 0, 2, 2], h)
-    out, env = grow(dims, table, parts, arrays, op_matrices, pieces)
-    swapped8 = [hand(after(got8[h], out), [3]) for h in both]
-    ends = [block[h].reshape(sec_dev // 2, rows, columns) for h in both for block in (got8, swapped8)]
-    return finish(dims, table, ends, op_matrices, env, out)
+        ends += [blocks(got8[h]), blocks(swapped8[h])]
+        owners += [([0, 0, 0, 3], h, False), ([0, 0, 0, 3], h, True)]
+        out = finish(dims, table, owners, ends, op_matrices, env, out, 1 << 20)
+        ends, owners = [], []
+    return out
 
 
 def solution(mesh):

time: 116 us -> 112 us (0.966)
  waiting for transfers between devices: 27.7 us -> 19.5 us
  starting transfers between devices: 53.5 us -> 58.6 us
  other arithmetic: 5.55 us -> 1.32 us
  Pallas kernels: 25.9 us -> 28.8 us
    ppermute x10 -> x12, waiting for transfers between devices: 8.62 us -> 2.62 us  [hand(): return lax.ppermute(block, ('sec', 'op'), pairs_of)]
    ppermute x10 -> x12, starting transfers between devices: 20.7 us -> 26.5 us  [hand(): return lax.ppermute(block, ('sec', 'op'), pairs_of)]
    select_n x4 -> x2, other arithmetic: 5.55 us -> 1.32 us  [line_of_four(): far = [across(jnp.where(spot == 2, made[h], got4[h])) for h in both]]
    pallas_call x2 -> x4, Pallas kernels: 7.42 us -> 11.4 us  [the longest x2 7.17 us: finish(): pl.pallas_call(functools.partial(finish_kernel, dims, ops_dev, parts), ou...]
    ppermute x10, waiting for transfers between devices: 16.6 us -> 13.9 us  [stream(): return lambda block: lax.ppermute(block, ('sec', 'op'), up + down)]
  transfers between devices with their start and end apart: 22 -> 24, of which waited for: 9 -> 7; matrix products, arithmetic and copies ran while one was open for 5% -> 1% of each run, Pallas kernels for 16% -> 22%
where the time goes in v4:
time: 112 us; the launch traced here: 110 us
  starting transfers between devices  58.6 us (52%)
  Pallas kernels  28.8 us (26%)
  waiting for transfers between devices  19.5 us (17%)
  local copies, waits for them, and re-layouts  1.52 us (1%)
  other arithmetic  1.32 us (1%)
    ppermute x10, starting transfers between devices, stream(): return lambda block: lax.ppermute(block, ('sec', 'op'), up + down)  29.5 us
    ppermute x12, starting transfers between devices, hand(): return lax.ppermute(block, ('sec', 'op'), pairs_of)  26.5 us
    ppermute x10, waiting for transfers between devices, stream(): return lambda block: lax.ppermute(block, ('sec', 'op'), up + down)  13.9 us
    pallas_call x1, Pallas kernels, grow(): pl.pallas_call(functools.partial(grow_kernel, dims, ops_dev, parts, len(g...  11.6 us
    pallas_call x2, Pallas kernels, finish(): pl.pallas_call(functools.partial(finish_kernel, dims, ops_dev, parts), ou...  7.17 us
    pallas_call x2, Pallas kernels, head(): pl.pallas_call(functools.partial(head_kernel, h), out_shape=jax.ShapeDtyp...  4.2 us
    pallas_call x2, Pallas kernels, blend(): pl.pallas_call(functools.partial(blend_kernel, dims, which), out_shape=[b...  3.32 us
    ppermute x2, waiting for transfers between devices, across(): return lax.ppermute(block, ('sec', 'blk', 'op'), pairs_of)  2.97 us
  transfers between devices with their start and end apart: 24, of which 7 were waited for; matrix products, arithmetic and copies ran while one was open for 1% of the time, Pallas kernels for 22%

profile of v4, /device:TPU:0, one launch (start us, length us, event | category | flops | bytes accessed | tf_op | source)
XLA Modules:
  0.0 110.1 jit_solution(6431900481166121823)
XLA Ops:
  0.0 2.2 %head.3 = bf16[6,128,512]{2,1,0:T(8,128)(2,1)} custom-call(bf16[6,256,512]{2,1,0:T(8,128)(2,1)} %env.7, bf16[2,6,128,512]{3,2,1,0:T(8,128)(2,1)} %bitcast.19), custom_call_target="tpu_custom_call" | custom-call | bytes 1572864 | tf_op jit(solution)/shard_map/head/pallas_call | solution.py:297
  2.2 5.8 %collective-permute-start.4 = (bf16[6,128,512]{2,1,0:T(8,128)(2,1)}, bf16[6,128,512]{2,1,0:T(8,128)(2,1)}, u32[]{:S(2)}, u32[]{:S(2)}) collective-permute-start(bf16[6,128,512]{2,1,0:T(8,128)(2,1)} %head.3), channel_id=1, source_target_pairs={{0,4},{4,8},{8,12},{13,9},{9,5},{5,1},{2,6},{6,10},{10,14},{15,11}... | collective-permute-start | bytes 2359304 | tf_op jit(solution)/shard_map/ppermute | solution.py:615
  8.0 2.0 %head.2 = bf16[6,128,512]{2,1,0:T(8,128)(2,1)} custom-call(bf16[6,256,512]{2,1,0:T(8,128)(2,1)} %env.7, bf16[2,6,128,512]{3,2,1,0:T(8,128)(2,1)} %bitcast.20), custom_call_target="tpu_custom_call" | custom-call | bytes 1572864 | tf_op jit(solution)/shard_map/head/pallas_call | solution.py:297
  10.1 3.5 %collective-permute-start = (bf16[6,128,512]{2,1,0:T(8,128)(2,1)}, bf16[6,128,512]{2,1,0:T(8,128)(2,1)}, u32[]{:S(2)}, u32[]{:S(2)}) collective-permute-start(bf16[6,128,512]{2,1,0:T(8,128)(2,1)} %head.2), channel_id=1, source_target_pairs={{0,4},{4,8},{8,12},{13,9},{9,5},{5,1},{2,6},{6,10},{10,14},{15,11}... | collective-permute-start | bytes 2359304 | tf_op jit(solution)/shard_map/ppermute | solution.py:615
  13.6 3.4 %collective-permute-done.4.first = bf16[6,128,512]{2,1,0:T(8,128)(2,1)} collective-permute-done((bf16[6,128,512]{2,1,0:T(8,128)(2,1)}, bf16[6,128,512]{2,1,0:T(8,128)(2,1)}, u32[]{:S(2)}, u32[]{:S(2)}) %collective-permute-start.4) | collective-permute-done | bytes 786464 | tf_op jit(solution)/shard_map/ppermute | solution.py:615
  17.0 1.3 %collective-permute-start.6 = (bf16[6,128,512]{2,1,0:T(8,128)(2,1)}, bf16[6,128,512]{2,1,0:T(8,128)(2,1)}, u32[]{:S(2)}, u32[]{:S(2)}) collective-permute-start(bf16[6,128,512]{2,1,0:T(8,128)(2,1)} %collective-permute-done.4.first), channel_id=1, source_target_pairs={{4,5},{9,8},{12,13},{1,0},{6,7},{11,10},{14,15},{3,2},{20,21},{25,... | collective-permute-start | bytes 2359304 | tf_op jit(solution)/shard_map/ppermute | solution.py:619
  18.2 1.6 %collective-permute-start.5 = (bf16[6,128,512]{2,1,0:T(8,128)(2,1)}, bf16[6,128,512]{2,1,0:T(8,128)(2,1)}, u32[]{:S(2)}, u32[]{:S(2)}) collective-permute-start(bf16[6,128,512]{2,1,0:T(8,128)(2,1)} %collective-permute-done.4.first), channel_id=1, source_target_pairs={{4,8},{9,5},{6,10},{11,7},{20,24},{25,21},{22,26},{27,23}} | collective-permute-start | bytes 2359304 | tf_op jit(solution)/shard_map/ppermute | solution.py:615
  19.8 5.6 %collective-permute-done.first = bf16[6,128,512]{2,1,0:T(8,128)(2,1)} collective-permute-done((bf16[6,128,512]{2,1,0:T(8,128)(2,1)}, bf16[6,128,512]{2,1,0:T(8,128)(2,1)}, u32[]{:S(2)}, u32[]{:S(2)}) %collective-permute-start) | collective-permute-done | bytes 786464 | tf_op jit(solution)/shard_map/ppermute | solution.py:615
  25.4 1.3 %collective-permute-start.2 = (bf16[6,128,512]{2,1,0:T(8,128)(2,1)}, bf16[6,128,512]{2,1,0:T(8,128)(2,1)}, u32[]{:S(2)}, u32[]{:S(2)}) collective-permute-start(bf16[6,128,512]{2,1,0:T(8,128)(2,1)} %collective-permute-done.first), channel_id=1, source_target_pairs={{4,5},{9,8},{12,13},{1,0},{6,7},{11,10},{14,15},{3,2},{20,21},{25,... | collective-permute-start | bytes 2359304 | tf_op jit(solution)/shard_map/ppermute | solution.py:619
  26.7 1.6 %collective-permute-start.1 = (bf16[6,128,512]{2,1,0:T(8,128)(2,1)}, bf16[6,128,512]{2,1,0:T(8,128)(2,1)}, u32[]{:S(2)}, u32[]{:S(2)}) collective-permute-start(bf16[6,128,512]{2,1,0:T(8,128)(2,1)} %collective-permute-done.first), channel_id=1, source_target_pairs={{4,8},{9,5},{6,10},{11,7},{20,24},{25,21},{22,26},{27,23}} | collective-permute-start | bytes 2359304 | tf_op jit(solution)/shard_map/ppermute | solution.py:615
  28.2 2.5 %tables.1.table = s32[232]{0:T(256)} custom-call(s32[8,24]{1,0:T(8,128)} %shift.1, s32[24]{0:T(128)} %slot.1, s32[3,24]{1,0:T(4,128)} %bitcast.36), custom_call_target="tpu_custom_call" | custom-call | flops 10000 | bytes 4000 | tf_op jit(solution)/shard_map/tables/pallas_call | solution.py:351
  30.7 0.0 collective-permute-done.5.second
  30.8 0.6 copy-done.7
  31.4 1.7 %blend.3 = (bf16[6,128,512]{2,1,0:T(8,128)(2,1)}, bf16[6,128,512]{2,1,0:T(8,128)(2,1)S(1)}) custom-call(s32[232]{0:T(256)S(1)} %copy-done.7, f32[3,24]{1,0:T(4,128)S(1)} %bitcast.34, bf16[6,128,512]{2,1,0:T(8,128)(2,1)} %collective-permute-done.5.second, bf16[6,128,512]{2,1,0:T(8,128)(2,1)} %collective-permute-done.4.first, ...), custom_call_target="tpu_custom_call" | custom-call | flops 4718592 | bytes 6291456 | tf_op jit(solution)/shard_map/blend/pallas_call | solution.py:412
  33.1 8.1 %collective-permute-start.10 = (bf16[6,128,512]{2,1,0:T(8,128)(2,1)}, bf16[6,128,512]{2,1,0:T(8,128)(2,1)}, u32[]{:S(2)}, u32[]{:S(2)}) collective-permute-start(bf16[6,128,512]{2,1,0:T(8,128)(2,1)} %get-tuple-element.22), channel_id=1, source_target_pairs={{0,4},{4,8},{8,12},{13,9},{9,5},{5,1},{2,6},{6,10},{10,14},{15,11}... | collective-permute-start | bytes 2359304 | tf_op jit(solution)/shard_map/ppermute | solution.py:615
  41.2 1.6 %blend.2 = (bf16[6,128,512]{2,1,0:T(8,128)(2,1)}, bf16[6,128,512]{2,1,0:T(8,128)(2,1)S(1)}) custom-call(s32[232]{0:T(256)S(1)} %copy-done.7, f32[3,24]{1,0:T(4,128)S(1)} %bitcast.35, bf16[6,128,512]{2,1,0:T(8,128)(2,1)} %collective-permute-done.1.second, bf16[6,128,512]{2,1,0:T(8,128)(2,1)} %collective-permute-done.first, ...), custom_call_target="tpu_custom_call" | custom-call | flops 4718592 | bytes 6291456 | tf_op jit(solution)/shard_map/blend/pallas_call | solution.py:412
  42.9 0.9 copy-done.5
  43.8 6.1 %collective-permute-start.3 = (bf16[6,128,512]{2,1,0:T(8,128)(2,1)}, bf16[6,128,512]{2,1,0:T(8,128)(2,1)S(1)}, u32[]{:S(2)}, u32[]{:S(2)}) collective-permute-start(bf16[6,128,512]{2,1,0:T(8,128)(2,1)} %get-tuple-element.18), channel_id=1, source_target_pairs={{0,4},{4,8},{8,12},{13,9},{9,5},{5,1},{2,6},{6,10},{10,14},{15,11}... | collective-permute-start | bytes 2359304 | tf_op jit(solution)/shard_map/ppermute | solution.py:615
  49.9 0.0 copy-start.2
  49.9 0.8 collective-permute-start.7
  50.8 0.7 collective-permute-start.8
  51.5 0.0 collective-permute-done.10.refs_15_
  51.5 1.2 %broadcast_select_fusion.1 = bf16[6,128,512]{2,1,0:T(8,128)(2,1)S(1)} fusion(bf16[6,128,512]{2,1,0:T(8,128)(2,1)} %copy-done.3, bf16[6,128,512]{2,1,0:T(8,128)(2,1)} %collective-permute-done.10.refs_15_, pred[]{:T(512)S(6)} %eq.8), kind=kLoop, calls=%fused_computation.1 | loop fusion | flops 393216 | bytes 2359297 | tf_op jit(solution)/shard_map/jit(_where)/select_n | solution.py:647
  52.7 1.3 %collective-permute-start.15 = (bf16[6,128,512]{2,1,0:T(8,128)(2,1)S(1)}, bf16[6,128,512]{2,1,0:T(8,128)(2,1)S(1)}, u32[]{:S(2)}, u32[]{:S(2)}) collective-permute-start(bf16[6,128,512]{2,1,0:T(8,128)(2,1)S(1)} %broadcast_select_fusion.1), channel_id=1, source_target_pairs={{8,11},{10,9},{5,6},{7,4},{12,15},{14,13},{1,2},{3,0},{24,27},{26,... | collective-permute-start | bytes 2359304 | tf_op jit(solution)/shard_map/ppermute | solution.py:624
  54.0 0.7 collective-permute-start.13
  54.8 4.9 %collective-permute-done.3.refs_21_ = bf16[6,128,512]{2,1,0:T(8,128)(2,1)S(1)} collective-permute-done((bf16[6,128,512]{2,1,0:T(8,128)(2,1)}, bf16[6,128,512]{2,1,0:T(8,128)(2,1)S(1)}, u32[]{:S(2)}, u32[]{:S(2)}) %collective-permute-start.3) | collective-permute-done | bytes 786464 | tf_op jit(solution)/shard_map/ppermute | solution.py:615
  59.7 0.1 broadcast_select_fusion
  59.7 1.3 %collective-permute-start.18 = (bf16[6,128,512]{2,1,0:T(8,128)(2,1)S(1)}, bf16[6,128,512]{2,1,0:T(8,128)(2,1)S(1)}, u32[]{:S(2)}, u32[]{:S(2)}) collective-permute-start(bf16[6,128,512]{2,1,0:T(8,128)(2,1)S(1)} %broadcast_select_fusion), channel_id=1, source_target_pairs={{8,11},{10,9},{5,6},{7,4},{12,15},{14,13},{1,2},{3,0},{24,27},{26,... | collective-permute-start | bytes 2359304 | tf_op jit(solution)/shard_map/ppermute | solution.py:624
  61.1 0.0 collective-permute-done.8.refs_20_
  61.1 0.7 collective-permute-start.9
  61.8 1.3 %collective-permute-start.11 = (bf16[6,128,512]{2,1,0:T(8,128)(2,1)}, bf16[6,128,512]{2,1,0:T(8,128)(2,1)S(1)}, u32[]{:S(2)}, u32[]{:S(2)}) collective-permute-start(bf16[6,128,512]{2,1,0:T(8,128)(2,1)} %collective-permute-done.10.refs_15_), channel_id=1, source_target_pairs={{4,5},{9,8},{8,9},{5,4},{12,13},{1,0},{6,7},{11,10},{10,11},{7,6},... | collective-permute-start | bytes 2359304 | tf_op jit(solution)/shard_map/ppermute | solution.py:619
  63.1 3.0 %collective-permute-done.15.refs_17_ = bf16[6,128,512]{2,1,0:T(8,128)(2,1)S(1)} collective-permute-done((bf16[6,128,512]{2,1,0:T(8,128)(2,1)S(1)}, bf16[6,128,512]{2,1,0:T(8,128)(2,1)S(1)}, u32[]{:S(2)}, u32[]{:S(2)}) %collective-permute-start.15) | collective-permute-done | bytes 786464 | tf_op jit(solution)/shard_map/ppermute | solution.py:624
  66.1 1.3 %collective-permute-start.12 = (bf16[6,128,512]{2,1,0:T(8,128)(2,1)S(1)}, bf16[6,128,512]{2,1,0:T(8,128)(2,1)S(1)}, u32[]{:S(2)}, u32[]{:S(2)}) collective-permute-start(bf16[6,128,512]{2,1,0:T(8,128)(2,1)S(1)} %collective-permute-done.3.refs_21_), channel_id=1, source_target_pairs={{4,5},{9,8},{8,9},{5,4},{12,13},{1,0},{6,7},{11,10},{10,11},{7,6},... | collective-permute-start | bytes 2359304 | tf_op jit(solution)/shard_map/ppermute | solution.py:619
  67.3 0.0 collective-permute-done.13
  67.4 7.8 %collective-permute-start.16 = (bf16[6,128,512]{2,1,0:T(8,128)(2,1)S(1)}, bf16[6,128,512]{2,1,0:T(8,128)(2,1)S(1)}, u32[]{:S(2)}, u32[]{:S(2)}) collective-permute-start(bf16[6,128,512]{2,1,0:T(8,128)(2,1)S(1)} %collective-permute-done.15.refs_17_), channel_id=1, source_target_pairs={{0,1},{13,12},{4,5},{9,8},{2,3},{15,14},{6,7},{11,10},{16,17},{29,... | collective-permute-start | bytes 2359304 | tf_op jit(solution)/shard_map/ppermute | solution.py:619
  75.2 1.3 %collective-permute-start.14 = (bf16[6,128,512]{2,1,0:T(8,128)(2,1)S(1)}, bf16[6,128,512]{2,1,0:T(8,128)(2,1)S(1)}, u32[]{:S(2)}, u32[]{:S(2)}) collective-permute-start(bf16[6,128,512]{2,1,0:T(8,128)(2,1)S(1)} %collective-permute-done.13), channel_id=1, source_target_pairs={{8,9},{5,4},{12,13},{1,0},{10,11},{7,6},{14,15},{3,2},{24,25},{21,... | collective-permute-start | bytes 2359304 | tf_op jit(solution)/shard_map/ppermute | solution.py:619
  76.5 6.8 %collective-permute-start.19 = (bf16[6,128,512]{2,1,0:T(8,128)(2,1)S(1)}, bf16[6,128,512]{2,1,0:T(8,128)(2,1)S(1)}, u32[]{:S(2)}, u32[]{:S(2)}) collective-permute-start(bf16[6,128,512]{2,1,0:T(8,128)(2,1)S(1)} %collective-permute-done.18.refs_23_), channel_id=1, source_target_pairs={{0,1},{13,12},{4,5},{9,8},{2,3},{15,14},{6,7},{11,10},{16,17},{29,... | collective-permute-start | bytes 2359304 | tf_op jit(solution)/shard_map/ppermute | solution.py:619
  83.3 0.7 collective-permute-start.22
  84.1 0.7 collective-permute-start.17
  84.8 0.4 collective-permute-done.19.refs_24_
  85.2 11.6 %grow.1 = (bf16[4,6,256,512]{3,2,1,0:T(8,128)(2,1)}, bf16[6,512,512]{2,1,0:T(8,128)(2,1)S(1)}) custom-call(s32[232]{0:T(256)S(1)} %copy-done.8, bf16[6,256,512]{2,1,0:T(8,128)(2,1)S(1)} %copy-done, bf16[3,256,512]{2,1,0:T(8,128)(2,1)} %bitcast.4.refs_1_, bf16[3,256,512]{2,1,0:T(8,128)(2,1)} %bitcast.5.refs_2_, bf16[3,256,512]{2,1,0:T(8,128)(2,1)} %bitcast.6.refs_3_, ...), custom_call_target="tpu_custom_call" | custom-call | flops 1048576 | bytes 4096 | tf_op jit(solution)/shard_map/grow/pallas_call | solution.py:518
  96.8 1.3 %collective-permute-start.23 = (bf16[6,128,512]{2,1,0:T(8,128)(2,1)S(1)}, bf16[6,128,512]{2,1,0:T(8,128)(2,1)S(1)}, u32[]{:S(2)}, u32[]{:S(2)}) collective-permute-start(bf16[6,128,512]{2,1,0:T(8,128)(2,1)S(1)} %collective-permute-done.22), channel_id=1, source_target_pairs={{12,13},{1,0},{14,15},{3,2},{28,29},{17,16},{30,31},{19,18}} | collective-permute-start | bytes 2359304 | tf_op jit(solution)/shard_map/ppermute | solution.py:619
  98.1 1.3 %collective-permute-start.21 = (bf16[6,128,512]{2,1,0:T(8,128)(2,1)S(1)}, bf16[6,128,512]{2,1,0:T(8,128)(2,1)S(1)}, u32[]{:S(2)}, u32[]{:S(2)}) collective-permute-start(bf16[6,128,512]{2,1,0:T(8,128)(2,1)S(1)} %collective-permute-done.9), channel_id=1, source_target_pairs={{8,9},{5,4},{12,13},{1,0},{10,11},{7,6},{14,15},{3,2},{24,25},{21,... | collective-permute-start | bytes 2359304 | tf_op jit(solution)/shard_map/ppermute | solution.py:619
  99.4 1.3 %collective-permute-start.20 = (bf16[6,128,512]{2,1,0:T(8,128)(2,1)S(1)}, bf16[6,128,512]{2,1,0:T(8,128)(2,1)S(1)}, u32[]{:S(2)}, u32[]{:S(2)}) collective-permute-start(bf16[6,128,512]{2,1,0:T(8,128)(2,1)S(1)} %collective-permute-done.17), channel_id=1, source_target_pairs={{12,13},{1,0},{14,15},{3,2},{28,29},{17,16},{30,31},{19,18}} | collective-permute-start | bytes 2359304 | tf_op jit(solution)/shard_map/ppermute | solution.py:619
  100.7 0.9 collective-permute-done.23
  101.6 1.3 %collective-permute-done.21 = bf16[6,128,512]{2,1,0:T(8,128)(2,1)S(1)} collective-permute-done((bf16[6,128,512]{2,1,0:T(8,128)(2,1)S(1)}, bf16[6,128,512]{2,1,0:T(8,128)(2,1)S(1)}, u32[]{:S(2)}, u32[]{:S(2)}) %collective-permute-start.21) | collective-permute-done | bytes 786464 | tf_op jit(solution)/shard_map/ppermute | solution.py:619
  102.9 4.7 %finish.2.refs_4_ = bf16[4,6,256,512]{3,2,1,0:T(8,128)(2,1)} custom-call(s32[232]{0:T(256)S(1)} %copy-done.8, bf16[3,256,512]{2,1,0:T(8,128)(2,1)S(1)} %bitcast.33, bf16[3,256,512]{2,1,0:T(8,128)(2,1)S(1)} %bitcast.28, bf16[3,256,512]{2,1,0:T(8,128)(2,1)S(1)} %bitcast.31, bf16[4,512,512]{2,1,0:T(8,128)(2,1)S(1)} %copy-done.2, ...), custom_call_target="tpu_custom_call", output_to_operand_aliasing={{}: (6, {})} | custom-call | flops 1048576 | bytes 4096 | tf_op jit(solution)/shard_map/finish/pallas_call | solution.py:587
  107.7 2.5 %finish.3 = bf16[4,6,256,512]{3,2,1,0:T(8,128)(2,1)} custom-call(s32[232]{0:T(256)S(1)} %copy-done.8, bf16[3,256,512]{2,1,0:T(8,128)(2,1)S(1)} %bitcast.29, bf16[3,256,512]{2,1,0:T(8,128)(2,1)S(1)} %bitcast.32, bf16[4,512,512]{2,1,0:T(8,128)(2,1)S(1)} %copy-done.2, ...), custom_call_target="tpu_custom_call", output_to_operand_aliasing={{}: (5, {})} | custom-call | flops 1048576 | bytes 4096 | tf_op jit(solution)/shard_map/finish/pallas_call | solution.py:587
  (30 shorter events, 0.1 us)
Async XLA Ops:
  0.0 30.8 %copy-start = (bf16[6,256,512]{2,1,0:T(8,128)(2,1)S(1)}, bf16[6,256,512]{2,1,0:T(8,128)(2,1)}, u32[]{:S(2)}) copy-start(bf16[6,256,512]{2,1,0:T(8,128)(2,1)} %refs_0_.1) | copy-start | bytes 4718596
  0.0 30.8 %copy-start.1 = (bf16[6,256,512]{2,1,0:T(8,128)(2,1)S(1)}, bf16[6,256,512]{2,1,0:T(8,128)(2,1)}, u32[]{:S(2)}) copy-start(bf16[6,256,512]{2,1,0:T(8,128)(2,1)} %env.7) | copy-start | bytes 4718596
  0.0 30.8 %copy-start.9 = (f32[24,3]{0,1:T(4,128)S(1)}, f32[24,3]{0,1:T(4,128)}, u32[]{:S(2)}) copy-start(f32[24,3]{0,1:T(4,128)} %param.13) | copy-start | bytes 868
  2.2 14.8 %collective-permute-start.4 = (bf16[6,128,512]{2,1,0:T(8,128)(2,1)}, bf16[6,128,512]{2,1,0:T(8,128)(2,1)}, u32[]{:S(2)}, u32[]{:S(2)}) collective-permute-start(bf16[6,128,512]{2,1,0:T(8,128)(2,1)} %head.3), channel_id=1, source_target_pairs={{0,4},{4,8},{8,12},{13,9},{9,5},{5,1},{2,6},{6,10},{10,14},{15,11}... | collective-permute-start | bytes 2359304 | tf_op jit(solution)/shard_map/ppermute | solution.py:615
  10.1 15.3 %collective-permute-start = (bf16[6,128,512]{2,1,0:T(8,128)(2,1)}, bf16[6,128,512]{2,1,0:T(8,128)(2,1)}, u32[]{:S(2)}, u32[]{:S(2)}) collective-permute-start(bf16[6,128,512]{2,1,0:T(8,128)(2,1)} %head.2), channel_id=1, source_target_pairs={{0,4},{4,8},{8,12},{13,9},{9,5},{5,1},{2,6},{6,10},{10,14},{15,11}... | collective-permute-start | bytes 2359304 | tf_op jit(solution)/shard_map/ppermute | solution.py:615
  17.0 13.8 %collective-permute-start.6 = (bf16[6,128,512]{2,1,0:T(8,128)(2,1)}, bf16[6,128,512]{2,1,0:T(8,128)(2,1)}, u32[]{:S(2)}, u32[]{:S(2)}) collective-permute-start(bf16[6,128,512]{2,1,0:T(8,128)(2,1)} %collective-permute-done.4.first), channel_id=1, source_target_pairs={{4,5},{9,8},{12,13},{1,0},{6,7},{11,10},{14,15},{3,2},{20,21},{25,... | collective-permute-start | bytes 2359304 | tf_op jit(solution)/shard_map/ppermute | solution.py:619
  18.2 12.5 %collective-permute-start.5 = (bf16[6,128,512]{2,1,0:T(8,128)(2,1)}, bf16[6,128,512]{2,1,0:T(8,128)(2,1)}, u32[]{:S(2)}, u32[]{:S(2)}) collective-permute-start(bf16[6,128,512]{2,1,0:T(8,128)(2,1)} %collective-permute-done.4.first), channel_id=1, source_target_pairs={{4,8},{9,5},{6,10},{11,7},{20,24},{25,21},{22,26},{27,23}} | collective-permute-start | bytes 2359304 | tf_op jit(solution)/shard_map/ppermute | solution.py:615
  25.4 15.8 %collective-permute-start.2 = (bf16[6,128,512]{2,1,0:T(8,128)(2,1)}, bf16[6,128,512]{2,1,0:T(8,128)(2,1)}, u32[]{:S(2)}, u32[]{:S(2)}) collective-permute-start(bf16[6,128,512]{2,1,0:T(8,128)(2,1)} %collective-permute-done.first), channel_id=1, source_target_pairs={{4,5},{9,8},{12,13},{1,0},{6,7},{11,10},{14,15},{3,2},{20,21},{25,... | collective-permute-start | bytes 2359304 | tf_op jit(solution)/shard_map/ppermute | solution.py:619
  26.7 14.5 %collective-permute-start.1 = (bf16[6,128,512]{2,1,0:T(8,128)(2,1)}, bf16[6,128,512]{2,1,0:T(8,128)(2,1)}, u32[]{:S(2)}, u32[]{:S(2)}) collective-permute-start(bf16[6,128,512]{2,1,0:T(8,128)(2,1)} %collective-permute-done.first), channel_id=1, source_target_pairs={{4,8},{9,5},{6,10},{11,7},{20,24},{25,21},{22,26},{27,23}} | collective-permute-start | bytes 2359304 | tf_op jit(solution)/shard_map/ppermute | solution.py:615
  30.8 0.6 copy-start.7
  33.1 9.8 %copy-start.3 = (bf16[6,128,512]{2,1,0:T(8,128)(2,1)}, bf16[6,128,512]{2,1,0:T(8,128)(2,1)S(1)}, u32[]{:S(2)}) copy-start(bf16[6,128,512]{2,1,0:T(8,128)(2,1)S(1)} %get-tuple-element.19.refs_13_) | copy-start | bytes 2359300
  33.1 18.4 %collective-permute-start.10 = (bf16[6,128,512]{2,1,0:T(8,128)(2,1)}, bf16[6,128,512]{2,1,0:T(8,128)(2,1)}, u32[]{:S(2)}, u32[]{:S(2)}) collective-permute-start(bf16[6,128,512]{2,1,0:T(8,128)(2,1)} %get-tuple-element.22), channel_id=1, source_target_pairs={{0,4},{4,8},{8,12},{13,9},{9,5},{5,1},{2,6},{6,10},{10,14},{15,11}... | collective-permute-start | bytes 2359304 | tf_op jit(solution)/shard_map/ppermute | solution.py:615
  42.9 0.9 copy-start.5
  42.9 42.3 %copy-start.8 = (s32[232]{0:T(256)S(1)}, s32[232]{0:T(256)}, u32[]{:S(2)}) copy-start(s32[232]{0:T(256)} %tables.1.table) | copy-start | bytes 2788
  43.8 41.4 %copy-start.4 = (bf16[6,128,512]{2,1,0:T(8,128)(2,1)S(1)}, bf16[6,128,512]{2,1,0:T(8,128)(2,1)}, u32[]{:S(2)}) copy-start(bf16[6,128,512]{2,1,0:T(8,128)(2,1)} %copy-done.3) | copy-start | bytes 2359300
  43.8 15.9 %collective-permute-start.3 = (bf16[6,128,512]{2,1,0:T(8,128)(2,1)}, bf16[6,128,512]{2,1,0:T(8,128)(2,1)S(1)}, u32[]{:S(2)}, u32[]{:S(2)}) collective-permute-start(bf16[6,128,512]{2,1,0:T(8,128)(2,1)} %get-tuple-element.18), channel_id=1, source_target_pairs={{0,4},{4,8},{8,12},{13,9},{9,5},{5,1},{2,6},{6,10},{10,14},{15,11}... | collective-permute-start | bytes 2359304 | tf_op jit(solution)/shard_map/ppermute | solution.py:615
  49.9 35.3 %copy-start.2 = (bf16[4,512,512]{2,1,0:T(8,128)(2,1)S(1)}, bf16[4,512,512]{2,1,0:T(8,128)(2,1)}, u32[]{:S(2)}) copy-start(bf16[4,512,512]{2,1,0:T(8,128)(2,1)} %refs_2_.1) | copy-start | bytes 6291460
  49.9 35.2 %copy-start.6 = (bf16[6,128,512]{2,1,0:T(8,128)(2,1)S(1)}, bf16[6,128,512]{2,1,0:T(8,128)(2,1)}, u32[]{:S(2)}) copy-start(bf16[6,128,512]{2,1,0:T(8,128)(2,1)} %copy-done.5) | copy-start | bytes 2359300
  49.9 11.1 %collective-permute-start.7 = (bf16[6,128,512]{2,1,0:T(8,128)(2,1)}, bf16[6,128,512]{2,1,0:T(8,128)(2,1)S(1)}, u32[]{:S(2)}, u32[]{:S(2)}) collective-permute-start(bf16[6,128,512]{2,1,0:T(8,128)(2,1)} %copy-done.3), channel_id=1, source_target_pairs={{8,9},{5,4},{10,11},{7,6},{24,25},{21,20},{26,27},{23,22}} | collective-permute-start | bytes 2359304 | tf_op jit(solution)/shard_map/ppermute | solution.py:619
  50.8 10.3 %collective-permute-start.8 = (bf16[6,128,512]{2,1,0:T(8,128)(2,1)}, bf16[6,128,512]{2,1,0:T(8,128)(2,1)S(1)}, u32[]{:S(2)}, u32[]{:S(2)}) collective-permute-start(bf16[6,128,512]{2,1,0:T(8,128)(2,1)} %copy-done.5), channel_id=1, source_target_pairs={{8,9},{5,4},{10,11},{7,6},{24,25},{21,20},{26,27},{23,22}} | collective-permute-start | bytes 2359304 | tf_op jit(solution)/shard_map/ppermute | solution.py:619
  52.7 13.3 %collective-permute-start.15 = (bf16[6,128,512]{2,1,0:T(8,128)(2,1)S(1)}, bf16[6,128,512]{2,1,0:T(8,128)(2,1)S(1)}, u32[]{:S(2)}, u32[]{:S(2)}) collective-permute-start(bf16[6,128,512]{2,1,0:T(8,128)(2,1)S(1)} %broadcast_select_fusion.1), channel_id=1, source_target_pairs={{8,11},{10,9},{5,6},{7,4},{12,15},{14,13},{1,2},{3,0},{24,27},{26,... | collective-permute-start | bytes 2359304 | tf_op jit(solution)/shard_map/ppermute | solution.py:624
  54.0 13.3 %collective-permute-start.13 = (bf16[6,128,512]{2,1,0:T(8,128)(2,1)}, bf16[6,128,512]{2,1,0:T(8,128)(2,1)S(1)}, u32[]{:S(2)}, u32[]{:S(2)}) collective-permute-start(bf16[6,128,512]{2,1,0:T(8,128)(2,1)} %collective-permute-done.10.refs_15_), channel_id=1, source_target_pairs={{4,8},{8,12},{9,5},{5,1},{6,10},{10,14},{11,7},{7,3},{20,24},{24,2... | collective-permute-start | bytes 2359304 | tf_op jit(solution)/shard_map/ppermute | solution.py:615
  59.7 15.4 %collective-permute-start.18 = (bf16[6,128,512]{2,1,0:T(8,128)(2,1)S(1)}, bf16[6,128,512]{2,1,0:T(8,128)(2,1)S(1)}, u32[]{:S(2)}, u32[]{:S(2)}) collective-permute-start(bf16[6,128,512]{2,1,0:T(8,128)(2,1)S(1)} %broadcast_select_fusion), channel_id=1, source_target_pairs={{8,11},{10,9},{5,6},{7,4},{12,15},{14,13},{1,2},{3,0},{24,27},{26,... | collective-permute-start | bytes 2359304 | tf_op jit(solution)/shard_map/ppermute | solution.py:624
  61.1 15.4 %collective-permute-start.9 = (bf16[6,128,512]{2,1,0:T(8,128)(2,1)S(1)}, bf16[6,128,512]{2,1,0:T(8,128)(2,1)S(1)}, u32[]{:S(2)}, u32[]{:S(2)}) collective-permute-start(bf16[6,128,512]{2,1,0:T(8,128)(2,1)S(1)} %collective-permute-done.3.refs_21_), channel_id=1, source_target_pairs={{4,8},{8,12},{9,5},{5,1},{6,10},{10,14},{11,7},{7,3},{20,24},{24,2... | collective-permute-start | bytes 2359304 | tf_op jit(solution)/shard_map/ppermute | solution.py:615
  61.8 21.5 %collective-permute-start.11 = (bf16[6,128,512]{2,1,0:T(8,128)(2,1)}, bf16[6,128,512]{2,1,0:T(8,128)(2,1)S(1)}, u32[]{:S(2)}, u32[]{:S(2)}) collective-permute-start(bf16[6,128,512]{2,1,0:T(8,128)(2,1)} %collective-permute-done.10.refs_15_), channel_id=1, source_target_pairs={{4,5},{9,8},{8,9},{5,4},{12,13},{1,0},{6,7},{11,10},{10,11},{7,6},... | collective-permute-start | bytes 2359304 | tf_op jit(solution)/shard_map/ppermute | solution.py:619
  66.1 18.0 %collective-permute-start.12 = (bf16[6,128,512]{2,1,0:T(8,128)(2,1)S(1)}, bf16[6,128,512]{2,1,0:T(8,128)(2,1)S(1)}, u32[]{:S(2)}, u32[]{:S(2)}) collective-permute-start(bf16[6,128,512]{2,1,0:T(8,128)(2,1)S(1)} %collective-permute-done.3.refs_21_), channel_id=1, source_target_pairs={{4,5},{9,8},{8,9},{5,4},{12,13},{1,0},{6,7},{11,10},{10,11},{7,6},... | collective-permute-start | bytes 2359304 | tf_op jit(solution)/shard_map/ppermute | solution.py:619
  67.4 16.7 %collective-permute-start.16 = (bf16[6,128,512]{2,1,0:T(8,128)(2,1)S(1)}, bf16[6,128,512]{2,1,0:T(8,128)(2,1)S(1)}, u32[]{:S(2)}, u32[]{:S(2)}) collective-permute-start(bf16[6,128,512]{2,1,0:T(8,128)(2,1)S(1)} %collective-permute-done.15.refs_17_), channel_id=1, source_target_pairs={{0,1},{13,12},{4,5},{9,8},{2,3},{15,14},{6,7},{11,10},{16,17},{29,... | collective-permute-start | bytes 2359304 | tf_op jit(solution)/shard_map/ppermute | solution.py:619
  75.2 8.9 %collective-permute-start.14 = (bf16[6,128,512]{2,1,0:T(8,128)(2,1)S(1)}, bf16[6,128,512]{2,1,0:T(8,128)(2,1)S(1)}, u32[]{:S(2)}, u32[]{:S(2)}) collective-permute-start(bf16[6,128,512]{2,1,0:T(8,128)(2,1)S(1)} %collective-permute-done.13), channel_id=1, source_target_pairs={{8,9},{5,4},{12,13},{1,0},{10,11},{7,6},{14,15},{3,2},{24,25},{21,... | collective-permute-start | bytes 2359304 | tf_op jit(solution)/shard_map/ppermute | solution.py:619
  76.5 8.7 %collective-permute-start.19 = (bf16[6,128,512]{2,1,0:T(8,128)(2,1)S(1)}, bf16[6,128,512]{2,1,0:T(8,128)(2,1)S(1)}, u32[]{:S(2)}, u32[]{:S(2)}) collective-permute-start(bf16[6,128,512]{2,1,0:T(8,128)(2,1)S(1)} %collective-permute-done.18.refs_23_), channel_id=1, source_target_pairs={{0,1},{13,12},{4,5},{9,8},{2,3},{15,14},{6,7},{11,10},{16,17},{29,... | collective-permute-start | bytes 2359304 | tf_op jit(solution)/shard_map/ppermute | solution.py:619
  83.3 13.5 %collective-permute-start.22 = (bf16[6,128,512]{2,1,0:T(8,128)(2,1)S(1)}, bf16[6,128,512]{2,1,0:T(8,128)(2,1)S(1)}, u32[]{:S(2)}, u32[]{:S(2)}) collective-permute-start(bf16[6,128,512]{2,1,0:T(8,128)(2,1)S(1)} %collective-permute-done.13), channel_id=1, source_target_pairs={{8,12},{5,1},{10,14},{7,3},{24,28},{21,17},{26,30},{23,19}} | collective-permute-start | bytes 2359304 | tf_op jit(solution)/shard_map/ppermute | solution.py:615
  84.1 15.3 %collective-permute-start.17 = (bf16[6,128,512]{2,1,0:T(8,128)(2,1)S(1)}, bf16[6,128,512]{2,1,0:T(8,128)(2,1)S(1)}, u32[]{:S(2)}, u32[]{:S(2)}) collective-permute-start(bf16[6,128,512]{2,1,0:T(8,128)(2,1)S(1)} %collective-permute-done.9), channel_id=1, source_target_pairs={{8,12},{5,1},{10,14},{7,3},{24,28},{21,17},{26,30},{23,19}} | collective-permute-start | bytes 2359304 | tf_op jit(solution)/shard_map/ppermute | solution.py:615
  96.8 4.8 %collective-permute-start.23 = (bf16[6,128,512]{2,1,0:T(8,128)(2,1)S(1)}, bf16[6,128,512]{2,1,0:T(8,128)(2,1)S(1)}, u32[]{:S(2)}, u32[]{:S(2)}) collective-permute-start(bf16[6,128,512]{2,1,0:T(8,128)(2,1)S(1)} %collective-permute-done.22), channel_id=1, source_target_pairs={{12,13},{1,0},{14,15},{3,2},{28,29},{17,16},{30,31},{19,18}} | collective-permute-start | bytes 2359304 | tf_op jit(solution)/shard_map/ppermute | solution.py:619
  98.1 4.8 %collective-permute-start.21 = (bf16[6,128,512]{2,1,0:T(8,128)(2,1)S(1)}, bf16[6,128,512]{2,1,0:T(8,128)(2,1)S(1)}, u32[]{:S(2)}, u32[]{:S(2)}) collective-permute-start(bf16[6,128,512]{2,1,0:T(8,128)(2,1)S(1)} %collective-permute-done.9), channel_id=1, source_target_pairs={{8,9},{5,4},{12,13},{1,0},{10,11},{7,6},{14,15},{3,2},{24,25},{21,... | collective-permute-start | bytes 2359304 | tf_op jit(solution)/shard_map/ppermute | solution.py:619
  99.4 8.3 %collective-permute-start.20 = (bf16[6,128,512]{2,1,0:T(8,128)(2,1)S(1)}, bf16[6,128,512]{2,1,0:T(8,128)(2,1)S(1)}, u32[]{:S(2)}, u32[]{:S(2)}) collective-permute-start(bf16[6,128,512]{2,1,0:T(8,128)(2,1)S(1)} %collective-permute-done.17), channel_id=1, source_target_pairs={{12,13},{1,0},{14,15},{3,2},{28,29},{17,16},{30,31},{19,18}} | collective-permute-start | bytes 2359304 | tf_op jit(solution)/shard_map/ppermute | solution.py:619

commit v5 on v4

--- a/solution.py
+++ b/solution.py
@@ -643,10 +643,9 @@
     near = [hand(made[h], [2]) for h in both]
     got6 = [late(got4[0]), late(after(got4[1], *near))]
     swapped4 = [hand(got4[h], [1, 2, 3]) for h in both]
-    swapped6 = [hand(got6[0], [2, 3])]
     far = [across(jnp.where(spot == 2, made[h], got4[h])) for h in both]
     back = [hand(after(far[h], got6[0]), [0, 1]) for h in both]
-    got8 = [last(got6[0]), last(after(got6[1], *swapped4, swapped6[0], back[0]))]
+    got8 = [last(got6[0]), last(after(got6[1], *swapped4, back[0]))]
     pieces = [block[h] for h in both for block in (made, near, got4, swapped4, far, back)]
 
     parts = [(0, None, h, False, h * sec_dev // 2) for h in both]
@@ -663,13 +662,14 @@
     for h in both:
         hold(got0[h], swapped0[h], [0, 0, 0, 1], h)
         hold(got4[h], swapped4[h], [0, 1, 1, 0], h)
-    hold(got6[0], swapped6[0], [0, 0, 2, 2], 0)
-    parts.append((len(arrays), [0, 0, 2, 2], 1, False, 0))
-    arrays.append(blocks(got6[1]))
+    for h in both:
+        parts.append((len(arrays), [0, 0, 2, 2], h, False, 0))
+        arrays.append(blocks(got6[h]))
     out, env = grow(dims, table, parts, arrays, op_matrices, pieces)
-    swapped6.append(hand(after(got6[1], out), [2, 3]))
+    swapped6 = [hand(after(got6[h], out), [2, 3]) for h in both]
     swapped8 = [hand(after(got8[h], out), [3]) for h in both]
-    ends, owners = [blocks(swapped6[1])], [([0, 0, 2, 2], 1, True)]
+    ends = [blocks(block) for block in swapped6]
+    owners = [([0, 0, 2, 2], h, True) for h in both]
     for h in both:
         ends += [blocks(got8[h]), blocks(swapped8[h])]
         owners += [([0, 0, 0, 3], h, False), ([0, 0, 0, 3], h, True)]

time: 112 us -> 113 us (level); the launches traced: 110 us -> 112 us
  waiting for transfers between devices: 19.5 us -> 26.9 us
  starting transfers between devices: 58.6 us -> 53.2 us
    ppermute x12, waiting for transfers between devices: 2.62 us -> 10.1 us  [hand(): return lax.ppermute(block, ('sec', 'op'), pairs_of)]
    ppermute x12, starting transfers between devices: 26.5 us -> 21 us  [hand(): return lax.ppermute(block, ('sec', 'op'), pairs_of)]
    pallas_call x2, Pallas kernels: 7.17 us -> 9.47 us  [finish(): pl.pallas_call(functools.partial(finish_kernel, dims, ops_dev, parts), ou...]
    pallas_call x1, Pallas kernels: 11.6 us -> 9.44 us  [grow(): pl.pallas_call(functools.partial(grow_kernel, dims, ops_dev, parts, len(g...]
  transfers between devices with their start and end apart: 24 -> 24, of which waited for: 7 -> 8; matrix products, arithmetic and copies ran while one was open for 1% -> 1% of each run, Pallas kernels for 22% -> 22%
where the time goes in v5:
time: 113 us; the launch traced here: 112 us
  starting transfers between devices  53.2 us (47%)
  Pallas kernels  28.9 us (26%)
  waiting for transfers between devices  26.9 us (24%)
  local copies, waits for them, and re-layouts  1.52 us (1%)
  other arithmetic  1.32 us (1%)
    ppermute x10, starting transfers between devices, stream(): return lambda block: lax.ppermute(block, ('sec', 'op'), up + down)  29.6 us
    ppermute x12, starting transfers between devices, hand(): return lax.ppermute(block, ('sec', 'op'), pairs_of)  21 us
    ppermute x10, waiting for transfers between devices, stream(): return lambda block: lax.ppermute(block, ('sec', 'op'), up + down)  13.9 us
    ppermute x12, waiting for transfers between devices, hand(): return lax.ppermute(block, ('sec', 'op'), pairs_of)  10.1 us
    pallas_call x2, Pallas kernels, finish(): pl.pallas_call(functools.partial(finish_kernel, dims, ops_dev, parts), ou...  9.47 us
    pallas_call x1, Pallas kernels, grow(): pl.pallas_call(functools.partial(grow_kernel, dims, ops_dev, parts, len(g...  9.44 us
    pallas_call x2, Pallas kernels, head(): pl.pallas_call(functools.partial(head_kernel, h), out_shape=jax.ShapeDtyp...  4.2 us
    pallas_call x2, Pallas kernels, blend(): pl.pallas_call(functools.partial(blend_kernel, dims, which), out_shape=[b...  3.32 us
  transfers between devices with their start and end apart: 24, of which 8 were waited for; matrix products, arithmetic and copies ran while one was open for 1% of the time, Pallas kernels for 22%

profile of v5, /device:TPU:0, one launch (start us, length us, event | category | flops | bytes accessed | tf_op | source)
XLA Modules:
  0.0 112.3 jit_solution(11478821786271839815)
XLA Ops:
  0.0 2.2 %head.3 = bf16[6,128,512]{2,1,0:T(8,128)(2,1)} custom-call(bf16[6,256,512]{2,1,0:T(8,128)(2,1)} %env.7, bf16[2,6,128,512]{3,2,1,0:T(8,128)(2,1)} %bitcast.19), custom_call_target="tpu_custom_call" | custom-call | bytes 1572864 | tf_op jit(solution)/shard_map/head/pallas_call | solution.py:297
  2.2 5.8 %collective-permute-start.4 = (bf16[6,128,512]{2,1,0:T(8,128)(2,1)}, bf16[6,128,512]{2,1,0:T(8,128)(2,1)}, u32[]{:S(2)}, u32[]{:S(2)}) collective-permute-start(bf16[6,128,512]{2,1,0:T(8,128)(2,1)} %head.3), channel_id=1, source_target_pairs={{0,4},{4,8},{8,12},{13,9},{9,5},{5,1},{2,6},{6,10},{10,14},{15,11}... | collective-permute-start | bytes 2359304 | tf_op jit(solution)/shard_map/ppermute | solution.py:615
  8.0 2.0 %head.2 = bf16[6,128,512]{2,1,0:T(8,128)(2,1)} custom-call(bf16[6,256,512]{2,1,0:T(8,128)(2,1)} %env.7, bf16[2,6,128,512]{3,2,1,0:T(8,128)(2,1)} %bitcast.20), custom_call_target="tpu_custom_call" | custom-call | bytes 1572864 | tf_op jit(solution)/shard_map/head/pallas_call | solution.py:297
  10.1 3.5 %collective-permute-start = (bf16[6,128,512]{2,1,0:T(8,128)(2,1)}, bf16[6,128,512]{2,1,0:T(8,128)(2,1)}, u32[]{:S(2)}, u32[]{:S(2)}) collective-permute-start(bf16[6,128,512]{2,1,0:T(8,128)(2,1)} %head.2), channel_id=1, source_target_pairs={{0,4},{4,8},{8,12},{13,9},{9,5},{5,1},{2,6},{6,10},{10,14},{15,11}... | collective-permute-start | bytes 2359304 | tf_op jit(solution)/shard_map/ppermute | solution.py:615
  13.6 3.4 %collective-permute-done.4.first = bf16[6,128,512]{2,1,0:T(8,128)(2,1)} collective-permute-done((bf16[6,128,512]{2,1,0:T(8,128)(2,1)}, bf16[6,128,512]{2,1,0:T(8,128)(2,1)}, u32[]{:S(2)}, u32[]{:S(2)}) %collective-permute-start.4) | collective-permute-done | bytes 786464 | tf_op jit(solution)/shard_map/ppermute | solution.py:615
  17.0 1.3 %collective-permute-start.6 = (bf16[6,128,512]{2,1,0:T(8,128)(2,1)}, bf16[6,128,512]{2,1,0:T(8,128)(2,1)}, u32[]{:S(2)}, u32[]{:S(2)}) collective-permute-start(bf16[6,128,512]{2,1,0:T(8,128)(2,1)} %collective-permute-done.4.first), channel_id=1, source_target_pairs={{4,5},{9,8},{12,13},{1,0},{6,7},{11,10},{14,15},{3,2},{20,21},{25,... | collective-permute-start | bytes 2359304 | tf_op jit(solution)/shard_map/ppermute | solution.py:619
  18.2 1.6 %collective-permute-start.5 = (bf16[6,128,512]{2,1,0:T(8,128)(2,1)}, bf16[6,128,512]{2,1,0:T(8,128)(2,1)}, u32[]{:S(2)}, u32[]{:S(2)}) collective-permute-start(bf16[6,128,512]{2,1,0:T(8,128)(2,1)} %collective-permute-done.4.first), channel_id=1, source_target_pairs={{4,8},{9,5},{6,10},{11,7},{20,24},{25,21},{22,26},{27,23}} | collective-permute-start | bytes 2359304 | tf_op jit(solution)/shard_map/ppermute | solution.py:615
  19.8 5.6 %collective-permute-done.first = bf16[6,128,512]{2,1,0:T(8,128)(2,1)} collective-permute-done((bf16[6,128,512]{2,1,0:T(8,128)(2,1)}, bf16[6,128,512]{2,1,0:T(8,128)(2,1)}, u32[]{:S(2)}, u32[]{:S(2)}) %collective-permute-start) | collective-permute-done | bytes 786464 | tf_op jit(solution)/shard_map/ppermute | solution.py:615
  25.4 1.3 %collective-permute-start.2 = (bf16[6,128,512]{2,1,0:T(8,128)(2,1)}, bf16[6,128,512]{2,1,0:T(8,128)(2,1)}, u32[]{:S(2)}, u32[]{:S(2)}) collective-permute-start(bf16[6,128,512]{2,1,0:T(8,128)(2,1)} %collective-permute-done.first), channel_id=1, source_target_pairs={{4,5},{9,8},{12,13},{1,0},{6,7},{11,10},{14,15},{3,2},{20,21},{25,... | collective-permute-start | bytes 2359304 | tf_op jit(solution)/shard_map/ppermute | solution.py:619
  26.7 1.6 %collective-permute-start.1 = (bf16[6,128,512]{2,1,0:T(8,128)(2,1)}, bf16[6,128,512]{2,1,0:T(8,128)(2,1)}, u32[]{:S(2)}, u32[]{:S(2)}) collective-permute-start(bf16[6,128,512]{2,1,0:T(8,128)(2,1)} %collective-permute-done.first), channel_id=1, source_target_pairs={{4,8},{9,5},{6,10},{11,7},{20,24},{25,21},{22,26},{27,23}} | collective-permute-start | bytes 2359304 | tf_op jit(solution)/shard_map/ppermute | solution.py:615
  28.2 2.5 %tables.1.table = s32[232]{0:T(256)} custom-call(s32[8,24]{1,0:T(8,128)} %shift.1, s32[24]{0:T(128)} %slot.1, s32[3,24]{1,0:T(4,128)} %bitcast.36), custom_call_target="tpu_custom_call" | custom-call | flops 10000 | bytes 4000 | tf_op jit(solution)/shard_map/tables/pallas_call | solution.py:351
  30.7 0.0 collective-permute-done.6.other
  30.8 0.6 copy-done.7
  31.4 1.7 %blend.3 = (bf16[6,128,512]{2,1,0:T(8,128)(2,1)}, bf16[6,128,512]{2,1,0:T(8,128)(2,1)S(1)}) custom-call(s32[232]{0:T(256)S(1)} %copy-done.7, f32[3,24]{1,0:T(4,128)S(1)} %bitcast.34, bf16[6,128,512]{2,1,0:T(8,128)(2,1)} %collective-permute-done.5.second, bf16[6,128,512]{2,1,0:T(8,128)(2,1)} %collective-permute-done.4.first, ...), custom_call_target="tpu_custom_call" | custom-call | flops 4718592 | bytes 6291456 | tf_op jit(solution)/shard_map/blend/pallas_call | solution.py:412
  33.1 8.1 %collective-permute-start.10 = (bf16[6,128,512]{2,1,0:T(8,128)(2,1)}, bf16[6,128,512]{2,1,0:T(8,128)(2,1)}, u32[]{:S(2)}, u32[]{:S(2)}) collective-permute-start(bf16[6,128,512]{2,1,0:T(8,128)(2,1)} %get-tuple-element.23), channel_id=1, source_target_pairs={{0,4},{4,8},{8,12},{13,9},{9,5},{5,1},{2,6},{6,10},{10,14},{15,11}... | collective-permute-start | bytes 2359304 | tf_op jit(solution)/shard_map/ppermute | solution.py:615
  41.2 0.0 collective-permute-done.2.other
  41.2 0.0 collective-permute-done.1.second
  41.2 1.6 %blend.2 = (bf16[6,128,512]{2,1,0:T(8,128)(2,1)}, bf16[6,128,512]{2,1,0:T(8,128)(2,1)S(1)}) custom-call(s32[232]{0:T(256)S(1)} %copy-done.7, f32[3,24]{1,0:T(4,128)S(1)} %bitcast.35, bf16[6,128,512]{2,1,0:T(8,128)(2,1)} %collective-permute-done.1.second, bf16[6,128,512]{2,1,0:T(8,128)(2,1)} %collective-permute-done.first, ...), custom_call_target="tpu_custom_call" | custom-call | flops 4718592 | bytes 6291456 | tf_op jit(solution)/shard_map/blend/pallas_call | solution.py:412
  42.9 0.9 copy-done.5
  43.8 6.2 %collective-permute-start.3 = (bf16[6,128,512]{2,1,0:T(8,128)(2,1)}, bf16[6,128,512]{2,1,0:T(8,128)(2,1)S(1)}, u32[]{:S(2)}, u32[]{:S(2)}) collective-permute-start(bf16[6,128,512]{2,1,0:T(8,128)(2,1)} %get-tuple-element.19), channel_id=1, source_target_pairs={{0,4},{4,8},{8,12},{13,9},{9,5},{5,1},{2,6},{6,10},{10,14},{15,11}... | collective-permute-start | bytes 2359304 | tf_op jit(solution)/shard_map/ppermute | solution.py:615
  50.0 0.0 copy-start.2
  50.0 0.8 collective-permute-start.7
  50.8 0.7 collective-permute-start.8
  51.6 1.2 %broadcast_select_fusion.1 = bf16[6,128,512]{2,1,0:T(8,128)(2,1)S(1)} fusion(bf16[6,128,512]{2,1,0:T(8,128)(2,1)} %copy-done.3, bf16[6,128,512]{2,1,0:T(8,128)(2,1)} %collective-permute-done.10.refs_14_, pred[]{:T(512)S(6)} %eq.8), kind=kLoop, calls=%fused_computation.1 | loop fusion | flops 393216 | bytes 2359297 | tf_op jit(solution)/shard_map/jit(_where)/select_n | solution.py:646
  52.8 1.3 %collective-permute-start.13 = (bf16[6,128,512]{2,1,0:T(8,128)(2,1)S(1)}, bf16[6,128,512]{2,1,0:T(8,128)(2,1)S(1)}, u32[]{:S(2)}, u32[]{:S(2)}) collective-permute-start(bf16[6,128,512]{2,1,0:T(8,128)(2,1)S(1)} %broadcast_select_fusion.1), channel_id=1, source_target_pairs={{8,11},{10,9},{5,6},{7,4},{12,15},{14,13},{1,2},{3,0},{24,27},{26,... | collective-permute-start | bytes 2359304 | tf_op jit(solution)/shard_map/ppermute | solution.py:624
  54.1 0.7 collective-permute-start.14
  54.8 4.9 %collective-permute-done.3.refs_20_ = bf16[6,128,512]{2,1,0:T(8,128)(2,1)S(1)} collective-permute-done((bf16[6,128,512]{2,1,0:T(8,128)(2,1)}, bf16[6,128,512]{2,1,0:T(8,128)(2,1)S(1)}, u32[]{:S(2)}, u32[]{:S(2)}) %collective-permute-start.3) | collective-permute-done | bytes 786464 | tf_op jit(solution)/shard_map/ppermute | solution.py:615
  59.7 0.1 broadcast_select_fusion
  59.8 1.3 %collective-permute-start.17 = (bf16[6,128,512]{2,1,0:T(8,128)(2,1)S(1)}, bf16[6,128,512]{2,1,0:T(8,128)(2,1)S(1)}, u32[]{:S(2)}, u32[]{:S(2)}) collective-permute-start(bf16[6,128,512]{2,1,0:T(8,128)(2,1)S(1)} %broadcast_select_fusion), channel_id=1, source_target_pairs={{8,11},{10,9},{5,6},{7,4},{12,15},{14,13},{1,2},{3,0},{24,27},{26,... | collective-permute-start | bytes 2359304 | tf_op jit(solution)/shard_map/ppermute | solution.py:624
  61.1 0.7 collective-permute-start.9
  61.8 1.3 %collective-permute-start.11 = (bf16[6,128,512]{2,1,0:T(8,128)(2,1)}, bf16[6,128,512]{2,1,0:T(8,128)(2,1)S(1)}, u32[]{:S(2)}, u32[]{:S(2)}) collective-permute-start(bf16[6,128,512]{2,1,0:T(8,128)(2,1)} %collective-permute-done.10.refs_14_), channel_id=1, source_target_pairs={{4,5},{9,8},{8,9},{5,4},{12,13},{1,0},{6,7},{11,10},{10,11},{7,6},... | collective-permute-start | bytes 2359304 | tf_op jit(solution)/shard_map/ppermute | solution.py:619
  63.1 3.0 %collective-permute-done.13.refs_16_ = bf16[6,128,512]{2,1,0:T(8,128)(2,1)S(1)} collective-permute-done((bf16[6,128,512]{2,1,0:T(8,128)(2,1)S(1)}, bf16[6,128,512]{2,1,0:T(8,128)(2,1)S(1)}, u32[]{:S(2)}, u32[]{:S(2)}) %collective-permute-start.13) | collective-permute-done | bytes 786464 | tf_op jit(solution)/shard_map/ppermute | solution.py:624
  66.1 1.3 %collective-permute-start.12 = (bf16[6,128,512]{2,1,0:T(8,128)(2,1)S(1)}, bf16[6,128,512]{2,1,0:T(8,128)(2,1)S(1)}, u32[]{:S(2)}, u32[]{:S(2)}) collective-permute-start(bf16[6,128,512]{2,1,0:T(8,128)(2,1)S(1)} %collective-permute-done.3.refs_20_), channel_id=1, source_target_pairs={{4,5},{9,8},{8,9},{5,4},{12,13},{1,0},{6,7},{11,10},{10,11},{7,6},... | collective-permute-start | bytes 2359304 | tf_op jit(solution)/shard_map/ppermute | solution.py:619
  67.4 7.8 %collective-permute-start.15 = (bf16[6,128,512]{2,1,0:T(8,128)(2,1)S(1)}, bf16[6,128,512]{2,1,0:T(8,128)(2,1)S(1)}, u32[]{:S(2)}, u32[]{:S(2)}) collective-permute-start(bf16[6,128,512]{2,1,0:T(8,128)(2,1)S(1)} %collective-permute-done.13.refs_16_), channel_id=1, source_target_pairs={{0,1},{13,12},{4,5},{9,8},{2,3},{15,14},{6,7},{11,10},{16,17},{29,... | collective-permute-start | bytes 2359304 | tf_op jit(solution)/shard_map/ppermute | solution.py:619
  75.2 1.3 %collective-permute-start.18 = (bf16[6,128,512]{2,1,0:T(8,128)(2,1)S(1)}, bf16[6,128,512]{2,1,0:T(8,128)(2,1)S(1)}, u32[]{:S(2)}, u32[]{:S(2)}) collective-permute-start(bf16[6,128,512]{2,1,0:T(8,128)(2,1)S(1)} %collective-permute-done.17.refs_22_), channel_id=1, source_target_pairs={{0,1},{13,12},{4,5},{9,8},{2,3},{15,14},{6,7},{11,10},{16,17},{29,... | collective-permute-start | bytes 2359304 | tf_op jit(solution)/shard_map/ppermute | solution.py:619
  76.6 0.7 collective-permute-start.22
  77.4 0.7 collective-permute-start.16
  78.1 0.4 collective-permute-done.18.refs_23_
  78.5 9.4 %grow.1 = (bf16[4,6,256,512]{3,2,1,0:T(8,128)(2,1)}, bf16[6,512,512]{2,1,0:T(8,128)(2,1)S(1)}) custom-call(s32[232]{0:T(256)S(1)} %copy-done.8, bf16[6,256,512]{2,1,0:T(8,128)(2,1)S(1)} %copy-done, bf16[3,256,512]{2,1,0:T(8,128)(2,1)} %bitcast.4.refs_1_, bf16[3,256,512]{2,1,0:T(8,128)(2,1)} %bitcast.5.refs_2_, bf16[3,256,512]{2,1,0:T(8,128)(2,1)} %bitcast.6.refs_3_, ...), custom_call_target="tpu_custom_call" | custom-call | flops 1048576 | bytes 4096 | tf_op jit(solution)/shard_map/grow/pallas_call | solution.py:518
  87.9 1.3 %collective-permute-start.23 = (bf16[6,128,512]{2,1,0:T(8,128)(2,1)S(1)}, bf16[6,128,512]{2,1,0:T(8,128)(2,1)S(1)}, u32[]{:S(2)}, u32[]{:S(2)}) collective-permute-start(bf16[6,128,512]{2,1,0:T(8,128)(2,1)S(1)} %collective-permute-done.22), channel_id=1, source_target_pairs={{12,13},{1,0},{14,15},{3,2},{28,29},{17,16},{30,31},{19,18}} | collective-permute-start | bytes 2359304 | tf_op jit(solution)/shard_map/ppermute | solution.py:619
  89.2 1.3 %collective-permute-start.21 = (bf16[6,128,512]{2,1,0:T(8,128)(2,1)S(1)}, bf16[6,128,512]{2,1,0:T(8,128)(2,1)S(1)}, u32[]{:S(2)}, u32[]{:S(2)}) collective-permute-start(bf16[6,128,512]{2,1,0:T(8,128)(2,1)S(1)} %collective-permute-done.9), channel_id=1, source_target_pairs={{8,9},{5,4},{12,13},{1,0},{10,11},{7,6},{14,15},{3,2},{24,25},{21,... | collective-permute-start | bytes 2359304 | tf_op jit(solution)/shard_map/ppermute | solution.py:619
  90.5 1.3 %collective-permute-start.20 = (bf16[6,128,512]{2,1,0:T(8,128)(2,1)S(1)}, bf16[6,128,512]{2,1,0:T(8,128)(2,1)S(1)}, u32[]{:S(2)}, u32[]{:S(2)}) collective-permute-start(bf16[6,128,512]{2,1,0:T(8,128)(2,1)S(1)} %collective-permute-done.14), channel_id=1, source_target_pairs={{8,9},{5,4},{12,13},{1,0},{10,11},{7,6},{14,15},{3,2},{24,25},{21,... | collective-permute-start | bytes 2359304 | tf_op jit(solution)/shard_map/ppermute | solution.py:619
  91.8 1.3 %collective-permute-start.19 = (bf16[6,128,512]{2,1,0:T(8,128)(2,1)S(1)}, bf16[6,128,512]{2,1,0:T(8,128)(2,1)S(1)}, u32[]{:S(2)}, u32[]{:S(2)}) collective-permute-start(bf16[6,128,512]{2,1,0:T(8,128)(2,1)S(1)} %collective-permute-done.16), channel_id=1, source_target_pairs={{12,13},{1,0},{14,15},{3,2},{28,29},{17,16},{30,31},{19,18}} | collective-permute-start | bytes 2359304 | tf_op jit(solution)/shard_map/ppermute | solution.py:619
  93.1 7.0 %collective-permute-done.23 = bf16[6,128,512]{2,1,0:T(8,128)(2,1)S(1)} collective-permute-done((bf16[6,128,512]{2,1,0:T(8,128)(2,1)S(1)}, bf16[6,128,512]{2,1,0:T(8,128)(2,1)S(1)}, u32[]{:S(2)}, u32[]{:S(2)}) %collective-permute-start.23) | collective-permute-done | bytes 786464 | tf_op jit(solution)/shard_map/ppermute | solution.py:619
  100.1 1.3 %collective-permute-done.21 = bf16[6,128,512]{2,1,0:T(8,128)(2,1)S(1)} collective-permute-done((bf16[6,128,512]{2,1,0:T(8,128)(2,1)S(1)}, bf16[6,128,512]{2,1,0:T(8,128)(2,1)S(1)}, u32[]{:S(2)}, u32[]{:S(2)}) %collective-permute-start.21) | collective-permute-done | bytes 786464 | tf_op jit(solution)/shard_map/ppermute | solution.py:619
  101.5 1.3 %collective-permute-done.20 = bf16[6,128,512]{2,1,0:T(8,128)(2,1)S(1)} collective-permute-done((bf16[6,128,512]{2,1,0:T(8,128)(2,1)S(1)}, bf16[6,128,512]{2,1,0:T(8,128)(2,1)S(1)}, u32[]{:S(2)}, u32[]{:S(2)}) %collective-permute-start.20) | collective-permute-done | bytes 786464 | tf_op jit(solution)/shard_map/ppermute | solution.py:619
  102.8 7.0 %finish.2.refs_4_ = bf16[4,6,256,512]{3,2,1,0:T(8,128)(2,1)} custom-call(s32[232]{0:T(256)S(1)} %copy-done.8, bf16[3,256,512]{2,1,0:T(8,128)(2,1)S(1)} %bitcast.33, bf16[3,256,512]{2,1,0:T(8,128)(2,1)S(1)} %bitcast.32, bf16[3,256,512]{2,1,0:T(8,128)(2,1)S(1)} %bitcast.30, bf16[3,256,512]{2,1,0:T(8,128)(2,1)S(1)} %bitcast.31, ...), custom_call_target="tpu_custom_call", output_to_operand_aliasing={{}: (7, {})} | custom-call | flops 1048576 | bytes 4096 | tf_op jit(solution)/shard_map/finish/pallas_call | solution.py:587
  109.8 2.5 %finish.3 = bf16[4,6,256,512]{3,2,1,0:T(8,128)(2,1)} custom-call(s32[232]{0:T(256)S(1)} %copy-done.8, bf16[3,256,512]{2,1,0:T(8,128)(2,1)S(1)} %bitcast.26, bf16[3,256,512]{2,1,0:T(8,128)(2,1)S(1)} %bitcast.27, bf16[4,512,512]{2,1,0:T(8,128)(2,1)S(1)} %copy-done.2, ...), custom_call_target="tpu_custom_call", output_to_operand_aliasing={{}: (5, {})} | custom-call | flops 1048576 | bytes 4096 | tf_op jit(solution)/shard_map/finish/pallas_call | solution.py:587
  (30 shorter events, 0.1 us)
Async XLA Ops:
  0.0 30.8 %copy-start = (bf16[6,256,512]{2,1,0:T(8,128)(2,1)S(1)}, bf16[6,256,512]{2,1,0:T(8,128)(2,1)}, u32[]{:S(2)}) copy-start(bf16[6,256,512]{2,1,0:T(8,128)(2,1)} %refs_0_.1) | copy-start | bytes 4718596
  0.0 30.8 %copy-start.1 = (bf16[6,256,512]{2,1,0:T(8,128)(2,1)S(1)}, bf16[6,256,512]{2,1,0:T(8,128)(2,1)}, u32[]{:S(2)}) copy-start(bf16[6,256,512]{2,1,0:T(8,128)(2,1)} %env.7) | copy-start | bytes 4718596
  0.0 30.8 %copy-start.9 = (f32[24,3]{0,1:T(4,128)S(1)}, f32[24,3]{0,1:T(4,128)}, u32[]{:S(2)}) copy-start(f32[24,3]{0,1:T(4,128)} %param.13) | copy-start | bytes 868
  2.2 14.8 %collective-permute-start.4 = (bf16[6,128,512]{2,1,0:T(8,128)(2,1)}, bf16[6,128,512]{2,1,0:T(8,128)(2,1)}, u32[]{:S(2)}, u32[]{:S(2)}) collective-permute-start(bf16[6,128,512]{2,1,0:T(8,128)(2,1)} %head.3), channel_id=1, source_target_pairs={{0,4},{4,8},{8,12},{13,9},{9,5},{5,1},{2,6},{6,10},{10,14},{15,11}... | collective-permute-start | bytes 2359304 | tf_op jit(solution)/shard_map/ppermute | solution.py:615
  10.1 15.3 %collective-permute-start = (bf16[6,128,512]{2,1,0:T(8,128)(2,1)}, bf16[6,128,512]{2,1,0:T(8,128)(2,1)}, u32[]{:S(2)}, u32[]{:S(2)}) collective-permute-start(bf16[6,128,512]{2,1,0:T(8,128)(2,1)} %head.2), channel_id=1, source_target_pairs={{0,4},{4,8},{8,12},{13,9},{9,5},{5,1},{2,6},{6,10},{10,14},{15,11}... | collective-permute-start | bytes 2359304 | tf_op jit(solution)/shard_map/ppermute | solution.py:615
  17.0 13.8 %collective-permute-start.6 = (bf16[6,128,512]{2,1,0:T(8,128)(2,1)}, bf16[6,128,512]{2,1,0:T(8,128)(2,1)}, u32[]{:S(2)}, u32[]{:S(2)}) collective-permute-start(bf16[6,128,512]{2,1,0:T(8,128)(2,1)} %collective-permute-done.4.first), channel_id=1, source_target_pairs={{4,5},{9,8},{12,13},{1,0},{6,7},{11,10},{14,15},{3,2},{20,21},{25,... | collective-permute-start | bytes 2359304 | tf_op jit(solution)/shard_map/ppermute | solution.py:619
  18.2 12.5 %collective-permute-start.5 = (bf16[6,128,512]{2,1,0:T(8,128)(2,1)}, bf16[6,128,512]{2,1,0:T(8,128)(2,1)}, u32[]{:S(2)}, u32[]{:S(2)}) collective-permute-start(bf16[6,128,512]{2,1,0:T(8,128)(2,1)} %collective-permute-done.4.first), channel_id=1, source_target_pairs={{4,8},{9,5},{6,10},{11,7},{20,24},{25,21},{22,26},{27,23}} | collective-permute-start | bytes 2359304 | tf_op jit(solution)/shard_map/ppermute | solution.py:615
  25.4 15.8 %collective-permute-start.2 = (bf16[6,128,512]{2,1,0:T(8,128)(2,1)}, bf16[6,128,512]{2,1,0:T(8,128)(2,1)}, u32[]{:S(2)}, u32[]{:S(2)}) collective-permute-start(bf16[6,128,512]{2,1,0:T(8,128)(2,1)} %collective-permute-done.first), channel_id=1, source_target_pairs={{4,5},{9,8},{12,13},{1,0},{6,7},{11,10},{14,15},{3,2},{20,21},{25,... | collective-permute-start | bytes 2359304 | tf_op jit(solution)/shard_map/ppermute | solution.py:619
  26.7 14.5 %collective-permute-start.1 = (bf16[6,128,512]{2,1,0:T(8,128)(2,1)}, bf16[6,128,512]{2,1,0:T(8,128)(2,1)}, u32[]{:S(2)}, u32[]{:S(2)}) collective-permute-start(bf16[6,128,512]{2,1,0:T(8,128)(2,1)} %collective-permute-done.first), channel_id=1, source_target_pairs={{4,8},{9,5},{6,10},{11,7},{20,24},{25,21},{22,26},{27,23}} | collective-permute-start | bytes 2359304 | tf_op jit(solution)/shard_map/ppermute | solution.py:615
  30.8 0.6 copy-start.7
  33.1 9.8 %copy-start.3 = (bf16[6,128,512]{2,1,0:T(8,128)(2,1)}, bf16[6,128,512]{2,1,0:T(8,128)(2,1)S(1)}, u32[]{:S(2)}) copy-start(bf16[6,128,512]{2,1,0:T(8,128)(2,1)S(1)} %get-tuple-element.20.refs_12_) | copy-start | bytes 2359300
  33.1 18.5 %collective-permute-start.10 = (bf16[6,128,512]{2,1,0:T(8,128)(2,1)}, bf16[6,128,512]{2,1,0:T(8,128)(2,1)}, u32[]{:S(2)}, u32[]{:S(2)}) collective-permute-start(bf16[6,128,512]{2,1,0:T(8,128)(2,1)} %get-tuple-element.23), channel_id=1, source_target_pairs={{0,4},{4,8},{8,12},{13,9},{9,5},{5,1},{2,6},{6,10},{10,14},{15,11}... | collective-permute-start | bytes 2359304 | tf_op jit(solution)/shard_map/ppermute | solution.py:615
  42.9 0.9 copy-start.5
  42.9 35.6 %copy-start.8 = (s32[232]{0:T(256)S(1)}, s32[232]{0:T(256)}, u32[]{:S(2)}) copy-start(s32[232]{0:T(256)} %tables.1.table) | copy-start | bytes 2788
  43.8 34.7 %copy-start.4 = (bf16[6,128,512]{2,1,0:T(8,128)(2,1)S(1)}, bf16[6,128,512]{2,1,0:T(8,128)(2,1)}, u32[]{:S(2)}) copy-start(bf16[6,128,512]{2,1,0:T(8,128)(2,1)} %copy-done.3) | copy-start | bytes 2359300
  43.8 16.0 %collective-permute-start.3 = (bf16[6,128,512]{2,1,0:T(8,128)(2,1)}, bf16[6,128,512]{2,1,0:T(8,128)(2,1)S(1)}, u32[]{:S(2)}, u32[]{:S(2)}) collective-permute-start(bf16[6,128,512]{2,1,0:T(8,128)(2,1)} %get-tuple-element.19), channel_id=1, source_target_pairs={{0,4},{4,8},{8,12},{13,9},{9,5},{5,1},{2,6},{6,10},{10,14},{15,11}... | collective-permute-start | bytes 2359304 | tf_op jit(solution)/shard_map/ppermute | solution.py:615
  50.0 28.5 %copy-start.2 = (bf16[4,512,512]{2,1,0:T(8,128)(2,1)S(1)}, bf16[4,512,512]{2,1,0:T(8,128)(2,1)}, u32[]{:S(2)}) copy-start(bf16[4,512,512]{2,1,0:T(8,128)(2,1)} %refs_2_.1) | copy-start | bytes 6291460
  50.0 28.5 %copy-start.6 = (bf16[6,128,512]{2,1,0:T(8,128)(2,1)S(1)}, bf16[6,128,512]{2,1,0:T(8,128)(2,1)}, u32[]{:S(2)}) copy-start(bf16[6,128,512]{2,1,0:T(8,128)(2,1)} %copy-done.5) | copy-start | bytes 2359300
  50.0 11.1 %collective-permute-start.7 = (bf16[6,128,512]{2,1,0:T(8,128)(2,1)}, bf16[6,128,512]{2,1,0:T(8,128)(2,1)S(1)}, u32[]{:S(2)}, u32[]{:S(2)}) collective-permute-start(bf16[6,128,512]{2,1,0:T(8,128)(2,1)} %copy-done.3), channel_id=1, source_target_pairs={{8,9},{5,4},{10,11},{7,6},{24,25},{21,20},{26,27},{23,22}} | collective-permute-start | bytes 2359304 | tf_op jit(solution)/shard_map/ppermute | solution.py:619
  50.8 10.3 %collective-permute-start.8 = (bf16[6,128,512]{2,1,0:T(8,128)(2,1)}, bf16[6,128,512]{2,1,0:T(8,128)(2,1)S(1)}, u32[]{:S(2)}, u32[]{:S(2)}) collective-permute-start(bf16[6,128,512]{2,1,0:T(8,128)(2,1)} %copy-done.5), channel_id=1, source_target_pairs={{8,9},{5,4},{10,11},{7,6},{24,25},{21,20},{26,27},{23,22}} | collective-permute-start | bytes 2359304 | tf_op jit(solution)/shard_map/ppermute | solution.py:619
  52.8 13.3 %collective-permute-start.13 = (bf16[6,128,512]{2,1,0:T(8,128)(2,1)S(1)}, bf16[6,128,512]{2,1,0:T(8,128)(2,1)S(1)}, u32[]{:S(2)}, u32[]{:S(2)}) collective-permute-start(bf16[6,128,512]{2,1,0:T(8,128)(2,1)S(1)} %broadcast_select_fusion.1), channel_id=1, source_target_pairs={{8,11},{10,9},{5,6},{7,4},{12,15},{14,13},{1,2},{3,0},{24,27},{26,... | collective-permute-start | bytes 2359304 | tf_op jit(solution)/shard_map/ppermute | solution.py:624
  54.1 13.3 %collective-permute-start.14 = (bf16[6,128,512]{2,1,0:T(8,128)(2,1)}, bf16[6,128,512]{2,1,0:T(8,128)(2,1)S(1)}, u32[]{:S(2)}, u32[]{:S(2)}) collective-permute-start(bf16[6,128,512]{2,1,0:T(8,128)(2,1)} %collective-permute-done.10.refs_14_), channel_id=1, source_target_pairs={{4,8},{8,12},{9,5},{5,1},{6,10},{10,14},{11,7},{7,3},{20,24},{24,2... | collective-permute-start | bytes 2359304 | tf_op jit(solution)/shard_map/ppermute | solution.py:615
  59.8 15.4 %collective-permute-start.17 = (bf16[6,128,512]{2,1,0:T(8,128)(2,1)S(1)}, bf16[6,128,512]{2,1,0:T(8,128)(2,1)S(1)}, u32[]{:S(2)}, u32[]{:S(2)}) collective-permute-start(bf16[6,128,512]{2,1,0:T(8,128)(2,1)S(1)} %broadcast_select_fusion), channel_id=1, source_target_pairs={{8,11},{10,9},{5,6},{7,4},{12,15},{14,13},{1,2},{3,0},{24,27},{26,... | collective-permute-start | bytes 2359304 | tf_op jit(solution)/shard_map/ppermute | solution.py:624
  61.1 15.5 %collective-permute-start.9 = (bf16[6,128,512]{2,1,0:T(8,128)(2,1)S(1)}, bf16[6,128,512]{2,1,0:T(8,128)(2,1)S(1)}, u32[]{:S(2)}, u32[]{:S(2)}) collective-permute-start(bf16[6,128,512]{2,1,0:T(8,128)(2,1)S(1)} %collective-permute-done.3.refs_20_), channel_id=1, source_target_pairs={{4,8},{8,12},{9,5},{5,1},{6,10},{10,14},{11,7},{7,3},{20,24},{24,2... | collective-permute-start | bytes 2359304 | tf_op jit(solution)/shard_map/ppermute | solution.py:615
  61.8 15.5 %collective-permute-start.11 = (bf16[6,128,512]{2,1,0:T(8,128)(2,1)}, bf16[6,128,512]{2,1,0:T(8,128)(2,1)S(1)}, u32[]{:S(2)}, u32[]{:S(2)}) collective-permute-start(bf16[6,128,512]{2,1,0:T(8,128)(2,1)} %collective-permute-done.10.refs_14_), channel_id=1, source_target_pairs={{4,5},{9,8},{8,9},{5,4},{12,13},{1,0},{6,7},{11,10},{10,11},{7,6},... | collective-permute-start | bytes 2359304 | tf_op jit(solution)/shard_map/ppermute | solution.py:619
  66.1 11.2 %collective-permute-start.12 = (bf16[6,128,512]{2,1,0:T(8,128)(2,1)S(1)}, bf16[6,128,512]{2,1,0:T(8,128)(2,1)S(1)}, u32[]{:S(2)}, u32[]{:S(2)}) collective-permute-start(bf16[6,128,512]{2,1,0:T(8,128)(2,1)S(1)} %collective-permute-done.3.refs_20_), channel_id=1, source_target_pairs={{4,5},{9,8},{8,9},{5,4},{12,13},{1,0},{6,7},{11,10},{10,11},{7,6},... | collective-permute-start | bytes 2359304 | tf_op jit(solution)/shard_map/ppermute | solution.py:619
  67.4 9.9 %collective-permute-start.15 = (bf16[6,128,512]{2,1,0:T(8,128)(2,1)S(1)}, bf16[6,128,512]{2,1,0:T(8,128)(2,1)S(1)}, u32[]{:S(2)}, u32[]{:S(2)}) collective-permute-start(bf16[6,128,512]{2,1,0:T(8,128)(2,1)S(1)} %collective-permute-done.13.refs_16_), channel_id=1, source_target_pairs={{0,1},{13,12},{4,5},{9,8},{2,3},{15,14},{6,7},{11,10},{16,17},{29,... | collective-permute-start | bytes 2359304 | tf_op jit(solution)/shard_map/ppermute | solution.py:619
  75.2 3.2 %collective-permute-start.18 = (bf16[6,128,512]{2,1,0:T(8,128)(2,1)S(1)}, bf16[6,128,512]{2,1,0:T(8,128)(2,1)S(1)}, u32[]{:S(2)}, u32[]{:S(2)}) collective-permute-start(bf16[6,128,512]{2,1,0:T(8,128)(2,1)S(1)} %collective-permute-done.17.refs_22_), channel_id=1, source_target_pairs={{0,1},{13,12},{4,5},{9,8},{2,3},{15,14},{6,7},{11,10},{16,17},{29,... | collective-permute-start | bytes 2359304 | tf_op jit(solution)/shard_map/ppermute | solution.py:619
  76.6 11.3 %collective-permute-start.22 = (bf16[6,128,512]{2,1,0:T(8,128)(2,1)S(1)}, bf16[6,128,512]{2,1,0:T(8,128)(2,1)S(1)}, u32[]{:S(2)}, u32[]{:S(2)}) collective-permute-start(bf16[6,128,512]{2,1,0:T(8,128)(2,1)S(1)} %collective-permute-done.14), channel_id=1, source_target_pairs={{8,12},{5,1},{10,14},{7,3},{24,28},{21,17},{26,30},{23,19}} | collective-permute-start | bytes 2359304 | tf_op jit(solution)/shard_map/ppermute | solution.py:615
  77.4 14.5 %collective-permute-start.16 = (bf16[6,128,512]{2,1,0:T(8,128)(2,1)S(1)}, bf16[6,128,512]{2,1,0:T(8,128)(2,1)S(1)}, u32[]{:S(2)}, u32[]{:S(2)}) collective-permute-start(bf16[6,128,512]{2,1,0:T(8,128)(2,1)S(1)} %collective-permute-done.9), channel_id=1, source_target_pairs={{8,12},{5,1},{10,14},{7,3},{24,28},{21,17},{26,30},{23,19}} | collective-permute-start | bytes 2359304 | tf_op jit(solution)/shard_map/ppermute | solution.py:615
  87.9 12.2 %collective-permute-start.23 = (bf16[6,128,512]{2,1,0:T(8,128)(2,1)S(1)}, bf16[6,128,512]{2,1,0:T(8,128)(2,1)S(1)}, u32[]{:S(2)}, u32[]{:S(2)}) collective-permute-start(bf16[6,128,512]{2,1,0:T(8,128)(2,1)S(1)} %collective-permute-done.22), channel_id=1, source_target_pairs={{12,13},{1,0},{14,15},{3,2},{28,29},{17,16},{30,31},{19,18}} | collective-permute-start | bytes 2359304 | tf_op jit(solution)/shard_map/ppermute | solution.py:619
  89.2 12.3 %collective-permute-start.21 = (bf16[6,128,512]{2,1,0:T(8,128)(2,1)S(1)}, bf16[6,128,512]{2,1,0:T(8,128)(2,1)S(1)}, u32[]{:S(2)}, u32[]{:S(2)}) collective-permute-start(bf16[6,128,512]{2,1,0:T(8,128)(2,1)S(1)} %collective-permute-done.9), channel_id=1, source_target_pairs={{8,9},{5,4},{12,13},{1,0},{10,11},{7,6},{14,15},{3,2},{24,25},{21,... | collective-permute-start | bytes 2359304 | tf_op jit(solution)/shard_map/ppermute | solution.py:619
  90.5 12.3 %collective-permute-start.20 = (bf16[6,128,512]{2,1,0:T(8,128)(2,1)S(1)}, bf16[6,128,512]{2,1,0:T(8,128)(2,1)S(1)}, u32[]{:S(2)}, u32[]{:S(2)}) collective-permute-start(bf16[6,128,512]{2,1,0:T(8,128)(2,1)S(1)} %collective-permute-done.14), channel_id=1, source_target_pairs={{8,9},{5,4},{12,13},{1,0},{10,11},{7,6},{14,15},{3,2},{24,25},{21,... | collective-permute-start | bytes 2359304 | tf_op jit(solution)/shard_map/ppermute | solution.py:619
  91.8 18.0 %collective-permute-start.19 = (bf16[6,128,512]{2,1,0:T(8,128)(2,1)S(1)}, bf16[6,128,512]{2,1,0:T(8,128)(2,1)S(1)}, u32[]{:S(2)}, u32[]{:S(2)}) collective-permute-start(bf16[6,128,512]{2,1,0:T(8,128)(2,1)S(1)} %collective-permute-done.16), channel_id=1, source_target_pairs={{12,13},{1,0},{14,15},{3,2},{28,29},{17,16},{30,31},{19,18}} | collective-permute-start | bytes 2359304 | tf_op jit(solution)/shard_map/ppermute | solution.py:619

commit v6 on v4

--- a/solution.py
+++ b/solution.py
@@ -496,19 +496,37 @@
     def drain(side):
         pltpu.make_async_copy(result.at[side], result.at[side], out_sem.at[side]).wait()
 
-    def step(i, carry):
+    def grown_of(i):
+        o, local = found[1, i], found[2, i]
+        block = ground[found[0, i]]
+        product = jnp.dot(block, op_ref[o], preferred_element_type=jnp.float32).astype(BF16)
+        return jnp.dot(product, env[local], preferred_element_type=jnp.float32).astype(BF16)
+
+    def send(i):
         side = lax.rem(i, DEPTH)
-        o, local = found[1, i], found[2, i]
-        product = jnp.dot(ground[found[0, i]], op_ref[o], preferred_element_type=jnp.float32).astype(BF16)
-        grown = jnp.dot(product, env[local], preferred_element_type=jnp.float32).astype(BF16)
-        pl.when(i >= DEPTH)(lambda: drain(side))
-        result[side] = grown
-        pltpu.make_async_copy(result.at[side], out_ref.at[o, local], out_sem.at[side]).start()
+        target = out_ref.at[found[1, i], found[2, i]]
+        pltpu.make_async_copy(result.at[side], target, out_sem.at[side]).start()
+
+    def step(n, carry):
+        i, j = 2 * n, 2 * n + 1
+        values = grown_of(i), grown_of(jnp.minimum(j, total - 1))
+
+        @pl.when(n >= 2)
+        def _():
+            drain(lax.rem(i, DEPTH))
+            drain(lax.rem(j, DEPTH))
+
+        result[lax.rem(i, DEPTH)] = values[0]
+        result[lax.rem(j, DEPTH)] = values[1]
+        send(i)
+        pl.when(j < total)(lambda: send(j))
         return carry
 
-    lax.fori_loop(0, total, step, 0)
+    steps = (total + 1) // 2
+    lax.fori_loop(0, steps, step, 0)
+    left = total - 2 * jnp.maximum(steps - 2, 0)
     for back in range(1, DEPTH + 1):
-        pl.when(total >= back)(lambda back=back: drain(lax.rem(total - back, DEPTH)))
+        pl.when(left >= back)(lambda back=back: drain(lax.rem(total - back, DEPTH)))
 
 
 def grow(dims, table, parts, grounds, op_matrices, pieces):
@@ -563,22 +581,39 @@
     def drain(side):
         pltpu.make_async_copy(result.at[side], result.at[side], out_sem.at[side]).wait()
 
-    def step(i, carry):
-        side = lax.rem(i, DEPTH)
+    def grown_of(i):
         which, s, o, local = (found[k, i] for k in range(4))
         block = grounds[0][s]
         for n in range(1, len(parts)):
             block = jnp.where(which == n, grounds[n][s], block)
         product = jnp.dot(block, op_ref[o], preferred_element_type=jnp.float32).astype(BF16)
-        grown = jnp.dot(product, env[local], preferred_element_type=jnp.float32).astype(BF16)
-        pl.when(i >= DEPTH)(lambda: drain(side))
-        result[side] = grown
-        pltpu.make_async_copy(result.at[side], out_ref.at[o, local], out_sem.at[side]).start()
+        return jnp.dot(product, env[local], preferred_element_type=jnp.float32).astype(BF16)
+
+    def send(i):
+        side = lax.rem(i, DEPTH)
+        target = out_ref.at[found[2, i], found[3, i]]
+        pltpu.make_async_copy(result.at[side], target, out_sem.at[side]).start()
+
+    def step(n, carry):
+        i, j = 2 * n, 2 * n + 1
+        values = grown_of(i), grown_of(jnp.minimum(j, total - 1))
+
+        @pl.when(n >= 2)
+        def _():
+            drain(lax.rem(i, DEPTH))
+            drain(lax.rem(j, DEPTH))
+
+        result[lax.rem(i, DEPTH)] = values[0]
+        result[lax.rem(j, DEPTH)] = values[1]
+        send(i)
+        pl.when(j < total)(lambda: send(j))
         return carry
 
-    lax.fori_loop(0, total, step, 0)
+    steps = (total + 1) // 2
+    lax.fori_loop(0, steps, step, 0)
+    left = total - 2 * jnp.maximum(steps - 2, 0)
     for back in range(1, DEPTH + 1):
-        pl.when(total >= back)(lambda back=back: drain(lax.rem(total - back, DEPTH)))
+        pl.when(left >= back)(lambda back=back: drain(lax.rem(total - back, DEPTH)))
 
 
 def finish(dims, table, parts, grounds, op_matrices, env, out, cost):

time: 112 us -> 112 us (level)
    pallas_call x1, Pallas kernels: 11.6 us -> 9.49 us  [grow(): pl.pallas_call(functools.partial(grow_kernel, dims, ops_dev, parts, len(g...]
    pallas_call x2, Pallas kernels: 7.17 us -> 8.56 us  [finish(): pl.pallas_call(functools.partial(finish_kernel, dims, ops_dev, parts), ou...]
  transfers between devices with their start and end apart: 24 -> 24, of which waited for: 7 -> 7; matrix products, arithmetic and copies ran while one was open for 1% -> 1% of each run, Pallas kernels for 22% -> 21%
where the time goes in v6:
time: 112 us; the launch traced here: 110 us
  starting transfers between devices  58.4 us (52%)
  Pallas kernels  28.1 us (25%)
  waiting for transfers between devices  20.3 us (18%)
  local copies, waits for them, and re-layouts  1.52 us (1%)
  other arithmetic  1.32 us (1%)
    ppermute x10, starting transfers between devices, stream(): return lambda block: lax.ppermute(block, ('sec', 'op'), up + down)  29.3 us
    ppermute x12, starting transfers between devices, hand(): return lax.ppermute(block, ('sec', 'op'), pairs_of)  26.5 us
    ppermute x10, waiting for transfers between devices, stream(): return lambda block: lax.ppermute(block, ('sec', 'op'), up + down)  13.9 us
    pallas_call x1, Pallas kernels, grow(): pl.pallas_call(functools.partial(grow_kernel, dims, ops_dev, parts, len(g...  9.49 us
    pallas_call x2, Pallas kernels, finish(): pl.pallas_call(functools.partial(finish_kernel, dims, ops_dev, parts), ou...  8.56 us
    pallas_call x2, Pallas kernels, head(): pl.pallas_call(functools.partial(head_kernel, h), out_shape=jax.ShapeDtyp...  4.2 us
    ppermute x12, waiting for transfers between devices, hand(): return lax.ppermute(block, ('sec', 'op'), pairs_of)  3.41 us
    pallas_call x2, Pallas kernels, blend(): pl.pallas_call(functools.partial(blend_kernel, dims, which), out_shape=[b...  3.32 us
  transfers between devices with their start and end apart: 24, of which 7 were waited for; matrix products, arithmetic and copies ran while one was open for 1% of the time, Pallas kernels for 21%

profile of v6, /device:TPU:0, one launch (start us, length us, event | category | flops | bytes accessed | tf_op | source)
XLA Modules:
  0.0 110.0 jit_solution(14426844850638636177)
XLA Ops:
  0.0 2.2 %head.3 = bf16[6,128,512]{2,1,0:T(8,128)(2,1)} custom-call(bf16[6,256,512]{2,1,0:T(8,128)(2,1)} %env.7, bf16[2,6,128,512]{3,2,1,0:T(8,128)(2,1)} %bitcast.19), custom_call_target="tpu_custom_call" | custom-call | bytes 1572864 | tf_op jit(solution)/shard_map/head/pallas_call | solution.py:297
  2.2 5.8 %collective-permute-start.4 = (bf16[6,128,512]{2,1,0:T(8,128)(2,1)}, bf16[6,128,512]{2,1,0:T(8,128)(2,1)}, u32[]{:S(2)}, u32[]{:S(2)}) collective-permute-start(bf16[6,128,512]{2,1,0:T(8,128)(2,1)} %head.3), channel_id=1, source_target_pairs={{0,4},{4,8},{8,12},{13,9},{9,5},{5,1},{2,6},{6,10},{10,14},{15,11}... | collective-permute-start | bytes 2359304 | tf_op jit(solution)/shard_map/ppermute | solution.py:650
  8.0 2.0 %head.2 = bf16[6,128,512]{2,1,0:T(8,128)(2,1)} custom-call(bf16[6,256,512]{2,1,0:T(8,128)(2,1)} %env.7, bf16[2,6,128,512]{3,2,1,0:T(8,128)(2,1)} %bitcast.20), custom_call_target="tpu_custom_call" | custom-call | bytes 1572864 | tf_op jit(solution)/shard_map/head/pallas_call | solution.py:297
  10.1 3.5 %collective-permute-start = (bf16[6,128,512]{2,1,0:T(8,128)(2,1)}, bf16[6,128,512]{2,1,0:T(8,128)(2,1)}, u32[]{:S(2)}, u32[]{:S(2)}) collective-permute-start(bf16[6,128,512]{2,1,0:T(8,128)(2,1)} %head.2), channel_id=1, source_target_pairs={{0,4},{4,8},{8,12},{13,9},{9,5},{5,1},{2,6},{6,10},{10,14},{15,11}... | collective-permute-start | bytes 2359304 | tf_op jit(solution)/shard_map/ppermute | solution.py:650
  13.6 3.4 %collective-permute-done.4.first = bf16[6,128,512]{2,1,0:T(8,128)(2,1)} collective-permute-done((bf16[6,128,512]{2,1,0:T(8,128)(2,1)}, bf16[6,128,512]{2,1,0:T(8,128)(2,1)}, u32[]{:S(2)}, u32[]{:S(2)}) %collective-permute-start.4) | collective-permute-done | bytes 786464 | tf_op jit(solution)/shard_map/ppermute | solution.py:650
  17.0 1.3 %collective-permute-start.6 = (bf16[6,128,512]{2,1,0:T(8,128)(2,1)}, bf16[6,128,512]{2,1,0:T(8,128)(2,1)}, u32[]{:S(2)}, u32[]{:S(2)}) collective-permute-start(bf16[6,128,512]{2,1,0:T(8,128)(2,1)} %collective-permute-done.4.first), channel_id=1, source_target_pairs={{4,5},{9,8},{12,13},{1,0},{6,7},{11,10},{14,15},{3,2},{20,21},{25,... | collective-permute-start | bytes 2359304 | tf_op jit(solution)/shard_map/ppermute | solution.py:654
  18.2 1.6 %collective-permute-start.5 = (bf16[6,128,512]{2,1,0:T(8,128)(2,1)}, bf16[6,128,512]{2,1,0:T(8,128)(2,1)}, u32[]{:S(2)}, u32[]{:S(2)}) collective-permute-start(bf16[6,128,512]{2,1,0:T(8,128)(2,1)} %collective-permute-done.4.first), channel_id=1, source_target_pairs={{4,8},{9,5},{6,10},{11,7},{20,24},{25,21},{22,26},{27,23}} | collective-permute-start | bytes 2359304 | tf_op jit(solution)/shard_map/ppermute | solution.py:650
  19.8 5.6 %collective-permute-done.first = bf16[6,128,512]{2,1,0:T(8,128)(2,1)} collective-permute-done((bf16[6,128,512]{2,1,0:T(8,128)(2,1)}, bf16[6,128,512]{2,1,0:T(8,128)(2,1)}, u32[]{:S(2)}, u32[]{:S(2)}) %collective-permute-start) | collective-permute-done | bytes 786464 | tf_op jit(solution)/shard_map/ppermute | solution.py:650
  25.4 1.3 %collective-permute-start.2 = (bf16[6,128,512]{2,1,0:T(8,128)(2,1)}, bf16[6,128,512]{2,1,0:T(8,128)(2,1)}, u32[]{:S(2)}, u32[]{:S(2)}) collective-permute-start(bf16[6,128,512]{2,1,0:T(8,128)(2,1)} %collective-permute-done.first), channel_id=1, source_target_pairs={{4,5},{9,8},{12,13},{1,0},{6,7},{11,10},{14,15},{3,2},{20,21},{25,... | collective-permute-start | bytes 2359304 | tf_op jit(solution)/shard_map/ppermute | solution.py:654
  26.7 1.6 %collective-permute-start.1 = (bf16[6,128,512]{2,1,0:T(8,128)(2,1)}, bf16[6,128,512]{2,1,0:T(8,128)(2,1)}, u32[]{:S(2)}, u32[]{:S(2)}) collective-permute-start(bf16[6,128,512]{2,1,0:T(8,128)(2,1)} %collective-permute-done.first), channel_id=1, source_target_pairs={{4,8},{9,5},{6,10},{11,7},{20,24},{25,21},{22,26},{27,23}} | collective-permute-start | bytes 2359304 | tf_op jit(solution)/shard_map/ppermute | solution.py:650
  28.2 2.5 %tables.1.table = s32[232]{0:T(256)} custom-call(s32[8,24]{1,0:T(8,128)} %shift.1, s32[24]{0:T(128)} %slot.1, s32[3,24]{1,0:T(4,128)} %bitcast.36), custom_call_target="tpu_custom_call" | custom-call | flops 10000 | bytes 4000 | tf_op jit(solution)/shard_map/tables/pallas_call | solution.py:351
  30.7 0.0 collective-permute-done.6.other
  30.8 0.6 copy-done.7
  31.4 1.7 %blend.3 = (bf16[6,128,512]{2,1,0:T(8,128)(2,1)}, bf16[6,128,512]{2,1,0:T(8,128)(2,1)S(1)}) custom-call(s32[232]{0:T(256)S(1)} %copy-done.7, f32[3,24]{1,0:T(4,128)S(1)} %bitcast.34, bf16[6,128,512]{2,1,0:T(8,128)(2,1)} %collective-permute-done.5.second, bf16[6,128,512]{2,1,0:T(8,128)(2,1)} %collective-permute-done.4.first, ...), custom_call_target="tpu_custom_call" | custom-call | flops 4718592 | bytes 6291456 | tf_op jit(solution)/shard_map/blend/pallas_call | solution.py:412
  33.1 8.1 %collective-permute-start.10 = (bf16[6,128,512]{2,1,0:T(8,128)(2,1)}, bf16[6,128,512]{2,1,0:T(8,128)(2,1)}, u32[]{:S(2)}, u32[]{:S(2)}) collective-permute-start(bf16[6,128,512]{2,1,0:T(8,128)(2,1)} %get-tuple-element.22), channel_id=1, source_target_pairs={{0,4},{4,8},{8,12},{13,9},{9,5},{5,1},{2,6},{6,10},{10,14},{15,11}... | collective-permute-start | bytes 2359304 | tf_op jit(solution)/shard_map/ppermute | solution.py:650
  41.2 0.0 collective-permute-done.2.other
  41.2 0.0 collective-permute-done.1.second
  41.2 1.6 %blend.2 = (bf16[6,128,512]{2,1,0:T(8,128)(2,1)}, bf16[6,128,512]{2,1,0:T(8,128)(2,1)S(1)}) custom-call(s32[232]{0:T(256)S(1)} %copy-done.7, f32[3,24]{1,0:T(4,128)S(1)} %bitcast.35, bf16[6,128,512]{2,1,0:T(8,128)(2,1)} %collective-permute-done.1.second, bf16[6,128,512]{2,1,0:T(8,128)(2,1)} %collective-permute-done.first, ...), custom_call_target="tpu_custom_call" | custom-call | flops 4718592 | bytes 6291456 | tf_op jit(solution)/shard_map/blend/pallas_call | solution.py:412
  42.9 0.9 copy-done.5
  43.8 5.9 %collective-permute-start.3 = (bf16[6,128,512]{2,1,0:T(8,128)(2,1)}, bf16[6,128,512]{2,1,0:T(8,128)(2,1)S(1)}, u32[]{:S(2)}, u32[]{:S(2)}) collective-permute-start(bf16[6,128,512]{2,1,0:T(8,128)(2,1)} %get-tuple-element.18), channel_id=1, source_target_pairs={{0,4},{4,8},{8,12},{13,9},{9,5},{5,1},{2,6},{6,10},{10,14},{15,11}... | collective-permute-start | bytes 2359304 | tf_op jit(solution)/shard_map/ppermute | solution.py:650
  49.7 0.0 copy-start.2
  49.7 0.8 collective-permute-start.7
  50.6 0.7 collective-permute-start.8
  51.3 0.0 collective-permute-done.10.refs_15_
  51.3 1.2 %broadcast_select_fusion.1 = bf16[6,128,512]{2,1,0:T(8,128)(2,1)S(1)} fusion(bf16[6,128,512]{2,1,0:T(8,128)(2,1)} %copy-done.3, bf16[6,128,512]{2,1,0:T(8,128)(2,1)} %collective-permute-done.10.refs_15_, pred[]{:T(512)S(6)} %eq.8), kind=kLoop, calls=%fused_computation.1 | loop fusion | flops 393216 | bytes 2359297 | tf_op jit(solution)/shard_map/jit(_where)/select_n | solution.py:682
  52.6 1.3 %collective-permute-start.15 = (bf16[6,128,512]{2,1,0:T(8,128)(2,1)S(1)}, bf16[6,128,512]{2,1,0:T(8,128)(2,1)S(1)}, u32[]{:S(2)}, u32[]{:S(2)}) collective-permute-start(bf16[6,128,512]{2,1,0:T(8,128)(2,1)S(1)} %broadcast_select_fusion.1), channel_id=1, source_target_pairs={{8,11},{10,9},{5,6},{7,4},{12,15},{14,13},{1,2},{3,0},{24,27},{26,... | collective-permute-start | bytes 2359304 | tf_op jit(solution)/shard_map/ppermute | solution.py:659
  53.9 0.7 collective-permute-start.13
  54.6 4.9 %collective-permute-done.3.refs_21_ = bf16[6,128,512]{2,1,0:T(8,128)(2,1)S(1)} collective-permute-done((bf16[6,128,512]{2,1,0:T(8,128)(2,1)}, bf16[6,128,512]{2,1,0:T(8,128)(2,1)S(1)}, u32[]{:S(2)}, u32[]{:S(2)}) %collective-permute-start.3) | collective-permute-done | bytes 786464 | tf_op jit(solution)/shard_map/ppermute | solution.py:650
  59.5 0.1 broadcast_select_fusion
  59.6 1.3 %collective-permute-start.18 = (bf16[6,128,512]{2,1,0:T(8,128)(2,1)S(1)}, bf16[6,128,512]{2,1,0:T(8,128)(2,1)S(1)}, u32[]{:S(2)}, u32[]{:S(2)}) collective-permute-start(bf16[6,128,512]{2,1,0:T(8,128)(2,1)S(1)} %broadcast_select_fusion), channel_id=1, source_target_pairs={{8,11},{10,9},{5,6},{7,4},{12,15},{14,13},{1,2},{3,0},{24,27},{26,... | collective-permute-start | bytes 2359304 | tf_op jit(solution)/shard_map/ppermute | solution.py:659
  60.9 0.7 collective-permute-start.9
  61.6 1.3 %collective-permute-start.11 = (bf16[6,128,512]{2,1,0:T(8,128)(2,1)}, bf16[6,128,512]{2,1,0:T(8,128)(2,1)S(1)}, u32[]{:S(2)}, u32[]{:S(2)}) collective-permute-start(bf16[6,128,512]{2,1,0:T(8,128)(2,1)} %collective-permute-done.10.refs_15_), channel_id=1, source_target_pairs={{4,5},{9,8},{8,9},{5,4},{12,13},{1,0},{6,7},{11,10},{10,11},{7,6},... | collective-permute-start | bytes 2359304 | tf_op jit(solution)/shard_map/ppermute | solution.py:654
  62.9 3.0 %collective-permute-done.15.refs_17_ = bf16[6,128,512]{2,1,0:T(8,128)(2,1)S(1)} collective-permute-done((bf16[6,128,512]{2,1,0:T(8,128)(2,1)S(1)}, bf16[6,128,512]{2,1,0:T(8,128)(2,1)S(1)}, u32[]{:S(2)}, u32[]{:S(2)}) %collective-permute-start.15) | collective-permute-done | bytes 786464 | tf_op jit(solution)/shard_map/ppermute | solution.py:659
  65.9 1.3 %collective-permute-start.12 = (bf16[6,128,512]{2,1,0:T(8,128)(2,1)S(1)}, bf16[6,128,512]{2,1,0:T(8,128)(2,1)S(1)}, u32[]{:S(2)}, u32[]{:S(2)}) collective-permute-start(bf16[6,128,512]{2,1,0:T(8,128)(2,1)S(1)} %collective-permute-done.3.refs_21_), channel_id=1, source_target_pairs={{4,5},{9,8},{8,9},{5,4},{12,13},{1,0},{6,7},{11,10},{10,11},{7,6},... | collective-permute-start | bytes 2359304 | tf_op jit(solution)/shard_map/ppermute | solution.py:654
  67.2 7.8 %collective-permute-start.16 = (bf16[6,128,512]{2,1,0:T(8,128)(2,1)S(1)}, bf16[6,128,512]{2,1,0:T(8,128)(2,1)S(1)}, u32[]{:S(2)}, u32[]{:S(2)}) collective-permute-start(bf16[6,128,512]{2,1,0:T(8,128)(2,1)S(1)} %collective-permute-done.15.refs_17_), channel_id=1, source_target_pairs={{0,1},{13,12},{4,5},{9,8},{2,3},{15,14},{6,7},{11,10},{16,17},{29,... | collective-permute-start | bytes 2359304 | tf_op jit(solution)/shard_map/ppermute | solution.py:654
  75.0 1.3 %collective-permute-start.14 = (bf16[6,128,512]{2,1,0:T(8,128)(2,1)S(1)}, bf16[6,128,512]{2,1,0:T(8,128)(2,1)S(1)}, u32[]{:S(2)}, u32[]{:S(2)}) collective-permute-start(bf16[6,128,512]{2,1,0:T(8,128)(2,1)S(1)} %collective-permute-done.13), channel_id=1, source_target_pairs={{8,9},{5,4},{12,13},{1,0},{10,11},{7,6},{14,15},{3,2},{24,25},{21,... | collective-permute-start | bytes 2359304 | tf_op jit(solution)/shard_map/ppermute | solution.py:654
  76.3 6.8 %collective-permute-start.19 = (bf16[6,128,512]{2,1,0:T(8,128)(2,1)S(1)}, bf16[6,128,512]{2,1,0:T(8,128)(2,1)S(1)}, u32[]{:S(2)}, u32[]{:S(2)}) collective-permute-start(bf16[6,128,512]{2,1,0:T(8,128)(2,1)S(1)} %collective-permute-done.18.refs_23_), channel_id=1, source_target_pairs={{0,1},{13,12},{4,5},{9,8},{2,3},{15,14},{6,7},{11,10},{16,17},{29,... | collective-permute-start | bytes 2359304 | tf_op jit(solution)/shard_map/ppermute | solution.py:654
  83.1 0.7 collective-permute-start.22
  83.9 0.7 collective-permute-start.17
  84.6 0.4 collective-permute-done.19.refs_24_
  85.0 9.5 %grow.1 = (bf16[4,6,256,512]{3,2,1,0:T(8,128)(2,1)}, bf16[6,512,512]{2,1,0:T(8,128)(2,1)S(1)}) custom-call(s32[232]{0:T(256)S(1)} %copy-done.8, bf16[6,256,512]{2,1,0:T(8,128)(2,1)S(1)} %copy-done, bf16[3,256,512]{2,1,0:T(8,128)(2,1)} %bitcast.4.refs_1_, bf16[3,256,512]{2,1,0:T(8,128)(2,1)} %bitcast.5.refs_2_, bf16[3,256,512]{2,1,0:T(8,128)(2,1)} %bitcast.6.refs_3_, ...), custom_call_target="tpu_custom_call" | custom-call | flops 1048576 | bytes 4096 | tf_op jit(solution)/shard_map/grow/pallas_call | solution.py:536
  94.5 1.3 %collective-permute-start.23 = (bf16[6,128,512]{2,1,0:T(8,128)(2,1)S(1)}, bf16[6,128,512]{2,1,0:T(8,128)(2,1)S(1)}, u32[]{:S(2)}, u32[]{:S(2)}) collective-permute-start(bf16[6,128,512]{2,1,0:T(8,128)(2,1)S(1)} %collective-permute-done.22), channel_id=1, source_target_pairs={{12,13},{1,0},{14,15},{3,2},{28,29},{17,16},{30,31},{19,18}} | collective-permute-start | bytes 2359304 | tf_op jit(solution)/shard_map/ppermute | solution.py:654
  95.8 1.3 %collective-permute-start.21 = (bf16[6,128,512]{2,1,0:T(8,128)(2,1)S(1)}, bf16[6,128,512]{2,1,0:T(8,128)(2,1)S(1)}, u32[]{:S(2)}, u32[]{:S(2)}) collective-permute-start(bf16[6,128,512]{2,1,0:T(8,128)(2,1)S(1)} %collective-permute-done.9), channel_id=1, source_target_pairs={{8,9},{5,4},{12,13},{1,0},{10,11},{7,6},{14,15},{3,2},{24,25},{21,... | collective-permute-start | bytes 2359304 | tf_op jit(solution)/shard_map/ppermute | solution.py:654
  97.1 1.3 %collective-permute-start.20 = (bf16[6,128,512]{2,1,0:T(8,128)(2,1)S(1)}, bf16[6,128,512]{2,1,0:T(8,128)(2,1)S(1)}, u32[]{:S(2)}, u32[]{:S(2)}) collective-permute-start(bf16[6,128,512]{2,1,0:T(8,128)(2,1)S(1)} %collective-permute-done.17), channel_id=1, source_target_pairs={{12,13},{1,0},{14,15},{3,2},{28,29},{17,16},{30,31},{19,18}} | collective-permute-start | bytes 2359304 | tf_op jit(solution)/shard_map/ppermute | solution.py:654
  98.4 1.7 %collective-permute-done.23 = bf16[6,128,512]{2,1,0:T(8,128)(2,1)S(1)} collective-permute-done((bf16[6,128,512]{2,1,0:T(8,128)(2,1)S(1)}, bf16[6,128,512]{2,1,0:T(8,128)(2,1)S(1)}, u32[]{:S(2)}, u32[]{:S(2)}) %collective-permute-start.23) | collective-permute-done | bytes 786464 | tf_op jit(solution)/shard_map/ppermute | solution.py:654
  100.1 1.3 %collective-permute-done.21 = bf16[6,128,512]{2,1,0:T(8,128)(2,1)S(1)} collective-permute-done((bf16[6,128,512]{2,1,0:T(8,128)(2,1)S(1)}, bf16[6,128,512]{2,1,0:T(8,128)(2,1)S(1)}, u32[]{:S(2)}, u32[]{:S(2)}) %collective-permute-start.21) | collective-permute-done | bytes 786464 | tf_op jit(solution)/shard_map/ppermute | solution.py:654
  101.4 6.2 %finish.2.refs_4_ = bf16[4,6,256,512]{3,2,1,0:T(8,128)(2,1)} custom-call(s32[232]{0:T(256)S(1)} %copy-done.8, bf16[3,256,512]{2,1,0:T(8,128)(2,1)S(1)} %bitcast.33, bf16[3,256,512]{2,1,0:T(8,128)(2,1)S(1)} %bitcast.28, bf16[3,256,512]{2,1,0:T(8,128)(2,1)S(1)} %bitcast.31, bf16[4,512,512]{2,1,0:T(8,128)(2,1)S(1)} %copy-done.2, ...), custom_call_target="tpu_custom_call", output_to_operand_aliasing={{}: (6, {})} | custom-call | flops 1048576 | bytes 4096 | tf_op jit(solution)/shard_map/finish/pallas_call | solution.py:622
  107.6 2.4 %finish.3 = bf16[4,6,256,512]{3,2,1,0:T(8,128)(2,1)} custom-call(s32[232]{0:T(256)S(1)} %copy-done.8, bf16[3,256,512]{2,1,0:T(8,128)(2,1)S(1)} %bitcast.29, bf16[3,256,512]{2,1,0:T(8,128)(2,1)S(1)} %bitcast.32, bf16[4,512,512]{2,1,0:T(8,128)(2,1)S(1)} %copy-done.2, ...), custom_call_target="tpu_custom_call", output_to_operand_aliasing={{}: (5, {})} | custom-call | flops 1048576 | bytes 4096 | tf_op jit(solution)/shard_map/finish/pallas_call | solution.py:622
  (30 shorter events, 0.1 us)
Async XLA Ops:
  0.0 30.8 %copy-start = (bf16[6,256,512]{2,1,0:T(8,128)(2,1)S(1)}, bf16[6,256,512]{2,1,0:T(8,128)(2,1)}, u32[]{:S(2)}) copy-start(bf16[6,256,512]{2,1,0:T(8,128)(2,1)} %refs_0_.1) | copy-start | bytes 4718596
  0.0 30.8 %copy-start.1 = (bf16[6,256,512]{2,1,0:T(8,128)(2,1)S(1)}, bf16[6,256,512]{2,1,0:T(8,128)(2,1)}, u32[]{:S(2)}) copy-start(bf16[6,256,512]{2,1,0:T(8,128)(2,1)} %env.7) | copy-start | bytes 4718596
  0.0 30.8 %copy-start.9 = (f32[24,3]{0,1:T(4,128)S(1)}, f32[24,3]{0,1:T(4,128)}, u32[]{:S(2)}) copy-start(f32[24,3]{0,1:T(4,128)} %param.13) | copy-start | bytes 868
  2.2 14.8 %collective-permute-start.4 = (bf16[6,128,512]{2,1,0:T(8,128)(2,1)}, bf16[6,128,512]{2,1,0:T(8,128)(2,1)}, u32[]{:S(2)}, u32[]{:S(2)}) collective-permute-start(bf16[6,128,512]{2,1,0:T(8,128)(2,1)} %head.3), channel_id=1, source_target_pairs={{0,4},{4,8},{8,12},{13,9},{9,5},{5,1},{2,6},{6,10},{10,14},{15,11}... | collective-permute-start | bytes 2359304 | tf_op jit(solution)/shard_map/ppermute | solution.py:650
  10.1 15.3 %collective-permute-start = (bf16[6,128,512]{2,1,0:T(8,128)(2,1)}, bf16[6,128,512]{2,1,0:T(8,128)(2,1)}, u32[]{:S(2)}, u32[]{:S(2)}) collective-permute-start(bf16[6,128,512]{2,1,0:T(8,128)(2,1)} %head.2), channel_id=1, source_target_pairs={{0,4},{4,8},{8,12},{13,9},{9,5},{5,1},{2,6},{6,10},{10,14},{15,11}... | collective-permute-start | bytes 2359304 | tf_op jit(solution)/shard_map/ppermute | solution.py:650
  17.0 13.8 %collective-permute-start.6 = (bf16[6,128,512]{2,1,0:T(8,128)(2,1)}, bf16[6,128,512]{2,1,0:T(8,128)(2,1)}, u32[]{:S(2)}, u32[]{:S(2)}) collective-permute-start(bf16[6,128,512]{2,1,0:T(8,128)(2,1)} %collective-permute-done.4.first), channel_id=1, source_target_pairs={{4,5},{9,8},{12,13},{1,0},{6,7},{11,10},{14,15},{3,2},{20,21},{25,... | collective-permute-start | bytes 2359304 | tf_op jit(solution)/shard_map/ppermute | solution.py:654
  18.2 12.5 %collective-permute-start.5 = (bf16[6,128,512]{2,1,0:T(8,128)(2,1)}, bf16[6,128,512]{2,1,0:T(8,128)(2,1)}, u32[]{:S(2)}, u32[]{:S(2)}) collective-permute-start(bf16[6,128,512]{2,1,0:T(8,128)(2,1)} %collective-permute-done.4.first), channel_id=1, source_target_pairs={{4,8},{9,5},{6,10},{11,7},{20,24},{25,21},{22,26},{27,23}} | collective-permute-start | bytes 2359304 | tf_op jit(solution)/shard_map/ppermute | solution.py:650
  25.4 15.8 %collective-permute-start.2 = (bf16[6,128,512]{2,1,0:T(8,128)(2,1)}, bf16[6,128,512]{2,1,0:T(8,128)(2,1)}, u32[]{:S(2)}, u32[]{:S(2)}) collective-permute-start(bf16[6,128,512]{2,1,0:T(8,128)(2,1)} %collective-permute-done.first), channel_id=1, source_target_pairs={{4,5},{9,8},{12,13},{1,0},{6,7},{11,10},{14,15},{3,2},{20,21},{25,... | collective-permute-start | bytes 2359304 | tf_op jit(solution)/shard_map/ppermute | solution.py:654
  26.7 14.5 %collective-permute-start.1 = (bf16[6,128,512]{2,1,0:T(8,128)(2,1)}, bf16[6,128,512]{2,1,0:T(8,128)(2,1)}, u32[]{:S(2)}, u32[]{:S(2)}) collective-permute-start(bf16[6,128,512]{2,1,0:T(8,128)(2,1)} %collective-permute-done.first), channel_id=1, source_target_pairs={{4,8},{9,5},{6,10},{11,7},{20,24},{25,21},{22,26},{27,23}} | collective-permute-start | bytes 2359304 | tf_op jit(solution)/shard_map/ppermute | solution.py:650
  30.8 0.6 copy-start.7
  33.1 9.8 %copy-start.3 = (bf16[6,128,512]{2,1,0:T(8,128)(2,1)}, bf16[6,128,512]{2,1,0:T(8,128)(2,1)S(1)}, u32[]{:S(2)}) copy-start(bf16[6,128,512]{2,1,0:T(8,128)(2,1)S(1)} %get-tuple-element.19.refs_13_) | copy-start | bytes 2359300
  33.1 18.2 %collective-permute-start.10 = (bf16[6,128,512]{2,1,0:T(8,128)(2,1)}, bf16[6,128,512]{2,1,0:T(8,128)(2,1)}, u32[]{:S(2)}, u32[]{:S(2)}) collective-permute-start(bf16[6,128,512]{2,1,0:T(8,128)(2,1)} %get-tuple-element.22), channel_id=1, source_target_pairs={{0,4},{4,8},{8,12},{13,9},{9,5},{5,1},{2,6},{6,10},{10,14},{15,11}... | collective-permute-start | bytes 2359304 | tf_op jit(solution)/shard_map/ppermute | solution.py:650
  42.9 0.9 copy-start.5
  42.9 42.1 %copy-start.8 = (s32[232]{0:T(256)S(1)}, s32[232]{0:T(256)}, u32[]{:S(2)}) copy-start(s32[232]{0:T(256)} %tables.1.table) | copy-start | bytes 2788
  43.8 41.2 %copy-start.4 = (bf16[6,128,512]{2,1,0:T(8,128)(2,1)S(1)}, bf16[6,128,512]{2,1,0:T(8,128)(2,1)}, u32[]{:S(2)}) copy-start(bf16[6,128,512]{2,1,0:T(8,128)(2,1)} %copy-done.3) | copy-start | bytes 2359300
  43.8 15.7 %collective-permute-start.3 = (bf16[6,128,512]{2,1,0:T(8,128)(2,1)}, bf16[6,128,512]{2,1,0:T(8,128)(2,1)S(1)}, u32[]{:S(2)}, u32[]{:S(2)}) collective-permute-start(bf16[6,128,512]{2,1,0:T(8,128)(2,1)} %get-tuple-element.18), channel_id=1, source_target_pairs={{0,4},{4,8},{8,12},{13,9},{9,5},{5,1},{2,6},{6,10},{10,14},{15,11}... | collective-permute-start | bytes 2359304 | tf_op jit(solution)/shard_map/ppermute | solution.py:650
  49.7 35.3 %copy-start.2 = (bf16[4,512,512]{2,1,0:T(8,128)(2,1)S(1)}, bf16[4,512,512]{2,1,0:T(8,128)(2,1)}, u32[]{:S(2)}) copy-start(bf16[4,512,512]{2,1,0:T(8,128)(2,1)} %refs_2_.1) | copy-start | bytes 6291460
  49.7 35.2 %copy-start.6 = (bf16[6,128,512]{2,1,0:T(8,128)(2,1)S(1)}, bf16[6,128,512]{2,1,0:T(8,128)(2,1)}, u32[]{:S(2)}) copy-start(bf16[6,128,512]{2,1,0:T(8,128)(2,1)} %copy-done.5) | copy-start | bytes 2359300
  49.7 11.1 %collective-permute-start.7 = (bf16[6,128,512]{2,1,0:T(8,128)(2,1)}, bf16[6,128,512]{2,1,0:T(8,128)(2,1)S(1)}, u32[]{:S(2)}, u32[]{:S(2)}) collective-permute-start(bf16[6,128,512]{2,1,0:T(8,128)(2,1)} %copy-done.3), channel_id=1, source_target_pairs={{8,9},{5,4},{10,11},{7,6},{24,25},{21,20},{26,27},{23,22}} | collective-permute-start | bytes 2359304 | tf_op jit(solution)/shard_map/ppermute | solution.py:654
  50.6 10.3 %collective-permute-start.8 = (bf16[6,128,512]{2,1,0:T(8,128)(2,1)}, bf16[6,128,512]{2,1,0:T(8,128)(2,1)S(1)}, u32[]{:S(2)}, u32[]{:S(2)}) collective-permute-start(bf16[6,128,512]{2,1,0:T(8,128)(2,1)} %copy-done.5), channel_id=1, source_target_pairs={{8,9},{5,4},{10,11},{7,6},{24,25},{21,20},{26,27},{23,22}} | collective-permute-start | bytes 2359304 | tf_op jit(solution)/shard_map/ppermute | solution.py:654
  52.6 13.3 %collective-permute-start.15 = (bf16[6,128,512]{2,1,0:T(8,128)(2,1)S(1)}, bf16[6,128,512]{2,1,0:T(8,128)(2,1)S(1)}, u32[]{:S(2)}, u32[]{:S(2)}) collective-permute-start(bf16[6,128,512]{2,1,0:T(8,128)(2,1)S(1)} %broadcast_select_fusion.1), channel_id=1, source_target_pairs={{8,11},{10,9},{5,6},{7,4},{12,15},{14,13},{1,2},{3,0},{24,27},{26,... | collective-permute-start | bytes 2359304 | tf_op jit(solution)/shard_map/ppermute | solution.py:659
  53.9 13.3 %collective-permute-start.13 = (bf16[6,128,512]{2,1,0:T(8,128)(2,1)}, bf16[6,128,512]{2,1,0:T(8,128)(2,1)S(1)}, u32[]{:S(2)}, u32[]{:S(2)}) collective-permute-start(bf16[6,128,512]{2,1,0:T(8,128)(2,1)} %collective-permute-done.10.refs_15_), channel_id=1, source_target_pairs={{4,8},{8,12},{9,5},{5,1},{6,10},{10,14},{11,7},{7,3},{20,24},{24,2... | collective-permute-start | bytes 2359304 | tf_op jit(solution)/shard_map/ppermute | solution.py:650
  59.6 15.4 %collective-permute-start.18 = (bf16[6,128,512]{2,1,0:T(8,128)(2,1)S(1)}, bf16[6,128,512]{2,1,0:T(8,128)(2,1)S(1)}, u32[]{:S(2)}, u32[]{:S(2)}) collective-permute-start(bf16[6,128,512]{2,1,0:T(8,128)(2,1)S(1)} %broadcast_select_fusion), channel_id=1, source_target_pairs={{8,11},{10,9},{5,6},{7,4},{12,15},{14,13},{1,2},{3,0},{24,27},{26,... | collective-permute-start | bytes 2359304 | tf_op jit(solution)/shard_map/ppermute | solution.py:659
  60.9 15.4 %collective-permute-start.9 = (bf16[6,128,512]{2,1,0:T(8,128)(2,1)S(1)}, bf16[6,128,512]{2,1,0:T(8,128)(2,1)S(1)}, u32[]{:S(2)}, u32[]{:S(2)}) collective-permute-start(bf16[6,128,512]{2,1,0:T(8,128)(2,1)S(1)} %collective-permute-done.3.refs_21_), channel_id=1, source_target_pairs={{4,8},{8,12},{9,5},{5,1},{6,10},{10,14},{11,7},{7,3},{20,24},{24,2... | collective-permute-start | bytes 2359304 | tf_op jit(solution)/shard_map/ppermute | solution.py:650
  61.6 21.5 %collective-permute-start.11 = (bf16[6,128,512]{2,1,0:T(8,128)(2,1)}, bf16[6,128,512]{2,1,0:T(8,128)(2,1)S(1)}, u32[]{:S(2)}, u32[]{:S(2)}) collective-permute-start(bf16[6,128,512]{2,1,0:T(8,128)(2,1)} %collective-permute-done.10.refs_15_), channel_id=1, source_target_pairs={{4,5},{9,8},{8,9},{5,4},{12,13},{1,0},{6,7},{11,10},{10,11},{7,6},... | collective-permute-start | bytes 2359304 | tf_op jit(solution)/shard_map/ppermute | solution.py:654
  65.9 18.0 %collective-permute-start.12 = (bf16[6,128,512]{2,1,0:T(8,128)(2,1)S(1)}, bf16[6,128,512]{2,1,0:T(8,128)(2,1)S(1)}, u32[]{:S(2)}, u32[]{:S(2)}) collective-permute-start(bf16[6,128,512]{2,1,0:T(8,128)(2,1)S(1)} %collective-permute-done.3.refs_21_), channel_id=1, source_target_pairs={{4,5},{9,8},{8,9},{5,4},{12,13},{1,0},{6,7},{11,10},{10,11},{7,6},... | collective-permute-start | bytes 2359304 | tf_op jit(solution)/shard_map/ppermute | solution.py:654
  67.2 16.7 %collective-permute-start.16 = (bf16[6,128,512]{2,1,0:T(8,128)(2,1)S(1)}, bf16[6,128,512]{2,1,0:T(8,128)(2,1)S(1)}, u32[]{:S(2)}, u32[]{:S(2)}) collective-permute-start(bf16[6,128,512]{2,1,0:T(8,128)(2,1)S(1)} %collective-permute-done.15.refs_17_), channel_id=1, source_target_pairs={{0,1},{13,12},{4,5},{9,8},{2,3},{15,14},{6,7},{11,10},{16,17},{29,... | collective-permute-start | bytes 2359304 | tf_op jit(solution)/shard_map/ppermute | solution.py:654
  75.0 8.9 %collective-permute-start.14 = (bf16[6,128,512]{2,1,0:T(8,128)(2,1)S(1)}, bf16[6,128,512]{2,1,0:T(8,128)(2,1)S(1)}, u32[]{:S(2)}, u32[]{:S(2)}) collective-permute-start(bf16[6,128,512]{2,1,0:T(8,128)(2,1)S(1)} %collective-permute-done.13), channel_id=1, source_target_pairs={{8,9},{5,4},{12,13},{1,0},{10,11},{7,6},{14,15},{3,2},{24,25},{21,... | collective-permute-start | bytes 2359304 | tf_op jit(solution)/shard_map/ppermute | solution.py:654
  76.3 8.7 %collective-permute-start.19 = (bf16[6,128,512]{2,1,0:T(8,128)(2,1)S(1)}, bf16[6,128,512]{2,1,0:T(8,128)(2,1)S(1)}, u32[]{:S(2)}, u32[]{:S(2)}) collective-permute-start(bf16[6,128,512]{2,1,0:T(8,128)(2,1)S(1)} %collective-permute-done.18.refs_23_), channel_id=1, source_target_pairs={{0,1},{13,12},{4,5},{9,8},{2,3},{15,14},{6,7},{11,10},{16,17},{29,... | collective-permute-start | bytes 2359304 | tf_op jit(solution)/shard_map/ppermute | solution.py:654
  83.1 11.3 %collective-permute-start.22 = (bf16[6,128,512]{2,1,0:T(8,128)(2,1)S(1)}, bf16[6,128,512]{2,1,0:T(8,128)(2,1)S(1)}, u32[]{:S(2)}, u32[]{:S(2)}) collective-permute-start(bf16[6,128,512]{2,1,0:T(8,128)(2,1)S(1)} %collective-permute-done.13), channel_id=1, source_target_pairs={{8,12},{5,1},{10,14},{7,3},{24,28},{21,17},{26,30},{23,19}} | collective-permute-start | bytes 2359304 | tf_op jit(solution)/shard_map/ppermute | solution.py:650
  83.9 13.2 %collective-permute-start.17 = (bf16[6,128,512]{2,1,0:T(8,128)(2,1)S(1)}, bf16[6,128,512]{2,1,0:T(8,128)(2,1)S(1)}, u32[]{:S(2)}, u32[]{:S(2)}) collective-permute-start(bf16[6,128,512]{2,1,0:T(8,128)(2,1)S(1)} %collective-permute-done.9), channel_id=1, source_target_pairs={{8,12},{5,1},{10,14},{7,3},{24,28},{21,17},{26,30},{23,19}} | collective-permute-start | bytes 2359304 | tf_op jit(solution)/shard_map/ppermute | solution.py:650
  94.5 5.6 %collective-permute-start.23 = (bf16[6,128,512]{2,1,0:T(8,128)(2,1)S(1)}, bf16[6,128,512]{2,1,0:T(8,128)(2,1)S(1)}, u32[]{:S(2)}, u32[]{:S(2)}) collective-permute-start(bf16[6,128,512]{2,1,0:T(8,128)(2,1)S(1)} %collective-permute-done.22), channel_id=1, source_target_pairs={{12,13},{1,0},{14,15},{3,2},{28,29},{17,16},{30,31},{19,18}} | collective-permute-start | bytes 2359304 | tf_op jit(solution)/shard_map/ppermute | solution.py:654
  95.8 5.6 %collective-permute-start.21 = (bf16[6,128,512]{2,1,0:T(8,128)(2,1)S(1)}, bf16[6,128,512]{2,1,0:T(8,128)(2,1)S(1)}, u32[]{:S(2)}, u32[]{:S(2)}) collective-permute-start(bf16[6,128,512]{2,1,0:T(8,128)(2,1)S(1)} %collective-permute-done.9), channel_id=1, source_target_pairs={{8,9},{5,4},{12,13},{1,0},{10,11},{7,6},{14,15},{3,2},{24,25},{21,... | collective-permute-start | bytes 2359304 | tf_op jit(solution)/shard_map/ppermute | solution.py:654
  97.1 10.5 %collective-permute-start.20 = (bf16[6,128,512]{2,1,0:T(8,128)(2,1)S(1)}, bf16[6,128,512]{2,1,0:T(8,128)(2,1)S(1)}, u32[]{:S(2)}, u32[]{:S(2)}) collective-permute-start(bf16[6,128,512]{2,1,0:T(8,128)(2,1)S(1)} %collective-permute-done.17), channel_id=1, source_target_pairs={{12,13},{1,0},{14,15},{3,2},{28,29},{17,16},{30,31},{19,18}} | collective-permute-start | bytes 2359304 | tf_op jit(solution)/shard_map/ppermute | solution.py:654
